TPU v7x, 768 devices: a whole 4x8x12 slice. The times are simulated.
768 devices in a mesh: slab: 8 (over x, core), tile: 96 (over z, y).
Axes of the slice: x: 4, y: 8, z: 12, core: 2. Of those that a mesh axis runs over, the one named last changes fastest.
Arguments:
- right_side: float32 [64, 1536, 128], P('slab', 'tile'), may hold values from -8 to 8
- diagonal: float32 [64, 1536, 128], P('slab', 'tile'), may hold values from 0.25 to 2
- inlet_index: int32 [8, 96, 384, 16], P('slab', 'tile'), may hold values from 0 to 16383
- plate_order: int32 [384], replicated, may hold values from 0 to 383, each once
- conductance: float32 [384], P('tile'), may hold values from 0.5 to 2
- plate_level: float32 [384], P('tile'), may hold values from -3 to 3
Outputs:
- solution: float32 [64, 1536, 128], P('slab', 'tile')
- residual: float32 [64, 1536, 128], P('slab', 'tile')
- inlet_flow: float32 [384], P('tile')
Inputs may be any that keep to these rules, and one draw needn't show every extreme that they name: `inlet_index`: each entry is a cell of the block of the device given by the first two indices. `plate_order`: each plate appears once.
All inputs are finite; a program needn't handle non-finite values.
Results may differ from a plain program's by a relative error of at most 0.0003.
Values sent between devices are 32-bit elements; how exact they have to be, the bound alone decides.
No kernel may reach another device: no remote copies, remote signals or barrier semaphores. Data moves between devices by JAX's collectives and lax.ppermute only.
A program may use at most 32 MiB of HBM per device.

v0:
```python
import jax
import jax.numpy as jnp
from jax import lax
from jax.sharding import PartitionSpec as P

STEPS = 4
BLOCKS = 2


GRAM_PAIRS = [(row_at, col_at) for row_at in range(5) for col_at in range(row_at, 5)]


def extended(block, sides, width):
    for axis, dim in sides:
        count = lax.axis_size(axis)
        forward = [(i, i + 1) for i in range(count - 1)]
        backward = [(target, source) for source, target in forward]
        low = lax.ppermute(
            lax.slice_in_dim(block, block.shape[dim] - width, None, axis=dim), axis, forward
        )
        high = lax.ppermute(lax.slice_in_dim(block, 0, width, axis=dim), axis, backward)
        block = jnp.concatenate([low, block, high], axis=dim)
    return block


def apply_shifted(padded, diagonal):
    center = padded[1:-1, 1:-1]
    zero_col = jnp.zeros_like(center[:, :, :1])
    beside = padded[2:, 1:-1] + padded[:-2, 1:-1]
    beside = beside + padded[1:-1, 2:] + padded[1:-1, :-2]
    beside = (
        beside
        + jnp.concatenate([center[:, :, 1:], zero_col], axis=2)
        + jnp.concatenate([zero_col, center[:, :, :-1]], axis=2)
    )
    return ((diagonal - 1.0) * center - beside) / 7.0


def cholesky_solve(matrix, rhs):
    factor = jnp.linalg.cholesky(matrix)
    forward = []
    for row_at in range(4):
        value = rhs[row_at]
        for col_at in range(row_at):
            value = value - factor[row_at, col_at] * forward[col_at]
        forward.append(value / factor[row_at, row_at])
    backward = [None] * 4
    for row_at in range(3, -1, -1):
        value = forward[row_at]
        for col_at in range(row_at + 1, 4):
            value = value - factor[col_at, row_at] * backward[col_at]
        backward[row_at] = value / factor[row_at, row_at]
    return jnp.stack(backward)


def solve_block(gram_vec):
    entries = {}
    for place, pair in enumerate(GRAM_PAIRS):
        entries[pair] = gram_vec[place]
        entries[pair[1], pair[0]] = gram_vec[place]
    gram = jnp.stack(
        [jnp.stack([entries[row_at, col_at] for col_at in range(5)]) for row_at in range(5)]
    )
    matrix = 7.0 * (gram[:4, 1:] + gram[:4, :4])
    matrix = 0.5 * (matrix + matrix.T)
    return cholesky_solve(matrix, gram[:4, 0])


def update(solution, residual, basis, coeffs):
    for degree in range(4):
        solution = solution + coeffs[degree] * basis[degree]
        residual = residual - 7.0 * coeffs[degree] * (basis[degree + 1] + basis[degree])
    return (solution, residual)


def local_products(basis):
    stacked = jnp.stack(basis).reshape(len(basis), -1)
    full = jnp.dot(
        stacked, stacked.T, precision=lax.Precision.HIGHEST, preferred_element_type=jnp.float32
    )
    return jnp.stack([full[pair[0], pair[1]] for pair in GRAM_PAIRS])


def on_device(right_side, diagonal, inlet_index, plate_order, conductance, plate_level):
    solution = jnp.zeros_like(right_side)
    residual = right_side
    for repeat in range(BLOCKS):
        basis = [residual]
        for degree in range(STEPS):
            padded = extended(basis[-1], (("slab", 0), ("tile", 1)), 1)
            basis.append(apply_shifted(padded, diagonal))
        local_gram = local_products(basis)
        gram_vec = lax.psum(local_gram, ("slab", "tile"))
        coeffs = solve_block(gram_vec)
        solution, residual = update(solution, residual, basis, coeffs)
    flat_field = solution.reshape(-1)
    inlets = inlet_index.shape[3]
    picked = jnp.take(flat_field, inlet_index[0, 0], axis=0)
    contrib = jnp.sum(picked, axis=1)
    ordered = jnp.take(contrib, plate_order, axis=0)
    per_tile = conductance.shape[0]
    summed = lax.psum(ordered, ("slab", "tile"))
    owned = lax.dynamic_slice_in_dim(summed, lax.axis_index("tile") * per_tile, per_tile)
    scale = 1.0 / jnp.sqrt(jnp.float32(lax.axis_size("slab") * lax.axis_size("tile") * inlets))
    header = owned * scale
    inlet_flow = conductance * (header - plate_level)
    return (solution, residual, inlet_flow)


def solution(mesh):
    in_specs = (
        P("slab", "tile", None),
        P("slab", "tile", None),
        P("slab", "tile", None, None),
        P(),
        P("tile"),
        P("tile"),
    )
    out_specs = (P("slab", "tile", None), P("slab", "tile", None), P("tile"))
    return jax.shard_map(
        on_device, mesh=mesh, in_specs=in_specs, out_specs=out_specs, check_vma=False
    )
```

profile of v0, /device:TPU:1, one launch (start us, length us, event | category | flops | bytes accessed | tf_op | source)
XLA Modules:
  0.0 577.9 jit_solution(8754724452361677093)
XLA Ops:
  1.3 4.5 collective-permute-start.1
  5.9 9.2 %collective-permute-start = (f32[1,16,128]{2,1,0:T(8,128)S(1)}, f32[1,16,128]{2,1,0:T(8,128)S(1)}, u32[]{:S(2)}, u32[]{:S(2)}) collective-permute-start(f32[1,16,128]{2,1,0:T(8,128)S(1)} %get-tuple-element.64), channel_id=1, source_target_pairs={{96,0},{192,96},{288,192},{384,288},{480,384},{576,480},{672,576},... | collective-permute-start | bytes 24584 | tf_op jit(solution)/shard_map/ppermute | solution.py:21
  17.3 4.1 collective-permute-start.3
  22.3 3.2 collective-permute-start.4
  25.6 2.3 collective-permute-start.5
  30.0 4.5 collective-permute-start.7
  35.3 2.9 collective-permute-start.8
  38.3 3.8 collective-permute-start.9
  44.2 4.5 collective-permute-start.11
  51.5 5.0 collective-permute-start.13
  58.6 4.5 collective-permute-start.15
  66.6 9.5 %stack.112 = f32[15]{0:T(128)S(1)} concatenate(f32[1]{0:T(128)} %bitcast.10, f32[1]{0:T(128)} %bitcast.12, f32[1]{0:T(128)} %bitcast.13, f32[1]{0:T(128)} %bitcast.14, f32[1]{0:T(128)} %bitcast.15, f32[1]{0:T(128)} %bitcast.16, f32[1]{0:T(128)} %bitcast.17, f32[1]{0:T(128)} %bitcast.18, f32[1]{0:T(128)} %bitcast.19, f32[1]{0:T(128)} %bitcast.20, f32[1]{0:T(128)} %bitcast.21, ...), dimensions={0} | concatenate | bytes 120 | tf_op jit(solution)/shard_map/stack | solution.py:81
  76.3 127.8 %psum.21 = f32[15]{0:T(128)S(1)} all-reduce(f32[15]{0:T(128)S(1)} %stack.112), channel_id=1, replica_groups=mesh['slab'=8,'tile'=96] {'slab','tile'}, use_global_device_ids=true, to_apply=%region_0.0 | all-reduce | flops 15 | bytes 120 | tf_op jit(solution)/shard_map/psum | solution.py:93
  204.9 2.0 maximum_bitcast_fusion.2
  206.9 2.0 maximum_bitcast_fusion
  224.6 2.6 collective-permute-start.16
  227.2 3.0 collective-permute-start.17
  232.3 4.0 collective-permute-start.19
  237.2 2.5 collective-permute-start.20
  239.7 4.7 collective-permute-start.21
  246.5 4.5 collective-permute-start.23
  253.8 5.0 collective-permute-start.25
  261.0 4.5 collective-permute-start.27
  266.4 1.9 collective-permute-start.28
  268.3 5.0 collective-permute-start.29
  275.4 4.5 collective-permute-start.31
  282.8 9.5 %stack.127 = f32[15]{0:T(128)S(1)} concatenate(f32[1]{0:T(128)} %bitcast.53, f32[1]{0:T(128)} %bitcast.55, f32[1]{0:T(128)} %bitcast.56, f32[1]{0:T(128)} %bitcast.57, f32[1]{0:T(128)} %bitcast.58, f32[1]{0:T(128)} %bitcast.59, f32[1]{0:T(128)} %bitcast.60, f32[1]{0:T(128)} %bitcast.61, f32[1]{0:T(128)} %bitcast.62, f32[1]{0:T(128)} %bitcast.63, f32[1]{0:T(128)} %bitcast.64, ...), dimensions={0} | concatenate | bytes 120 | tf_op jit(solution)/shard_map/stack | solution.py:81
  292.4 120.4 %psum.22 = f32[15]{0:T(128)S(1)} all-reduce(f32[15]{0:T(128)S(1)} %stack.127), channel_id=1, replica_groups=mesh['slab'=8,'tile'=96] {'slab','tile'}, use_global_device_ids=true, to_apply=%region_3.5 | all-reduce | flops 15 | bytes 120 | tf_op jit(solution)/shard_map/psum | solution.py:93
  415.7 2.0 maximum_bitcast_fusion.5
  433.5 34.3 %gather_fusion = f32[6144]{0:T(1024)S(1)} fusion(f32[16384]{0:T(1024)S(1)} %bitcast.136, s32[6144]{0:T(1024)S(1)} %broadcast_clamp_fusion), kind=kCustom, calls=%fused_computation | custom fusion | bytes 73728 | tf_op jit(solution)/shard_map/jit(_take)/gather | solution.py:98
  468.1 2.8 gather_fusion.1
  470.9 105.7 %psum.23 = f32[384]{0:T(512)S(1)} all-reduce(f32[384]{0:T(512)S(1)} %and_select_fusion), channel_id=1, replica_groups=mesh['slab'=8,'tile'=96] {'slab','tile'}, use_global_device_ids=true, to_apply=%region_5.7 | all-reduce | flops 384 | bytes 3072 | tf_op jit(solution)/shard_map/psum | solution.py:102
  (148 shorter events, 43.6 us)
Async XLA Ops:
  1.3 13.7 %collective-permute-start.1 = (f32[1,16,128]{2,1,0:T(8,128)S(1)}, f32[1,16,128]{2,1,0:T(8,128)S(1)}, u32[]{:S(2)}, u32[]{:S(2)}) collective-permute-start(f32[1,16,128]{2,1,0:T(8,128)S(1)} %get-tuple-element.65), channel_id=1, source_target_pairs={{0,96},{96,192},{192,288},{288,384},{384,480},{480,576},{576,672},... | collective-permute-start | bytes 24584 | tf_op jit(solution)/shard_map/ppermute | solution.py:18
  5.9 10.2 %collective-permute-start = (f32[1,16,128]{2,1,0:T(8,128)S(1)}, f32[1,16,128]{2,1,0:T(8,128)S(1)}, u32[]{:S(2)}, u32[]{:S(2)}) collective-permute-start(f32[1,16,128]{2,1,0:T(8,128)S(1)} %get-tuple-element.64), channel_id=1, source_target_pairs={{96,0},{192,96},{288,192},{384,288},{480,384},{576,480},{672,576},... | collective-permute-start | bytes 24584 | tf_op jit(solution)/shard_map/ppermute | solution.py:21
  16.0 5.5 collective-permute-start.2
  17.3 4.9 collective-permute-start.3
  22.3 5.6 collective-permute-start.4
  25.6 3.1 collective-permute-start.5
  28.7 5.9 %collective-permute-start.6 = (f32[10,1,128]{2,1,0:T(1,128)S(1)}, f32[10,1,128]{2,1,0:T(1,128)S(1)}, u32[]{:S(2)}, u32[]{:S(2)}) collective-permute-start(f32[10,1,128]{2,1,0:T(1,128)S(1)} %get-tuple-element.32), channel_id=1, source_target_pairs={{1,0},{2,1},{3,2},{4,3},{5,4},{6,5},{7,6},{8,7},{9,8},{10,9},{11,1... | collective-permute-start | bytes 15368 | tf_op jit(solution)/shard_map/ppermute | solution.py:21
  30.0 5.2 collective-permute-start.7
  35.3 6.8 %collective-permute-start.8 = (f32[1,16,128]{2,1,0:T(8,128)S(1)}, f32[1,16,128]{2,1,0:T(8,128)S(1)}, u32[]{:S(2)}, u32[]{:S(2)}) collective-permute-start(f32[1,16,128]{2,1,0:T(8,128)S(1)} %get-tuple-element.57), channel_id=1, source_target_pairs={{96,0},{192,96},{288,192},{384,288},{480,384},{576,480},{672,576},... | collective-permute-start | bytes 24584 | tf_op jit(solution)/shard_map/ppermute | solution.py:21
  38.3 4.6 collective-permute-start.9
  42.9 5.9 %collective-permute-start.10 = (f32[10,1,128]{2,1,0:T(1,128)S(1)}, f32[10,1,128]{2,1,0:T(1,128)S(1)}, u32[]{:S(2)}, u32[]{:S(2)}) collective-permute-start(f32[10,1,128]{2,1,0:T(1,128)S(1)} %get-tuple-element.30), channel_id=1, source_target_pairs={{1,0},{2,1},{3,2},{4,3},{5,4},{6,5},{7,6},{8,7},{9,8},{10,9},{11,1... | collective-permute-start | bytes 15368 | tf_op jit(solution)/shard_map/ppermute | solution.py:21
  44.2 5.3 collective-permute-start.11
  49.6 7.1 %collective-permute-start.12 = (f32[1,16,128]{2,1,0:T(8,128)S(1)}, f32[1,16,128]{2,1,0:T(8,128)S(1)}, u32[]{:S(2)}, u32[]{:S(2)}) collective-permute-start(f32[1,16,128]{2,1,0:T(8,128)S(1)} %get-tuple-element.55), channel_id=1, source_target_pairs={{96,0},{192,96},{288,192},{384,288},{480,384},{576,480},{672,576},... | collective-permute-start | bytes 24584 | tf_op jit(solution)/shard_map/ppermute | solution.py:21
  51.5 5.8 %collective-permute-start.13 = (f32[1,16,128]{2,1,0:T(8,128)S(1)}, f32[1,16,128]{2,1,0:T(8,128)S(1)}, u32[]{:S(2)}, u32[]{:S(2)}) collective-permute-start(f32[1,16,128]{2,1,0:T(8,128)S(1)} %get-tuple-element.54), channel_id=1, source_target_pairs={{0,96},{96,192},{192,288},{288,384},{384,480},{480,576},{576,672},... | collective-permute-start | bytes 24584 | tf_op jit(solution)/shard_map/ppermute | solution.py:18
  57.3 5.9 %collective-permute-start.14 = (f32[10,1,128]{2,1,0:T(1,128)S(1)}, f32[10,1,128]{2,1,0:T(1,128)S(1)}, u32[]{:S(2)}, u32[]{:S(2)}) collective-permute-start(f32[10,1,128]{2,1,0:T(1,128)S(1)} %get-tuple-element.28), channel_id=1, source_target_pairs={{1,0},{2,1},{3,2},{4,3},{5,4},{6,5},{7,6},{8,7},{9,8},{10,9},{11,1... | collective-permute-start | bytes 15368 | tf_op jit(solution)/shard_map/ppermute | solution.py:21
  58.6 5.3 collective-permute-start.15
  224.6 5.6 collective-permute-start.16
  227.2 3.8 collective-permute-start.17
  231.0 5.4 collective-permute-start.18
  232.3 4.7 collective-permute-start.19
  237.2 7.3 %collective-permute-start.20 = (f32[1,16,128]{2,1,0:T(8,128)S(1)}, f32[1,16,128]{2,1,0:T(8,128)S(1)}, u32[]{:S(2)}, u32[]{:S(2)}) collective-permute-start(f32[1,16,128]{2,1,0:T(8,128)S(1)} %get-tuple-element.45), channel_id=1, source_target_pairs={{96,0},{192,96},{288,192},{384,288},{480,384},{576,480},{672,576},... | collective-permute-start | bytes 24584 | tf_op jit(solution)/shard_map/ppermute | solution.py:21
  239.7 5.5 collective-permute-start.21
  245.2 5.9 %collective-permute-start.22 = (f32[10,1,128]{2,1,0:T(1,128)S(1)}, f32[10,1,128]{2,1,0:T(1,128)S(1)}, u32[]{:S(2)}, u32[]{:S(2)}) collective-permute-start(f32[10,1,128]{2,1,0:T(1,128)S(1)} %get-tuple-element.24), channel_id=1, source_target_pairs={{1,0},{2,1},{3,2},{4,3},{5,4},{6,5},{7,6},{8,7},{9,8},{10,9},{11,1... | collective-permute-start | bytes 15368 | tf_op jit(solution)/shard_map/ppermute | solution.py:21
  246.5 5.3 collective-permute-start.23
  251.9 7.1 %collective-permute-start.24 = (f32[1,16,128]{2,1,0:T(8,128)S(1)}, f32[1,16,128]{2,1,0:T(8,128)S(1)}, u32[]{:S(2)}, u32[]{:S(2)}) collective-permute-start(f32[1,16,128]{2,1,0:T(8,128)S(1)} %get-tuple-element.41), channel_id=1, source_target_pairs={{96,0},{192,96},{288,192},{384,288},{480,384},{576,480},{672,576},... | collective-permute-start | bytes 24584 | tf_op jit(solution)/shard_map/ppermute | solution.py:21
  253.8 5.8 %collective-permute-start.25 = (f32[1,16,128]{2,1,0:T(8,128)S(1)}, f32[1,16,128]{2,1,0:T(8,128)S(1)}, u32[]{:S(2)}, u32[]{:S(2)}) collective-permute-start(f32[1,16,128]{2,1,0:T(8,128)S(1)} %get-tuple-element.40), channel_id=1, source_target_pairs={{0,96},{96,192},{192,288},{288,384},{384,480},{480,576},{576,672},... | collective-permute-start | bytes 24584 | tf_op jit(solution)/shard_map/ppermute | solution.py:18
  259.7 5.9 %collective-permute-start.26 = (f32[10,1,128]{2,1,0:T(1,128)S(1)}, f32[10,1,128]{2,1,0:T(1,128)S(1)}, u32[]{:S(2)}, u32[]{:S(2)}) collective-permute-start(f32[10,1,128]{2,1,0:T(1,128)S(1)} %get-tuple-element.22), channel_id=1, source_target_pairs={{1,0},{2,1},{3,2},{4,3},{5,4},{6,5},{7,6},{8,7},{9,8},{10,9},{11,1... | collective-permute-start | bytes 15368 | tf_op jit(solution)/shard_map/ppermute | solution.py:21
  261.0 5.3 collective-permute-start.27
  266.4 7.1 %collective-permute-start.28 = (f32[1,16,128]{2,1,0:T(8,128)S(1)}, f32[1,16,128]{2,1,0:T(8,128)S(1)}, u32[]{:S(2)}, u32[]{:S(2)}) collective-permute-start(f32[1,16,128]{2,1,0:T(8,128)S(1)} %get-tuple-element.37), channel_id=1, source_target_pairs={{96,0},{192,96},{288,192},{384,288},{480,384},{576,480},{672,576},... | collective-permute-start | bytes 24584 | tf_op jit(solution)/shard_map/ppermute | solution.py:21
  268.3 5.8 %collective-permute-start.29 = (f32[1,16,128]{2,1,0:T(8,128)S(1)}, f32[1,16,128]{2,1,0:T(8,128)S(1)}, u32[]{:S(2)}, u32[]{:S(2)}) collective-permute-start(f32[1,16,128]{2,1,0:T(8,128)S(1)} %get-tuple-element.36), channel_id=1, source_target_pairs={{0,96},{96,192},{192,288},{288,384},{384,480},{480,576},{576,672},... | collective-permute-start | bytes 24584 | tf_op jit(solution)/shard_map/ppermute | solution.py:18
  274.1 5.9 %collective-permute-start.30 = (f32[10,1,128]{2,1,0:T(1,128)S(1)}, f32[10,1,128]{2,1,0:T(1,128)S(1)}, u32[]{:S(2)}, u32[]{:S(2)}) collective-permute-start(f32[10,1,128]{2,1,0:T(1,128)S(1)} %get-tuple-element.20), channel_id=1, source_target_pairs={{1,0},{2,1},{3,2},{4,3},{5,4},{6,5},{7,6},{8,7},{9,8},{10,9},{11,1... | collective-permute-start | bytes 15368 | tf_op jit(solution)/shard_map/ppermute | solution.py:21
  275.4 5.3 collective-permute-start.31
  (7 other events, 271.3 us)
where the time goes:
time: 580 us; the launch traced here: 578 us
  blocking collectives  354 us (61%)
  starting transfers between devices  105 us (18%)
  local copies, waits for them, and re-layouts  64.6 us (11%)
  between operations  27.2 us (5%)
  other arithmetic  14.1 us (2%)
  waiting for transfers between devices  10.3 us (2%)
    psum x2, blocking collectives, on_device(): gram_vec = lax.psum(local_gram, ('slab', 'tile'))  248 us
    psum x1, blocking collectives, on_device(): summed = lax.psum(ordered, ('slab', 'tile'))  106 us
    ppermute x16, starting transfers between devices, extended(): lax.ppermute(lax.slice_in_dim(block, block.shape[dim] - width, None, axis...  68.7 us
    ppermute x16, starting transfers between devices, extended(): lax.ppermute(lax.slice_in_dim(block, 0, width, axis=dim), axis, backward)  36.6 us
    gather x2, local copies, waits for them, and re-layouts, on_device(): picked = jnp.take(flat_field, inlet_index[0, 0], axis=0)  34.4 us
    another operation x2, local copies, waits for them, and re-layouts, local_products(): return jnp.stack([full[pair[0], pair[1]] for pair in GRAM_PAIRS])  19.1 us
  transfers between devices with their start and end apart: 32, of which 15 were waited for; matrix products, arithmetic and copies ran while one was open for 0% of the time, Pallas kernels for 0%

commit v1 on v0

v1 whole, which is shorter than its diff:
```python
import functools

import jax
import jax.numpy as jnp
from jax import lax
from jax.experimental import pallas as pl
from jax.experimental.pallas import tpu as pltpu
from jax.sharding import PartitionSpec as P

HALO = 8
DEGREE = 8
FIELDS = 8
OWNED = 4
LANES = 128
MOMENT_LANE = 32
LOW_LANE = 64


def two_sum(a, b):
    s = a + b
    v = s - a
    return s, (a - (s - v)) + (b - v)


def quick_two_sum(a, b):
    s = a + b
    return s, b - (s - a)


def split(a):
    c = a * 4097.0
    high = c - (c - a)
    return high, a - high


def two_prod(a, b):
    p = a * b
    ah, al = split(a)
    bh, bl = split(b)
    return p, ((ah * bh - p) + ah * bl + al * bh) + al * bl


def dd_add(x, y):
    s, e = two_sum(x[0], y[0])
    t, f = two_sum(x[1], y[1])
    s, e = quick_two_sum(s, e + t)
    return quick_two_sum(s, e + f)


def dd_mul(x, y):
    p, e = two_prod(x[0], y[0])
    return quick_two_sum(p, e + (x[0] * y[1] + x[1] * y[0]))


def dd_scale(x, power):
    return x[0] * power, x[1] * power


def dd_neg(x):
    return -x[0], -x[1]


def dd_sum(terms):
    total = terms[0]
    for term in terms[1:]:
        total = dd_add(total, term)
    return total


def lane_of(shape):
    return lax.broadcasted_iota(jnp.int32, shape, len(shape) - 1)


def basis_kernel(own, low, high, index, order, payload, basis, last, alpha, beta, even, odd, parts, sums):
    cz = own.shape[1]
    wide_y = own.shape[2]
    cy = wide_y - 2 * HALO
    for place, source in enumerate((low, own, high)):
        at = pl.ds(place * cz, cz)
        even[at] = source[0]
        diag = source[1]
        inside = jnp.where(diag > 0.0, 0.25, 0.0)
        beta[at] = inside
        alpha[at] = (diag - 1.0) * inside
    lane = lane_of((wide_y, LANES))
    planes = 3 * cz

    def emit(field, degree):
        for z in range(cz):
            value = field[cz + z, HALO : HALO + cy, :]
            if degree < FIELDS:
                basis[pl.ds(z * cy * FIELDS + degree, cy, stride=FIELDS), :] = value
            else:
                last[pl.ds(z * cy, cy), :] = value

    def product(first, second, slot):
        total = None
        for z in range(cz):
            term = first[cz + z, HALO : HALO + cy, :] * second[cz + z, HALO : HALO + cy, :]
            term = term[:8] + term[8:]
            total = term if total is None else total + term
        parts[pl.ds(slot * 8, 8), :] = total

    emit(even, 0)
    product(even, even, 0)
    now, later = even, odd
    for degree in range(DEGREE):

        def plane(z, carry, now=now, later=later, degree=degree):
            value = now[z]
            beside = now[z - 1] + now[z + 1]
            beside = beside + pltpu.roll(value, 1, 0) + pltpu.roll(value, wide_y - 1, 0)
            beside = beside + jnp.where(lane == 0, 0.0, pltpu.roll(value, 1, 1))
            beside = beside + jnp.where(lane == LANES - 1, 0.0, pltpu.roll(value, LANES - 1, 1))
            fresh = alpha[z] * value - beta[z] * beside
            if degree == 0:
                later[z] = 0.5 * fresh
            else:
                later[z] = fresh - later[z]
            return carry

        lax.fori_loop(degree + 1, planes - 1 - degree, plane, 0, unroll=2)
        emit(later, degree + 1)
        product(now, later, 2 * degree + 1)
        product(later, later, 2 * degree + 2)
        now, later = later, now

    slots = parts.shape[0] // 8
    for slot in range(2 * DEGREE + 1, slots):
        parts[pl.ds(slot * 8, 8), :] = jnp.zeros((8, LANES), jnp.float32)
    value = parts[pl.ds(0, slots, stride=8), :]
    error = jnp.zeros_like(value)
    for row in range(1, 8):
        value, extra = two_sum(value, parts[pl.ds(row, slots, stride=8), :])
        error = error + extra
    step = LANES // 2
    while step:
        value, extra = two_sum(value, pltpu.roll(value, step, 1))
        error = error + pltpu.roll(error, step, 1) + extra
        step //= 2
    value, error = quick_two_sum(value, error)
    lane_s = lane_of((slots, LANES))
    row_s = lax.broadcasted_iota(jnp.int32, (slots, LANES), 0)
    placed = jnp.where(lane_s == MOMENT_LANE + row_s, value, 0.0)
    placed = placed + jnp.where(lane_s == LOW_LANE + row_s, error, 0.0)
    moments = jnp.sum(placed, axis=0, keepdims=True)

    lane_v = lane_of((FIELDS, LANES))
    inlets = index.shape[0] // order.shape[0]

    def plate(at, carry):
        start = order[at] * inlets
        total = None
        for slot in range(inlets):
            cell = index[start + slot]
            row = pl.multiple_of((cell >> 7) * FIELDS, FIELDS)
            picked = jnp.where(lane_v == (cell & 127), basis[pl.ds(row, FIELDS), :], 0.0)
            total = picked if total is None else total + picked
        sums[pl.ds(pl.multiple_of(at * FIELDS, FIELDS), FIELDS), :] = total
        return carry

    lax.fori_loop(0, order.shape[0], plate, 0, unroll=2)
    tiles = payload.shape[0]
    lane_t = lane_of((tiles, LANES))
    out = jnp.broadcast_to(moments, (tiles, LANES))
    for slot in range(OWNED * FIELDS):
        column = sums[pl.ds(slot, tiles, stride=OWNED * FIELDS), :]
        out = jnp.where(lane_t == slot, jnp.sum(column, axis=1, keepdims=True), out)
    payload[...] = out


def sum_rows(rows):
    count = rows.shape[0]
    value = rows[pl.ds(0, 8), :]
    error = jnp.zeros_like(value)
    for at in range(8, count, 8):
        value, extra = two_sum(value, rows[pl.ds(at, 8), :])
        error = error + extra
    for step in (4, 2, 1):
        value, extra = two_sum(value, pltpu.roll(value, step, 0))
        error = error + pltpu.roll(error, step, 0) + extra
    lane = lane_of((8, LANES))
    shifted = pltpu.roll(error, LOW_LANE - MOMENT_LANE, 1)
    return value + jnp.where(lane < MOMENT_LANE, error, 0.0) + jnp.where(lane >= LOW_LANE, shifted, 0.0)


def rows_kernel(rows, out):
    out[...] = sum_rows(rows)


def fold(moments, lane):
    total = jnp.zeros_like(moments)
    for j in range(1, 2 * DEGREE + 1):
        total = jnp.where(lane == LOW_LANE - j, moments[:, j : j + 1], total)
    return jnp.where(lane >= LOW_LANE, pltpu.roll(moments, LOW_LANE, 1), total)


def shift(row, amount):
    return pltpu.roll(row, (-amount) % LANES, 1)


def apply_operator(coeffs):
    count = len(coeffs)
    terms = [[] for _ in range(count + 1)]
    for j, value in enumerate(coeffs):
        terms[j].append(dd_add(dd_scale(value, 8.0), dd_neg(value)))
        if j == 0:
            terms[1].append(dd_scale(value, 8.0))
        else:
            terms[j + 1].append(dd_scale(value, 4.0))
            terms[j - 1].append(dd_scale(value, 4.0))
    return [dd_sum(group) for group in terms]


def multiply(left, right):
    terms = [[] for _ in range(len(left) + len(right) - 1)]
    for i, a in enumerate(left):
        for j, b in enumerate(right):
            half = dd_scale(dd_mul(a, b), 0.5)
            terms[i + j].append(half)
            terms[abs(i - j)].append(half)
    return [dd_sum(group) for group in terms]


def square(values):
    terms = [[] for _ in range(2 * len(values) - 1)]
    for i, a in enumerate(values):
        for j in range(i, len(values)):
            term = dd_mul(a, values[j])
            if i == j:
                term = dd_scale(term, 0.5)
            terms[i + j].append(term)
            terms[j - i].append(term)
    return [dd_sum(group) for group in terms]


def galerkin(folded):
    high, low = folded
    moment = high + low
    beside = dd_add((shift(high, 1), shift(low, 1)), (shift(high, -1), shift(low, -1)))
    eight = dd_scale(folded, 8.0)
    weight = dd_add(dd_add(dd_scale(beside, 4.0), eight), dd_neg(folded))
    weight = weight[0] + weight[1]

    def entry(source, j):
        return jnp.broadcast_to(source[:, LOW_LANE + j : LOW_LANE + j + 1], source.shape)

    weights = [entry(weight, j) for j in range(7)]
    rhs = [entry(moment, j) for j in range(4)]
    matrix = [[0.5 * (weights[i + j] + weights[abs(i - j)]) for j in range(4)] for i in range(4)]
    for k in range(4):
        for i in range(k + 1, 4):
            factor = matrix[i][k] / matrix[k][k]
            for j in range(k + 1, i + 1):
                matrix[i][j] = matrix[i][j] - factor * matrix[j][k]
            rhs[i] = rhs[i] - factor * rhs[k]
    result = [None] * 4
    for i in range(3, -1, -1):
        value = rhs[i]
        for j in range(i + 1, 4):
            value = value - matrix[j][i] * result[j]
        result[i] = value / matrix[i][i]
    return result


def final_kernel(rows, basis, last, conductance, level, solution, residual, flow, scale=1.0):
    row = sum_rows(rows)
    lane = lane_of((8, LANES))
    high = pltpu.roll(row, LANES - MOMENT_LANE, 1)
    low = pltpu.roll(row, LANES - LOW_LANE, 1)
    valid = lane <= 2 * DEGREE
    high, low = quick_two_sum(jnp.where(valid, high, 0.0), jnp.where(valid, low, 0.0))
    first = (high[:, 0:1], low[:, 0:1])
    second = (high[:, 1:2], low[:, 1:2])
    even = lane % 2 == 0
    base = (jnp.where(even, first[0], second[0]), jnp.where(even, first[1], second[1]))
    twice = dd_add(dd_scale((high, low), 2.0), dd_neg(base))
    mu = tuple(jnp.where(valid, value, 0.0) for value in twice)
    mu = (fold(mu[0], lane), fold(mu[1], lane))
    zero = jnp.zeros((8, LANES), jnp.float32)
    first_coeffs = galerkin(mu)
    change = apply_operator([(value, zero) for value in first_coeffs])
    poly = [dd_neg(value) for value in change]
    poly[0] = dd_add(poly[0], (zero + 1.0, zero))
    nu = None
    for c, value in enumerate(square(poly)):
        if c == 0:
            overlap = mu
        else:
            up = (shift(mu[0], c), shift(mu[1], c))
            down = (shift(mu[0], -c), shift(mu[1], -c))
            overlap = dd_scale(dd_add(up, down), 0.5)
        term = dd_mul(value, overlap)
        nu = term if nu is None else dd_add(nu, term)
    second_coeffs = galerkin(nu)
    gain = multiply([(value, zero) for value in second_coeffs], poly)
    drop = apply_operator(gain)
    solved = list(gain)
    for j in range(4):
        solved[j] = dd_add(gain[j], (first_coeffs[j], zero))
    left = [dd_neg(value) for value in drop]
    for j in range(5):
        left[j] = dd_add(left[j], poly[j])
    solved = [value[0] + value[1] for value in solved]
    left = [value[0] + value[1] for value in left]

    cells = solution.shape[0]
    for at in range(0, cells, 8):
        fields = [basis[pl.ds(at * FIELDS + k, 8, stride=FIELDS), :] for k in range(FIELDS)]
        fields.append(last[pl.ds(at, 8), :])
        total = solved[0] * fields[0]
        rest = left[0] * fields[0]
        for k in range(1, DEGREE + 1):
            if k < FIELDS:
                total = total + solved[k] * fields[k]
            rest = rest + left[k] * fields[k]
        solution[pl.ds(at, 8), :] = total
        residual[pl.ds(at, 8), :] = rest

    weights = zero
    for k in range(FIELDS):
        weights = jnp.where(lane % FIELDS == k, solved[k], weights)
    header = row * weights
    for step in (4, 2, 1):
        header = header + shift(header, step)
    for q in range(OWNED):
        flow[q] = conductance[q] * (header[0, q * FIELDS] * scale - level[q])


VMEM = pl.BlockSpec(memory_space=pltpu.VMEM)
SMEM = pl.BlockSpec(memory_space=pltpu.SMEM)


def on_device(right_side, diagonal, inlet_index, plate_order, conductance, plate_level):
    cz, cy, nx = right_side.shape
    slabs, tiles = lax.axis_size("slab"), lax.axis_size("tile")
    plates, inlets = inlet_index.shape[2:]
    f32 = jnp.float32

    def both_ways(to_next, to_previous, axis):
        count = lax.axis_size(axis)
        forward = [(i, i + 1) for i in range(count - 1)]
        backward = [(target, source) for source, target in forward]
        return lax.ppermute(to_next, axis, forward), lax.ppermute(to_previous, axis, backward)

    own = jnp.stack([right_side, diagonal])
    before, after = both_ways(own[:, :, cy - HALO :], own[:, :, :HALO], "tile")
    own = jnp.concatenate([before, own, after], axis=2)
    low, high = both_ways(own, own, "slab")

    wide = (3 * cz, cy + 2 * HALO, nx)
    cells = cz * cy
    payload, basis, last = pl.pallas_call(
        basis_kernel,
        out_shape=(
            jax.ShapeDtypeStruct((tiles, LANES), f32),
            jax.ShapeDtypeStruct((cells * FIELDS, nx), f32),
            jax.ShapeDtypeStruct((cells, nx), f32),
        ),
        in_specs=[VMEM, VMEM, VMEM, SMEM, SMEM],
        out_specs=(VMEM, VMEM, VMEM),
        scratch_shapes=[
            pltpu.VMEM(wide, f32),
            pltpu.VMEM(wide, f32),
            pltpu.VMEM(wide, f32),
            pltpu.VMEM(wide, f32),
            pltpu.VMEM((24 * 8, nx), f32),
            pltpu.VMEM((plates * FIELDS, nx), f32),
        ],
        compiler_params=pltpu.CompilerParams(vmem_limit_bytes=32 * 1024 * 1024),
        name="basis",
    )(own, low, high, inlet_index.reshape(plates * inlets), plate_order)

    arrived = lax.all_to_all(payload.reshape(tiles, 1, LANES), "tile", 0, 0, tiled=True)
    row = pl.pallas_call(
        rows_kernel,
        out_shape=jax.ShapeDtypeStruct((8, LANES), f32),
        in_specs=[VMEM],
        out_specs=VMEM,
        name="rows",
    )(arrived.reshape(tiles, LANES))
    copies = jnp.broadcast_to(row[:1, None, :], (slabs, 1, LANES))
    arrived = lax.all_to_all(copies, "slab", 0, 0, tiled=True)
    arrived = arrived.reshape(slabs, LANES)
    if slabs % 8:
        arrived = jnp.pad(arrived, ((0, 8 - slabs % 8), (0, 0)))
    scale = float(1.0 / (slabs * tiles * inlets) ** 0.5)
    solution, residual, flow = pl.pallas_call(
        functools.partial(final_kernel, scale=scale),
        out_shape=(
            jax.ShapeDtypeStruct((cells, nx), f32),
            jax.ShapeDtypeStruct((cells, nx), f32),
            jax.ShapeDtypeStruct((OWNED,), f32),
        ),
        in_specs=[VMEM, VMEM, VMEM, SMEM, SMEM],
        out_specs=(VMEM, VMEM, SMEM),
        compiler_params=pltpu.CompilerParams(vmem_limit_bytes=16 * 1024 * 1024),
        name="final",
    )(arrived, basis, last, conductance, plate_level)
    return (solution.reshape(cz, cy, nx), residual.reshape(cz, cy, nx), flow)


def solution(mesh):
    in_specs = (
        P("slab", "tile", None),
        P("slab", "tile", None),
        P("slab", "tile", None, None),
        P(),
        P("tile"),
        P("tile"),
    )
    out_specs = (P("slab", "tile", None), P("slab", "tile", None), P("tile"))
    return jax.shard_map(
        on_device, mesh=mesh, in_specs=in_specs, out_specs=out_specs, check_vma=False
    )
```

time: 580 us -> 93.2 us (0.16)
  blocking collectives: 354 us -> 40.6 us
  starting transfers between devices: 105 us -> 18.1 us
  local copies, waits for them, and re-layouts: 64.6 us -> 1.62 us
  between operations: 27.2 us -> 0.75 us
  Pallas kernels: 0 us -> 24.1 us
  other arithmetic: 14.1 us -> 0.87 us
    psum x3 -> x0, blocking collectives: 354 us -> none  [the longest x2 248 us: on_device(): gram_vec = lax.psum(local_gram, ('slab', 'tile'))]
    ppermute x32 -> x4, starting transfers between devices: 105 us -> 18.1 us  [the longest x2 12.1 us: both_ways(): lax.ppermute(to_previous, axis, backward)]
    all_to_all x0 -> x2, blocking collectives: none -> 40.6 us  [the longest x1 29.3 us: on_device(): lax.all_to_all(payload.reshape(tiles, 1, LANES), 'tile', 0, 0, tiled=True)]
    gather x3 -> x0, local copies, waits for them, and re-layouts: 37.2 us -> none  [the longest x2 34.4 us: on_device(): picked = jnp.take(flat_field, inlet_index[0, 0], axis=0)]
    pallas_call x0 -> x3, Pallas kernels: none -> 24.1 us  [the longest x1 20 us: on_device(): pl.pallas_call(basis_kernel, out_shape=(jax.ShapeDtypeStruct((tiles, LANE...]
    another operation x4 -> x0, local copies, waits for them, and re-layouts: 19.6 us -> none  [the longest x2 19.1 us: local_products(): return jnp.stack([full[pair[0], pair[1]] for pair in GRAM_PAIRS])]
    another operation x14 -> x1, other arithmetic: 10.2 us -> 0.85 us  [on_device(): own = jnp.stack([right_side, diagonal])]
    slice x29 -> x0, local copies, waits for them, and re-layouts: 5.97 us -> none  [the longest x2 1.46 us: local_products(): return jnp.stack([full[pair[0], pair[1]] for pair in GRAM_PAIRS])]
  transfers between devices with their start and end apart: 32 -> 4, of which waited for: 15 -> 2; matrix products, arithmetic and copies ran while one was open for 0% -> 0% of each run, Pallas kernels for 0% -> 0%
where the time goes in v1:
time: 93.2 us; the launch traced here: 92.8 us
  blocking collectives  40.6 us (44%)
  Pallas kernels  24.1 us (26%)
  starting transfers between devices  18.1 us (19%)
  waiting for transfers between devices  6.72 us (7%)
  local copies, waits for them, and re-layouts  1.62 us (2%)
    all_to_all x1, blocking collectives, on_device(): lax.all_to_all(payload.reshape(tiles, 1, LANES), 'tile', 0, 0, tiled=True)  29.3 us
    pallas_call x1, Pallas kernels, on_device(): pl.pallas_call(basis_kernel, out_shape=(jax.ShapeDtypeStruct((tiles, LANE...  20 us
    ppermute x2, starting transfers between devices, both_ways(): lax.ppermute(to_previous, axis, backward)  12.1 us
    all_to_all x1, blocking collectives, on_device(): arrived = lax.all_to_all(copies, 'slab', 0, 0, tiled=True)  11.3 us
    ppermute x2, starting transfers between devices, both_ways(): lax.ppermute(to_next, axis, forward)  5.95 us
    ppermute x2, waiting for transfers between devices, both_ways(): lax.ppermute(to_previous, axis, backward)  3.7 us
    ppermute x2, waiting for transfers between devices, both_ways(): lax.ppermute(to_next, axis, forward)  3.02 us
    pallas_call x1, Pallas kernels, on_device(): pl.pallas_call(functools.partial(final_kernel, scale=scale), out_shape=(j...  2.66 us
  transfers between devices with their start and end apart: 4, of which 2 were waited for; matrix products, arithmetic and copies ran while one was open for 0% of the time, Pallas kernels for 0%

profile of v1, /device:TPU:1, one launch (start us, length us, event | category | flops | bytes accessed | tf_op | source)
XLA Modules:
  0.0 92.8 jit_solution(8928857287076309316)
XLA Ops:
  0.6 0.0 copy-start.3
  0.6 0.0 copy-start.4
  0.6 0.9 fusion
  1.5 4.0 %collective-permute-start = (f32[2,8,8,128]{3,2,1,0:T(8,128)S(1)}, f32[2,8,8,128]{3,2,1,0:T(8,128)S(1)}, u32[]{:S(2)}, u32[]{:S(2)}) collective-permute-start(f32[2,8,8,128]{3,2,1,0:T(8,128)S(1)} %get-tuple-element.15), channel_id=1, source_target_pairs={{0,1},{1,2},{2,3},{3,4},{4,5},{5,6},{6,7},{7,8},{8,9},{9,10},{10,1... | collective-permute-start | bytes 196616 | tf_op jit(solution)/shard_map/ppermute | solution.py:344
  5.5 0.0 copy-start.5
  5.6 1.3 %collective-permute-start.1 = (f32[2,8,8,128]{3,2,1,0:T(8,128)S(1)}, f32[2,8,8,128]{3,2,1,0:T(8,128)S(1)}, u32[]{:S(2)}, u32[]{:S(2)}) collective-permute-start(f32[2,8,8,128]{3,2,1,0:T(8,128)S(1)} %get-tuple-element.16), channel_id=1, source_target_pairs={{1,0},{2,1},{3,2},{4,3},{5,4},{6,5},{7,6},{8,7},{9,8},{10,9},{11,1... | collective-permute-start | bytes 196616 | tf_op jit(solution)/shard_map/ppermute | solution.py:344
  6.9 0.0 collective-permute-done
  6.9 3.7 %collective-permute-done.1 = f32[2,8,8,128]{3,2,1,0:T(8,128)S(1)} collective-permute-done((f32[2,8,8,128]{3,2,1,0:T(8,128)S(1)}, f32[2,8,8,128]{3,2,1,0:T(8,128)S(1)}, u32[]{:S(2)}, u32[]{:S(2)}) %collective-permute-start.1) | collective-permute-done | bytes 65568 | tf_op jit(solution)/shard_map/ppermute | solution.py:344
  10.6 0.0 copy-done.3
  10.6 0.0 copy-done.4
  10.6 10.8 %collective-permute-start.3 = (f32[2,8,32,128]{3,2,1,0:T(8,128)S(1)}, f32[2,8,32,128]{3,2,1,0:T(8,128)S(1)}, u32[]{:S(2)}, u32[]{:S(2)}) collective-permute-start(f32[2,8,32,128]{3,2,1,0:T(8,128)S(1)} %pad_maximum_fusion.own), channel_id=1, source_target_pairs={{96,0},{192,96},{288,192},{384,288},{480,384},{576,480},{672,576},... | collective-permute-start | bytes 786440 | tf_op jit(solution)/shard_map/ppermute | solution.py:344
  21.4 1.9 %collective-permute-start.2 = (f32[2,8,32,128]{3,2,1,0:T(8,128)S(1)}, f32[2,8,32,128]{3,2,1,0:T(8,128)S(1)}, u32[]{:S(2)}, u32[]{:S(2)}) collective-permute-start(f32[2,8,32,128]{3,2,1,0:T(8,128)S(1)} %pad_maximum_fusion.own), channel_id=1, source_target_pairs={{0,96},{96,192},{192,288},{288,384},{384,480},{480,576},{576,672},... | collective-permute-start | bytes 786440 | tf_op jit(solution)/shard_map/ppermute | solution.py:344
  23.4 0.0 copy-done.5
  23.4 0.1 copy.10
  23.5 0.0 copy-start
  23.5 0.1 reshape.27.index
  23.6 0.0 collective-permute-done.3.high
  23.6 3.0 %collective-permute-done.2.low = f32[2,8,32,128]{3,2,1,0:T(8,128)S(1)} collective-permute-done((f32[2,8,32,128]{3,2,1,0:T(8,128)S(1)}, f32[2,8,32,128]{3,2,1,0:T(8,128)S(1)}, u32[]{:S(2)}, u32[]{:S(2)}) %collective-permute-start.2) | collective-permute-done | bytes 262176 | tf_op jit(solution)/shard_map/ppermute | solution.py:344
  26.7 0.0 copy-done
  26.7 20.0 %basis.1 = (f32[96,128]{1,0:T(8,128)S(1)}, f32[1024,128]{1,0:T(8,128)S(1)}, f32[128,128]{1,0:T(8,128)S(1)}) custom-call(f32[2,8,32,128]{3,2,1,0:T(8,128)S(1)} %pad_maximum_fusion.own, f32[2,8,32,128]{3,2,1,0:T(8,128)S(1)} %collective-permute-done.2.low, f32[2,8,32,128]{3,2,1,0:T(8,128)S(1)} %collective-permute-done.3.high, s32[6144]{0:T(1024)S(1)} %reshape.27.index, ...), custom_call_target="tpu_custom_call" | custom-call | tf_op jit(solution)/shard_map/basis/pallas_call | solution.py:353
  46.6 29.3 %all_to_all.10 = f32[96,1,128]{2,1,0:T(1,128)} all-to-all(f32[96,1,128]{2,1,0:T(1,128)S(1)} %bitcast.13), channel_id=1, replica_groups=mesh['slab'=8,'tile'=96] {'tile'}, dimensions={0} | all-to-all | bytes 98304 | tf_op jit(solution)/shard_map/all_to_all | solution.py:374
  75.9 1.5 %rows.1 = f32[8,128]{1,0:T(8,128)} custom-call(f32[96,128]{1,0:T(8,128)} %bitcast.19), custom_call_target="tpu_custom_call" | custom-call | tf_op jit(solution)/shard_map/rows/pallas_call | solution.py:375
  77.4 0.7 slice_bitcast_fusion
  78.1 11.3 %all_to_all.11 = f32[8,1,128]{2,1,0:T(1,128)S(1)} all-to-all(f32[8,1,128]{2,1,0:T(1,128)S(1)} %broadcast_in_dim.9), channel_id=1, replica_groups=mesh['slab'=8,'tile'=96] {'slab'}, dimensions={0} | all-to-all | bytes 8192 | tf_op jit(solution)/shard_map/all_to_all | solution.py:383
  89.4 0.0 copy-start.1
  89.4 0.0 copy-start.2
  89.4 0.7 copy-done.1
  90.1 0.0 copy-done.2
  90.1 2.7 %final.1 = (f32[128,128]{1,0:T(8,128)}, f32[128,128]{1,0:T(8,128)}, f32[4]{0:T(128)}) custom-call(f32[8,128]{1,0:T(8,128)S(1)} %bitcast.14, f32[1024,128]{1,0:T(8,128)S(1)} %get-tuple-element.10.basis, f32[128,128]{1,0:T(8,128)S(1)} %get-tuple-element.11.last, f32[4]{0:T(128)S(1)} %copy-done.1, f32[4]{0:T(128)S(1)} %copy-done.2), custom_call_target="tpu_custom_call" | custom-call | tf_op jit(solution)/shard_map/final/pallas_call | solution.py:388
  (2 shorter events, 0.0 us)
Async XLA Ops:
  0.6 9.9 %copy-start.3 = (f32[8,16,128]{2,1,0:T(8,128)S(1)}, f32[8,16,128]{2,1,0:T(8,128)}, u32[]{:S(2)}) copy-start(f32[8,16,128]{2,1,0:T(8,128)} %param.6) | copy-start | bytes 196612
  0.6 9.9 %copy-start.4 = (f32[8,16,128]{2,1,0:T(8,128)S(1)}, f32[8,16,128]{2,1,0:T(8,128)}, u32[]{:S(2)}) copy-start(f32[8,16,128]{2,1,0:T(8,128)} %param.7) | copy-start | bytes 196612
  1.5 5.4 %collective-permute-start = (f32[2,8,8,128]{3,2,1,0:T(8,128)S(1)}, f32[2,8,8,128]{3,2,1,0:T(8,128)S(1)}, u32[]{:S(2)}, u32[]{:S(2)}) collective-permute-start(f32[2,8,8,128]{3,2,1,0:T(8,128)S(1)} %get-tuple-element.15), channel_id=1, source_target_pairs={{0,1},{1,2},{2,3},{3,4},{4,5},{5,6},{6,7},{7,8},{8,9},{9,10},{10,1... | collective-permute-start | bytes 196616 | tf_op jit(solution)/shard_map/ppermute | solution.py:344
  5.5 17.8 %copy-start.5 = (s32[1,1,384,16]{2,3,1,0:T(8,128)S(1)}, s32[1,1,384,16]{2,3,1,0:T(8,128)}, u32[]{:S(2)}) copy-start(s32[1,1,384,16]{2,3,1,0:T(8,128)} %param.8) | copy-start | bytes 73732
  5.6 5.0 %collective-permute-start.1 = (f32[2,8,8,128]{3,2,1,0:T(8,128)S(1)}, f32[2,8,8,128]{3,2,1,0:T(8,128)S(1)}, u32[]{:S(2)}, u32[]{:S(2)}) collective-permute-start(f32[2,8,8,128]{3,2,1,0:T(8,128)S(1)} %get-tuple-element.16), channel_id=1, source_target_pairs={{1,0},{2,1},{3,2},{4,3},{5,4},{6,5},{7,6},{8,7},{9,8},{10,9},{11,1... | collective-permute-start | bytes 196616 | tf_op jit(solution)/shard_map/ppermute | solution.py:344
  10.6 13.0 %collective-permute-start.3 = (f32[2,8,32,128]{3,2,1,0:T(8,128)S(1)}, f32[2,8,32,128]{3,2,1,0:T(8,128)S(1)}, u32[]{:S(2)}, u32[]{:S(2)}) collective-permute-start(f32[2,8,32,128]{3,2,1,0:T(8,128)S(1)} %pad_maximum_fusion.own), channel_id=1, source_target_pairs={{96,0},{192,96},{288,192},{384,288},{480,384},{576,480},{672,576},... | collective-permute-start | bytes 786440 | tf_op jit(solution)/shard_map/ppermute | solution.py:344
  21.4 5.2 %collective-permute-start.2 = (f32[2,8,32,128]{3,2,1,0:T(8,128)S(1)}, f32[2,8,32,128]{3,2,1,0:T(8,128)S(1)}, u32[]{:S(2)}, u32[]{:S(2)}) collective-permute-start(f32[2,8,32,128]{3,2,1,0:T(8,128)S(1)} %pad_maximum_fusion.own), channel_id=1, source_target_pairs={{0,96},{96,192},{192,288},{288,384},{384,480},{480,576},{576,672},... | collective-permute-start | bytes 786440 | tf_op jit(solution)/shard_map/ppermute | solution.py:344
  23.5 3.2 %copy-start = (s32[384]{0:T(512)S(1)}, s32[384]{0:T(512)}, u32[]{:S(2)}) copy-start(s32[384]{0:T(512)} %order.1) | copy-start | bytes 4612
  89.4 0.7 copy-start.1
  89.4 0.7 copy-start.2

commit v2 on v1

--- a/solution.py
+++ b/solution.py
@@ -14,6 +14,8 @@
 LANES = 128
 MOMENT_LANE = 32
 LOW_LANE = 64
+SLAB = ("x", "core")
+TILE = ("z", "y")
 
 
 def two_sum(a, b):
@@ -71,23 +73,61 @@
     return lax.broadcasted_iota(jnp.int32, shape, len(shape) - 1)
 
 
-def basis_kernel(own, low, high, index, order, payload, basis, last, alpha, beta, even, odd, parts, sums):
+def prepare_kernel(index, order, conductance, level, hot, table, plate_of, owner):
+    plate_of[...] = order[...]
+    cells = index[...]
+    inlets, plates = cells.shape
+    lane = lane_of((inlets, LANES))
+    slot = lax.broadcasted_iota(jnp.int32, (inlets, LANES), 0)
+    packed = LANES // inlets
+    for row in range(plates // packed):
+        total = jnp.zeros((inlets, LANES), jnp.int32)
+        for place in range(packed):
+            at = row * packed + place
+            cell = jnp.broadcast_to(cells[:, at : at + 1], (inlets, LANES))
+            hot[pl.ds(at * inlets, inlets), :] = jnp.where(lane == (cell & 127), 1.0, 0.0)
+            total = total + jnp.where(lane == slot + place * inlets, (cell >> 7) * FIELDS, 0)
+        table[pl.ds(row, 1), :] = jnp.sum(total, axis=0, keepdims=True)
+    lane = lane_of((8, LANES))
+    first = lax.broadcasted_iota(jnp.int32, (8, LANES), 0) == 0
+    values = jnp.zeros((8, LANES), jnp.float32)
+    for q in range(OWNED):
+        values = jnp.where(lane == q * FIELDS, jnp.where(first, conductance[q], level[q]), values)
+    owner[...] = values
+
+
+def basis_kernel(
+    own, low, high, hot, table, order, payload, basis, last,
+    alpha, beta, even, odd, parts, sums, index, plate_of, arrivals,
+):
+    copies = [
+        pltpu.make_async_copy(table, index, arrivals.at[0]),
+        pltpu.make_async_copy(order, plate_of, arrivals.at[1]),
+    ]
+    for copy in copies:
+        copy.start()
     cz = own.shape[1]
     wide_y = own.shape[2]
     cy = wide_y - 2 * HALO
     for place, source in enumerate((low, own, high)):
         at = pl.ds(place * cz, cz)
-        even[at] = source[0]
+        even[at, HALO : HALO + wide_y, :] = source[0]
         diag = source[1]
         inside = jnp.where(diag > 0.0, 0.25, 0.0)
         beta[at] = inside
         alpha[at] = (diag - 1.0) * inside
     lane = lane_of((wide_y, LANES))
     planes = 3 * cz
+    edge = jnp.zeros((planes, HALO, LANES), jnp.float32)
+    for field in (even, odd):
+        field[:, :HALO, :] = edge
+        field[:, HALO + wide_y :, :] = edge
+    rows = pl.ds(HALO, wide_y)
+    inner = pl.ds(2 * HALO, cy)
 
     def emit(field, degree):
         for z in range(cz):
-            value = field[cz + z, HALO : HALO + cy, :]
+            value = field[cz + z, inner, :]
             if degree < FIELDS:
                 basis[pl.ds(z * cy * FIELDS + degree, cy, stride=FIELDS), :] = value
             else:
@@ -96,7 +136,7 @@
     def product(first, second, slot):
         total = None
         for z in range(cz):
-            term = first[cz + z, HALO : HALO + cy, :] * second[cz + z, HALO : HALO + cy, :]
+            term = first[cz + z, inner, :] * second[cz + z, inner, :]
             term = term[:8] + term[8:]
             total = term if total is None else total + term
         parts[pl.ds(slot * 8, 8), :] = total
@@ -106,20 +146,20 @@
     now, later = even, odd
     for degree in range(DEGREE):
 
-        def plane(z, carry, now=now, later=later, degree=degree):
-            value = now[z]
-            beside = now[z - 1] + now[z + 1]
-            beside = beside + pltpu.roll(value, 1, 0) + pltpu.roll(value, wide_y - 1, 0)
+        def plane(z, now=now, later=later, degree=degree):
+            value = now[z, rows, :]
+            beside = now[z - 1, rows, :] + now[z + 1, rows, :]
+            beside = beside + now[z, pl.ds(HALO - 1, wide_y), :] + now[z, pl.ds(HALO + 1, wide_y), :]
             beside = beside + jnp.where(lane == 0, 0.0, pltpu.roll(value, 1, 1))
             beside = beside + jnp.where(lane == LANES - 1, 0.0, pltpu.roll(value, LANES - 1, 1))
             fresh = alpha[z] * value - beta[z] * beside
             if degree == 0:
-                later[z] = 0.5 * fresh
+                later[z, rows, :] = 0.5 * fresh
             else:
-                later[z] = fresh - later[z]
-            return carry
-
-        lax.fori_loop(degree + 1, planes - 1 - degree, plane, 0, unroll=2)
+                later[z, rows, :] = fresh - later[z, rows, :]
+
+        for z in range(degree + 1, planes - 1 - degree):
+            plane(z)
         emit(later, degree + 1)
         product(now, later, 2 * degree + 1)
         product(later, later, 2 * degree + 2)
@@ -145,28 +185,39 @@
     placed = placed + jnp.where(lane_s == LOW_LANE + row_s, error, 0.0)
     moments = jnp.sum(placed, axis=0, keepdims=True)
 
-    lane_v = lane_of((FIELDS, LANES))
-    inlets = index.shape[0] // order.shape[0]
+    for copy in copies:
+        copy.wait()
+    plates = sums.shape[0] // FIELDS
+    inlets = hot.shape[0] // plates
 
     def plate(at, carry):
-        start = order[at] * inlets
-        total = None
+        of = plate_of[at]
+        start = pl.multiple_of(of * inlets, inlets)
+        line, place = of >> 3, (of & 7) * inlets
+        totals = [None, None]
         for slot in range(inlets):
-            cell = index[start + slot]
-            row = pl.multiple_of((cell >> 7) * FIELDS, FIELDS)
-            picked = jnp.where(lane_v == (cell & 127), basis[pl.ds(row, FIELDS), :], 0.0)
-            total = picked if total is None else total + picked
-        sums[pl.ds(pl.multiple_of(at * FIELDS, FIELDS), FIELDS), :] = total
+            row = pl.multiple_of(index[line, place + slot], FIELDS)
+            picked = basis[pl.ds(row, FIELDS), :] * hot[pl.ds(start + slot, FIELDS, stride=0), :]
+            side = slot % 2
+            totals[side] = picked if totals[side] is None else totals[side] + picked
+        sums[pl.ds(pl.multiple_of(at * FIELDS, FIELDS), FIELDS), :] = totals[0] + totals[1]
         return carry
 
-    lax.fori_loop(0, order.shape[0], plate, 0, unroll=2)
-    tiles = payload.shape[0]
+    lax.fori_loop(0, plates, plate, 0, unroll=8)
+    tiles = plates // OWNED
     lane_t = lane_of((tiles, LANES))
     out = jnp.broadcast_to(moments, (tiles, LANES))
     for slot in range(OWNED * FIELDS):
         column = sums[pl.ds(slot, tiles, stride=OWNED * FIELDS), :]
         out = jnp.where(lane_t == slot, jnp.sum(column, axis=1, keepdims=True), out)
-    payload[...] = out
+    for at in range(0, payload.shape[0], tiles):
+        payload[pl.ds(at, tiles), :] = out
+
+
+def with_error(value, error):
+    lane = lane_of(value.shape)
+    shifted = pltpu.roll(error, LOW_LANE - MOMENT_LANE, 1)
+    return value + jnp.where(lane < MOMENT_LANE, error, 0.0) + jnp.where(lane >= LOW_LANE, shifted, 0.0)
 
 
 def sum_rows(rows):
@@ -179,13 +230,19 @@
     for step in (4, 2, 1):
         value, extra = two_sum(value, pltpu.roll(value, step, 0))
         error = error + pltpu.roll(error, step, 0) + extra
-    lane = lane_of((8, LANES))
-    shifted = pltpu.roll(error, LOW_LANE - MOMENT_LANE, 1)
-    return value + jnp.where(lane < MOMENT_LANE, error, 0.0) + jnp.where(lane >= LOW_LANE, shifted, 0.0)
+    return with_error(value, error)
 
 
 def rows_kernel(rows, out):
-    out[...] = sum_rows(rows)
+    count = out.shape[0] // 2
+    value = rows[pl.ds(0, count), :]
+    error = jnp.zeros_like(value)
+    for at in range(count, rows.shape[0], count):
+        value, extra = two_sum(value, rows[pl.ds(at, count), :])
+        error = error + extra
+    value = with_error(value, error)
+    out[pl.ds(0, count), :] = value
+    out[pl.ds(count, count), :] = value
 
 
 def fold(moments, lane):
@@ -263,7 +320,7 @@
     return result
 
 
-def final_kernel(rows, basis, last, conductance, level, solution, residual, flow, scale=1.0):
+def final_kernel(rows, basis, last, owner, solution, residual, flow, scale=1.0):
     row = sum_rows(rows)
     lane = lane_of((8, LANES))
     high = pltpu.roll(row, LANES - MOMENT_LANE, 1)
@@ -323,8 +380,9 @@
     header = row * weights
     for step in (4, 2, 1):
         header = header + shift(header, step)
+    result = owner[0:1, :] * (header[0:1, :] * scale - owner[1:2, :])
     for q in range(OWNED):
-        flow[q] = conductance[q] * (header[0, q * FIELDS] * scale - level[q])
+        flow[q] = result[0, q * FIELDS]
 
 
 VMEM = pl.BlockSpec(memory_space=pltpu.VMEM)
@@ -333,7 +391,8 @@
 
 def on_device(right_side, diagonal, inlet_index, plate_order, conductance, plate_level):
     cz, cy, nx = right_side.shape
-    slabs, tiles = lax.axis_size("slab"), lax.axis_size("tile")
+    tiles = lax.axis_size(TILE)
+    devices = lax.axis_size(SLAB) * tiles
     plates, inlets = inlet_index.shape[2:]
     f32 = jnp.float32
 
@@ -344,47 +403,67 @@
         return lax.ppermute(to_next, axis, forward), lax.ppermute(to_previous, axis, backward)
 
     own = jnp.stack([right_side, diagonal])
-    before, after = both_ways(own[:, :, cy - HALO :], own[:, :, :HALO], "tile")
+    before, after = both_ways(own[:, :, cy - HALO :], own[:, :, :HALO], TILE)
     own = jnp.concatenate([before, own, after], axis=2)
-    low, high = both_ways(own, own, "slab")
+    low, high = both_ways(own, own, SLAB)
+
+    hot, table, order, owner = pl.pallas_call(
+        prepare_kernel,
+        out_shape=(
+            jax.ShapeDtypeStruct((plates * inlets, LANES), f32),
+            jax.ShapeDtypeStruct((plates * inlets // LANES, LANES), jnp.int32),
+            jax.ShapeDtypeStruct((plates,), jnp.int32),
+            jax.ShapeDtypeStruct((8, LANES), f32),
+        ),
+        in_specs=[VMEM, VMEM, SMEM, SMEM],
+        out_specs=(VMEM,) * 4,
+        compiler_params=pltpu.CompilerParams(vmem_limit_bytes=4 * 1024 * 1024),
+        cost_estimate=pl.CostEstimate(flops=800000, bytes_accessed=3200000, transcendentals=0),
+        name="prepare",
+    )(inlet_index[0, 0].T, plate_order, conductance, plate_level)
 
     wide = (3 * cz, cy + 2 * HALO, nx)
+    tall = (wide[0], wide[1] + 2 * HALO, nx)
     cells = cz * cy
+    copies = lax.axis_size("x")
     payload, basis, last = pl.pallas_call(
         basis_kernel,
         out_shape=(
-            jax.ShapeDtypeStruct((tiles, LANES), f32),
+            jax.ShapeDtypeStruct((copies * tiles, LANES), f32),
             jax.ShapeDtypeStruct((cells * FIELDS, nx), f32),
             jax.ShapeDtypeStruct((cells, nx), f32),
         ),
-        in_specs=[VMEM, VMEM, VMEM, SMEM, SMEM],
+        in_specs=[VMEM] * 6,
         out_specs=(VMEM, VMEM, VMEM),
         scratch_shapes=[
             pltpu.VMEM(wide, f32),
             pltpu.VMEM(wide, f32),
-            pltpu.VMEM(wide, f32),
-            pltpu.VMEM(wide, f32),
+            pltpu.VMEM(tall, f32),
+            pltpu.VMEM(tall, f32),
             pltpu.VMEM((24 * 8, nx), f32),
             pltpu.VMEM((plates * FIELDS, nx), f32),
+            pltpu.SMEM((plates * inlets // LANES, LANES), jnp.int32),
+            pltpu.SMEM((plates,), jnp.int32),
+            pltpu.SemaphoreType.DMA((2,)),
         ],
-        compiler_params=pltpu.CompilerParams(vmem_limit_bytes=32 * 1024 * 1024),
+        compiler_params=pltpu.CompilerParams(vmem_limit_bytes=8 * 1024 * 1024),
         name="basis",
-    )(own, low, high, inlet_index.reshape(plates * inlets), plate_order)
-
-    arrived = lax.all_to_all(payload.reshape(tiles, 1, LANES), "tile", 0, 0, tiled=True)
-    row = pl.pallas_call(
+    )(own, low, high, hot, table, order)
+
+    group = copies * lax.axis_size("z")
+    width = lax.axis_size("y")
+    arrived = lax.all_to_all(payload.reshape(group, width, LANES), ("x", "z"), 0, 0, tiled=True)
+    ends = lax.axis_size("core") * width
+    rows = pl.pallas_call(
         rows_kernel,
-        out_shape=jax.ShapeDtypeStruct((8, LANES), f32),
+        out_shape=jax.ShapeDtypeStruct((ends, LANES), f32),
         in_specs=[VMEM],
         out_specs=VMEM,
+        compiler_params=pltpu.CompilerParams(vmem_limit_bytes=2 * 1024 * 1024),
         name="rows",
-    )(arrived.reshape(tiles, LANES))
-    copies = jnp.broadcast_to(row[:1, None, :], (slabs, 1, LANES))
-    arrived = lax.all_to_all(copies, "slab", 0, 0, tiled=True)
-    arrived = arrived.reshape(slabs, LANES)
-    if slabs % 8:
-        arrived = jnp.pad(arrived, ((0, 8 - slabs % 8), (0, 0)))
-    scale = float(1.0 / (slabs * tiles * inlets) ** 0.5)
+    )(arrived.reshape(group * width, LANES))
+    arrived = lax.all_to_all(rows.reshape(ends, 1, LANES), ("core", "y"), 0, 0, tiled=True)
+    scale = float(1.0 / (devices * inlets) ** 0.5)
     solution, residual, flow = pl.pallas_call(
         functools.partial(final_kernel, scale=scale),
         out_shape=(
@@ -392,24 +471,27 @@
             jax.ShapeDtypeStruct((cells, nx), f32),
             jax.ShapeDtypeStruct((OWNED,), f32),
         ),
-        in_specs=[VMEM, VMEM, VMEM, SMEM, SMEM],
+        in_specs=[VMEM, VMEM, VMEM, VMEM],
         out_specs=(VMEM, VMEM, SMEM),
-        compiler_params=pltpu.CompilerParams(vmem_limit_bytes=16 * 1024 * 1024),
+        compiler_params=pltpu.CompilerParams(vmem_limit_bytes=4 * 1024 * 1024),
         name="final",
-    )(arrived, basis, last, conductance, plate_level)
+    )(arrived.reshape(ends, LANES), basis, last, owner)
     return (solution.reshape(cz, cy, nx), residual.reshape(cz, cy, nx), flow)
 
 
 def solution(mesh):
+    slabs, tiles = mesh.devices.shape
+    chips = mesh.devices.reshape(slabs // 2, 2, tiles // 8, 8)
+    fine = jax.sharding.Mesh(chips, SLAB + TILE)
     in_specs = (
-        P("slab", "tile", None),
-        P("slab", "tile", None),
-        P("slab", "tile", None, None),
+        P(SLAB, TILE, None),
+        P(SLAB, TILE, None),
+        P(SLAB, TILE, None, None),
         P(),
-        P("tile"),
-        P("tile"),
+        P(TILE),
+        P(TILE),
     )
-    out_specs = (P("slab", "tile", None), P("slab", "tile", None), P("tile"))
+    out_specs = (P(SLAB, TILE, None), P(SLAB, TILE, None), P(TILE))
     return jax.shard_map(
-        on_device, mesh=mesh, in_specs=in_specs, out_specs=out_specs, check_vma=False
+        on_device, mesh=fine, in_specs=in_specs, out_specs=out_specs, check_vma=False
     )

time: 93.2 us -> 91.8 us (0.985)
  waiting for transfers between devices: 6.72 us -> 3.71 us
  Pallas kernels: 24.1 us -> 21.9 us
  blocking collectives: 40.6 us -> 42.5 us
  local copies, waits for them, and re-layouts: 1.62 us -> 2.72 us
    ppermute x2, waiting for transfers between devices: 3.02 us -> 0.01 us  [both_ways(): lax.ppermute(to_next, axis, forward)]
    unnamed x13 -> x8, local copies, waits for them, and re-layouts: 0.81 us -> 2.72 us
    all_to_all x2, blocking collectives: 40.6 us -> 42.5 us  [the longest x1 26.4 us: on_device(): lax.all_to_all(payload.reshape(group, width, LANES), ('x', 'z'), 0, 0, ti...]
    pallas_call x2 -> x3, Pallas kernels: 21.4 us -> 19.8 us  [the longest x1 17.7 us: on_device(): pl.pallas_call(basis_kernel, out_shape=(jax.ShapeDtypeStruct((copies * ti...]
  transfers between devices with their start and end apart: 4 -> 4, of which waited for: 2 -> 1; matrix products, arithmetic and copies ran while one was open for 0% -> 0% of each run, Pallas kernels for 0% -> 2%
where the time goes in v2:
time: 91.8 us; the launch traced here: 91.3 us
  blocking collectives  42.5 us (46%)
  Pallas kernels  21.9 us (24%)
  starting transfers between devices  18.1 us (20%)
  waiting for transfers between devices  3.71 us (4%)
  local copies, waits for them, and re-layouts  2.72 us (3%)
  other arithmetic  1.71 us (2%)
    all_to_all x1, blocking collectives, on_device(): lax.all_to_all(payload.reshape(group, width, LANES), ('x', 'z'), 0, 0, ti...  26.4 us
    pallas_call x1, Pallas kernels, on_device(): pl.pallas_call(basis_kernel, out_shape=(jax.ShapeDtypeStruct((copies * ti...  17.7 us
    all_to_all x1, blocking collectives, on_device(): lax.all_to_all(rows.reshape(ends, 1, LANES), ('core', 'y'), 0, 0, tiled=T...  16.1 us
    ppermute x2, starting transfers between devices, both_ways(): lax.ppermute(to_previous, axis, backward)  12.1 us
    ppermute x2, starting transfers between devices, both_ways(): lax.ppermute(to_next, axis, forward)  5.95 us
    ppermute x2, waiting for transfers between devices, both_ways(): lax.ppermute(to_previous, axis, backward)  3.7 us
    unnamed x8, local copies, waits for them, and re-layouts  2.72 us
    pallas_call x1, Pallas kernels, on_device(): pl.pallas_call(functools.partial(final_kernel, scale=scale), out_shape=(j...  2.12 us
  transfers between devices with their start and end apart: 4, of which 1 were waited for; matrix products, arithmetic and copies ran while one was open for 0% of the time, Pallas kernels for 2%

profile of v2, /device:TPU:1, one launch (start us, length us, event | category | flops | bytes accessed | tf_op | source)
XLA Modules:
  0.0 91.3 jit_solution(16393234067149812082)
XLA Ops:
  0.6 0.8 fusion
  1.5 4.0 %collective-permute-start = (f32[2,8,8,128]{3,2,1,0:T(8,128)S(1)}, f32[2,8,8,128]{3,2,1,0:T(8,128)S(1)}, u32[]{:S(2)}, u32[]{:S(2)}) collective-permute-start(f32[2,8,8,128]{3,2,1,0:T(8,128)S(1)} %get-tuple-element.23), channel_id=1, source_target_pairs={{0,1},{1,2},{2,3},{3,4},{4,5},{5,6},{6,7},{7,8},{8,9},{9,10},{10,1... | collective-permute-start | bytes 196616 | tf_op jit(solution)/shard_map/ppermute | solution.py:403
  5.5 1.3 %collective-permute-start.1 = (f32[2,8,8,128]{3,2,1,0:T(8,128)S(1)}, f32[2,8,8,128]{3,2,1,0:T(8,128)S(1)}, u32[]{:S(2)}, u32[]{:S(2)}) collective-permute-start(f32[2,8,8,128]{3,2,1,0:T(8,128)S(1)} %get-tuple-element.24), channel_id=1, source_target_pairs={{1,0},{2,1},{3,2},{4,3},{5,4},{6,5},{7,6},{8,7},{9,8},{10,9},{11,1... | collective-permute-start | bytes 196616 | tf_op jit(solution)/shard_map/ppermute | solution.py:403
  6.8 0.0 collective-permute-done
  6.8 3.7 %collective-permute-done.1 = f32[2,8,8,128]{3,2,1,0:T(8,128)S(1)} collective-permute-done((f32[2,8,8,128]{3,2,1,0:T(8,128)S(1)}, f32[2,8,8,128]{3,2,1,0:T(8,128)S(1)}, u32[]{:S(2)}, u32[]{:S(2)}) %collective-permute-start.1) | collective-permute-done | bytes 65568 | tf_op jit(solution)/shard_map/ppermute | solution.py:403
  10.5 0.9 pad_maximum_fusion.own
  11.4 10.8 %collective-permute-start.3 = (f32[2,8,32,128]{3,2,1,0:T(8,128)S(1)}, f32[2,8,32,128]{3,2,1,0:T(8,128)S(1)}, u32[]{:S(2)}, u32[]{:S(2)}) collective-permute-start(f32[2,8,32,128]{3,2,1,0:T(8,128)S(1)} %pad_maximum_fusion.own), channel_id=1, source_target_pairs={{96,0},{192,96},{288,192},{384,288},{480,384},{576,480},{672,576},... | collective-permute-start | bytes 786440 | tf_op jit(solution)/shard_map/ppermute | solution.py:403
  22.2 1.9 %collective-permute-start.2 = (f32[2,8,32,128]{3,2,1,0:T(8,128)S(1)}, f32[2,8,32,128]{3,2,1,0:T(8,128)S(1)}, u32[]{:S(2)}, u32[]{:S(2)}) collective-permute-start(f32[2,8,32,128]{3,2,1,0:T(8,128)S(1)} %pad_maximum_fusion.own), channel_id=1, source_target_pairs={{0,96},{96,192},{192,288},{288,384},{384,480},{480,576},{576,672},... | collective-permute-start | bytes 786440 | tf_op jit(solution)/shard_map/ppermute | solution.py:403
  24.2 0.0 copy-start
  24.2 0.7 copy-done
  24.9 0.0 copy-start.1
  24.9 0.7 copy-done.1
  25.6 0.0 copy-start.2
  25.6 0.7 copy-done.2
  26.2 0.0 copy-start.3
  26.2 0.7 copy-done.3
  26.9 1.9 %prepare.1 = (f32[6144,128]{1,0:T(8,128)S(1)}, s32[48,128]{1,0:T(8,128)S(1)}, s32[384]{0:T(512)S(1)}, f32[8,128]{1,0:T(8,128)S(1)}) custom-call(s32[16,384]{1,0:T(8,128)S(1)} %bitcast.17, s32[384]{0:T(512)S(1)} %copy-done.1, f32[4]{0:T(128)S(1)} %copy-done.2, f32[4]{0:T(128)S(1)} %copy-done.3), custom_call_target="tpu_custom_call" | custom-call | flops 800000 | bytes 3200000 | tf_op jit(solution)/shard_map/prepare/pallas_call | solution.py:410
  28.8 0.0 collective-permute-done.3.high
  28.8 0.0 collective-permute-done.2.low
  28.8 17.7 %basis.1 = (f32[384,128]{1,0:T(8,128)S(1)}, f32[1024,128]{1,0:T(8,128)S(1)}, f32[128,128]{1,0:T(8,128)S(1)}) custom-call(f32[2,8,32,128]{3,2,1,0:T(8,128)S(1)} %pad_maximum_fusion.own, f32[2,8,32,128]{3,2,1,0:T(8,128)S(1)} %collective-permute-done.2.low, f32[2,8,32,128]{3,2,1,0:T(8,128)S(1)} %collective-permute-done.3.high, ...), custom_call_target="tpu_custom_call" | custom-call | tf_op jit(solution)/shard_map/basis/pallas_call | solution.py:429
  46.6 26.4 %all_to_all.10 = f32[48,8,128]{2,1,0:T(8,128)S(1)} all-to-all(f32[48,8,128]{2,1,0:T(8,128)S(1)} %bitcast.14), channel_id=1, replica_groups=mesh['x'=4,'core'=2,'z'=12,'y'=8] {'x','z'}, dimensions={0} | all-to-all | bytes 393216 | tf_op jit(solution)/shard_map/all_to_all | solution.py:455
  72.9 0.1 rows.1
  73.1 16.1 %all_to_all.11 = f32[16,1,128]{2,1,0:T(1,128)S(1)} all-to-all(f32[16,1,128]{2,1,0:T(1,128)S(1)} %bitcast.16), channel_id=1, replica_groups=mesh['x'=4,'core'=2,'z'=12,'y'=8] {'core','y'}, dimensions={0} | all-to-all | bytes 16384 | tf_op jit(solution)/shard_map/all_to_all | solution.py:465
  89.2 2.1 %final.1 = (f32[128,128]{1,0:T(8,128)}, f32[128,128]{1,0:T(8,128)}, f32[4]{0:T(128)}) custom-call(f32[16,128]{1,0:T(8,128)S(1)} %bitcast.15, f32[1024,128]{1,0:T(8,128)S(1)} %get-tuple-element.17.basis, f32[128,128]{1,0:T(8,128)S(1)} %get-tuple-element.18.last, f32[8,128]{1,0:T(8,128)S(1)} %get-tuple-element.19.owner), custom_call_target="tpu_custom_call" | custom-call | tf_op jit(solution)/shard_map/final/pallas_call | solution.py:467
Async XLA Ops:
  1.5 5.4 %collective-permute-start = (f32[2,8,8,128]{3,2,1,0:T(8,128)S(1)}, f32[2,8,8,128]{3,2,1,0:T(8,128)S(1)}, u32[]{:S(2)}, u32[]{:S(2)}) collective-permute-start(f32[2,8,8,128]{3,2,1,0:T(8,128)S(1)} %get-tuple-element.23), channel_id=1, source_target_pairs={{0,1},{1,2},{2,3},{3,4},{4,5},{5,6},{6,7},{7,8},{8,9},{9,10},{10,1... | collective-permute-start | bytes 196616 | tf_op jit(solution)/shard_map/ppermute | solution.py:403
  5.5 5.0 %collective-permute-start.1 = (f32[2,8,8,128]{3,2,1,0:T(8,128)S(1)}, f32[2,8,8,128]{3,2,1,0:T(8,128)S(1)}, u32[]{:S(2)}, u32[]{:S(2)}) collective-permute-start(f32[2,8,8,128]{3,2,1,0:T(8,128)S(1)} %get-tuple-element.24), channel_id=1, source_target_pairs={{1,0},{2,1},{3,2},{4,3},{5,4},{6,5},{7,6},{8,7},{9,8},{10,9},{11,1... | collective-permute-start | bytes 196616 | tf_op jit(solution)/shard_map/ppermute | solution.py:403
  11.4 17.4 %collective-permute-start.3 = (f32[2,8,32,128]{3,2,1,0:T(8,128)S(1)}, f32[2,8,32,128]{3,2,1,0:T(8,128)S(1)}, u32[]{:S(2)}, u32[]{:S(2)}) collective-permute-start(f32[2,8,32,128]{3,2,1,0:T(8,128)S(1)} %pad_maximum_fusion.own), channel_id=1, source_target_pairs={{96,0},{192,96},{288,192},{384,288},{480,384},{576,480},{672,576},... | collective-permute-start | bytes 786440 | tf_op jit(solution)/shard_map/ppermute | solution.py:403
  22.2 6.6 %collective-permute-start.2 = (f32[2,8,32,128]{3,2,1,0:T(8,128)S(1)}, f32[2,8,32,128]{3,2,1,0:T(8,128)S(1)}, u32[]{:S(2)}, u32[]{:S(2)}) collective-permute-start(f32[2,8,32,128]{3,2,1,0:T(8,128)S(1)} %pad_maximum_fusion.own), channel_id=1, source_target_pairs={{0,96},{96,192},{192,288},{288,384},{384,480},{480,576},{576,672},... | collective-permute-start | bytes 786440 | tf_op jit(solution)/shard_map/ppermute | solution.py:403
  24.2 0.7 copy-start
  24.9 0.7 copy-start.1
  25.6 0.7 copy-start.2
  26.2 0.7 copy-start.3

commit v3 on v2

--- a/solution.py
+++ b/solution.py
@@ -11,9 +11,12 @@
 DEGREE = 8
 FIELDS = 8
 OWNED = 4
+WIDTH = 8
+PACKED = 4
 LANES = 128
-MOMENT_LANE = 32
-LOW_LANE = 64
+HIGH_LANE = 48
+LOW_LANE = 96
+CENTER = 64
 SLAB = ("x", "core")
 TILE = ("z", "y")
 
@@ -73,9 +76,18 @@
     return lax.broadcasted_iota(jnp.int32, shape, len(shape) - 1)
 
 
-def prepare_kernel(index, order, conductance, level, hot, table, plate_of, owner):
-    plate_of[...] = order[...]
-    cells = index[...]
+def prepare_kernel(index, order, conductance, level, hot, table, plate_of, owner, cells, factor, offset, arrivals):
+    copies = [
+        pltpu.make_async_copy(source, target, arrivals.at[at])
+        for at, (source, target) in enumerate(
+            ((index, cells), (order, plate_of), (conductance, factor), (level, offset))
+        )
+    ]
+    for copy in copies:
+        copy.start()
+    for copy in copies:
+        copy.wait()
+    cells = cells[...]
     inlets, plates = cells.shape
     lane = lane_of((inlets, LANES))
     slot = lax.broadcasted_iota(jnp.int32, (inlets, LANES), 0)
@@ -92,7 +104,7 @@
     first = lax.broadcasted_iota(jnp.int32, (8, LANES), 0) == 0
     values = jnp.zeros((8, LANES), jnp.float32)
     for q in range(OWNED):
-        values = jnp.where(lane == q * FIELDS, jnp.where(first, conductance[q], level[q]), values)
+        values = jnp.where(lane == q * FIELDS, jnp.where(first, factor[q], offset[q]), values)
     owner[...] = values
 
 
@@ -178,25 +190,29 @@
         value, extra = two_sum(value, pltpu.roll(value, step, 1))
         error = error + pltpu.roll(error, step, 1) + extra
         step //= 2
-    value, error = quick_two_sum(value, error)
     lane_s = lane_of((slots, LANES))
     row_s = lax.broadcasted_iota(jnp.int32, (slots, LANES), 0)
-    placed = jnp.where(lane_s == MOMENT_LANE + row_s, value, 0.0)
-    placed = placed + jnp.where(lane_s == LOW_LANE + row_s, error, 0.0)
+    parity = row_s % 2 == 0
+    base = jnp.where(parity, value[0:1], value[1:2])
+    base_error = jnp.where(parity, error[0:1], error[1:2])
+    value, extra = two_sum(2.0 * value, -base)
+    error = (2.0 * error - base_error) + extra
+    value, error = quick_two_sum(value, error)
+    placed = jnp.where(jnp.abs(lane_s - HIGH_LANE) == row_s, value, 0.0)
+    placed = placed + jnp.where(jnp.abs(lane_s - LOW_LANE) == row_s, error, 0.0)
+    placed = jnp.where(row_s <= 2 * DEGREE, placed, 0.0)
     moments = jnp.sum(placed, axis=0, keepdims=True)
 
     for copy in copies:
         copy.wait()
     plates = sums.shape[0] // FIELDS
-    inlets = hot.shape[0] // plates
+    inlets = index.shape[0] // plates
 
     def plate(at, carry):
-        of = plate_of[at]
-        start = pl.multiple_of(of * inlets, inlets)
-        line, place = of >> 3, (of & 7) * inlets
+        start = pl.multiple_of(plate_of[at] * inlets, inlets)
         totals = [None, None]
         for slot in range(inlets):
-            row = pl.multiple_of(index[line, place + slot], FIELDS)
+            row = pl.multiple_of(index[start + slot], FIELDS)
             picked = basis[pl.ds(row, FIELDS), :] * hot[pl.ds(start + slot, FIELDS, stride=0), :]
             side = slot % 2
             totals[side] = picked if totals[side] is None else totals[side] + picked
@@ -204,52 +220,63 @@
         return carry
 
     lax.fori_loop(0, plates, plate, 0, unroll=8)
-    tiles = plates // OWNED
-    lane_t = lane_of((tiles, LANES))
-    out = jnp.broadcast_to(moments, (tiles, LANES))
-    for slot in range(OWNED * FIELDS):
-        column = sums[pl.ds(slot, tiles, stride=OWNED * FIELDS), :]
-        out = jnp.where(lane_t == slot, jnp.sum(column, axis=1, keepdims=True), out)
-    for at in range(0, payload.shape[0], tiles):
-        payload[pl.ds(at, tiles), :] = out
+    lines = plates // (OWNED * WIDTH * PACKED)
+    lane_w = lane_of((WIDTH, LANES))
+    span = OWNED * FIELDS
+    rows_per = WIDTH * (lines + 1)
+    sources = payload.shape[0] // rows_per
+
+    for line in range(lines):
+        out = jnp.zeros((WIDTH, LANES), jnp.float32)
+        for at in range(LANES):
+            place, slot = divmod(at, span)
+            first = (line * PACKED + place) * WIDTH * span + slot
+            column = sums[pl.ds(first, WIDTH, stride=span), :]
+            out = jnp.where(lane_w == at, jnp.sum(column, axis=1, keepdims=True), out)
+        for at in range(sources):
+            payload[pl.ds(at * rows_per + line, WIDTH, stride=lines + 1), :] = out
+    out = jnp.broadcast_to(moments, (WIDTH, LANES))
+    for at in range(sources):
+        payload[pl.ds(at * rows_per + lines, WIDTH, stride=lines + 1), :] = out
 
 
 def with_error(value, error):
     lane = lane_of(value.shape)
-    shifted = pltpu.roll(error, LOW_LANE - MOMENT_LANE, 1)
-    return value + jnp.where(lane < MOMENT_LANE, error, 0.0) + jnp.where(lane >= LOW_LANE, shifted, 0.0)
-
-
-def sum_rows(rows):
-    count = rows.shape[0]
+    shifted = pltpu.roll(error, LOW_LANE - HIGH_LANE, 1)
+    first = lane < OWNED * FIELDS
+    return value + jnp.where(first, error, 0.0) + jnp.where(lane >= LOW_LANE - 2 * DEGREE, shifted, 0.0)
+
+
+def sum_rows(rows, step):
     value = rows[pl.ds(0, 8), :]
     error = jnp.zeros_like(value)
-    for at in range(8, count, 8):
+    for at in range(8, rows.shape[0], 8):
         value, extra = two_sum(value, rows[pl.ds(at, 8), :])
         error = error + extra
-    for step in (4, 2, 1):
+    while step < 8:
         value, extra = two_sum(value, pltpu.roll(value, step, 0))
         error = error + pltpu.roll(error, step, 0) + extra
-    return with_error(value, error)
-
-
-def rows_kernel(rows, out):
-    count = out.shape[0] // 2
-    value = rows[pl.ds(0, count), :]
-    error = jnp.zeros_like(value)
-    for at in range(count, rows.shape[0], count):
-        value, extra = two_sum(value, rows[pl.ds(at, count), :])
-        error = error + extra
-    value = with_error(value, error)
-    out[pl.ds(0, count), :] = value
-    out[pl.ds(count, count), :] = value
-
-
-def fold(moments, lane):
-    total = jnp.zeros_like(moments)
-    for j in range(1, 2 * DEGREE + 1):
-        total = jnp.where(lane == LOW_LANE - j, moments[:, j : j + 1], total)
-    return jnp.where(lane >= LOW_LANE, pltpu.roll(moments, LOW_LANE, 1), total)
+        step *= 2
+    return value, error
+
+
+def rows_kernel(rows, out, lines=1):
+    value, error = sum_rows(rows, lines + 1)
+    moments = with_error(value, error)[lines : lines + 1]
+    total = value + error
+    depth = lines * PACKED
+    row = lax.broadcasted_iota(jnp.int32, (8, LANES), 0)
+    first = lane_of((1, LANES)) < OWNED * FIELDS
+    made = []
+    for z in range(depth):
+        line = total[z // PACKED : z // PACKED + 1]
+        place = (z % PACKED) * OWNED * FIELDS
+        if place:
+            line = pltpu.roll(line, LANES - place, 1)
+        made.append(jnp.where(first, line, moments))
+    for at in range(0, out.shape[0], depth):
+        for z in range(depth):
+            out[pl.ds(at + z, 1), :] = made[z]
 
 
 def shift(row, amount):
@@ -300,14 +327,16 @@
     weight = weight[0] + weight[1]
 
     def entry(source, j):
-        return jnp.broadcast_to(source[:, LOW_LANE + j : LOW_LANE + j + 1], source.shape)
+        return jnp.broadcast_to(source[:, CENTER + j : CENTER + j + 1], source.shape)
 
     weights = [entry(weight, j) for j in range(7)]
     rhs = [entry(moment, j) for j in range(4)]
     matrix = [[0.5 * (weights[i + j] + weights[abs(i - j)]) for j in range(4)] for i in range(4)]
+    inverse = []
     for k in range(4):
+        inverse.append(1.0 / matrix[k][k])
         for i in range(k + 1, 4):
-            factor = matrix[i][k] / matrix[k][k]
+            factor = matrix[i][k] * inverse[k]
             for j in range(k + 1, i + 1):
                 matrix[i][j] = matrix[i][j] - factor * matrix[j][k]
             rhs[i] = rhs[i] - factor * rhs[k]
@@ -316,24 +345,17 @@
         value = rhs[i]
         for j in range(i + 1, 4):
             value = value - matrix[j][i] * result[j]
-        result[i] = value / matrix[i][i]
+        result[i] = value * inverse[i]
     return result
 
 
 def final_kernel(rows, basis, last, owner, solution, residual, flow, scale=1.0):
-    row = sum_rows(rows)
+    row = with_error(*sum_rows(rows, 1))
     lane = lane_of((8, LANES))
-    high = pltpu.roll(row, LANES - MOMENT_LANE, 1)
-    low = pltpu.roll(row, LANES - LOW_LANE, 1)
-    valid = lane <= 2 * DEGREE
-    high, low = quick_two_sum(jnp.where(valid, high, 0.0), jnp.where(valid, low, 0.0))
-    first = (high[:, 0:1], low[:, 0:1])
-    second = (high[:, 1:2], low[:, 1:2])
-    even = lane % 2 == 0
-    base = (jnp.where(even, first[0], second[0]), jnp.where(even, first[1], second[1]))
-    twice = dd_add(dd_scale((high, low), 2.0), dd_neg(base))
-    mu = tuple(jnp.where(valid, value, 0.0) for value in twice)
-    mu = (fold(mu[0], lane), fold(mu[1], lane))
+    valid = jnp.abs(lane - CENTER) <= 2 * DEGREE
+    high = jnp.where(valid, pltpu.roll(row, CENTER - HIGH_LANE, 1), 0.0)
+    low = jnp.where(valid, pltpu.roll(row, LANES + CENTER - LOW_LANE, 1), 0.0)
+    mu = quick_two_sum(high, low)
     zero = jnp.zeros((8, LANES), jnp.float32)
     first_coeffs = galerkin(mu)
     change = apply_operator([(value, zero) for value in first_coeffs])
@@ -402,7 +424,7 @@
         backward = [(target, source) for source, target in forward]
         return lax.ppermute(to_next, axis, forward), lax.ppermute(to_previous, axis, backward)
 
-    own = jnp.stack([right_side, diagonal])
+    own = lax.optimization_barrier(jnp.stack([right_side, diagonal]))
     before, after = both_ways(own[:, :, cy - HALO :], own[:, :, :HALO], TILE)
     own = jnp.concatenate([before, own, after], axis=2)
     low, high = both_ways(own, own, SLAB)
@@ -410,13 +432,19 @@
     hot, table, order, owner = pl.pallas_call(
         prepare_kernel,
         out_shape=(
-            jax.ShapeDtypeStruct((plates * inlets, LANES), f32),
+            jax.ShapeDtypeStruct((plates * inlets + 8, LANES), f32),
             jax.ShapeDtypeStruct((plates * inlets // LANES, LANES), jnp.int32),
             jax.ShapeDtypeStruct((plates,), jnp.int32),
             jax.ShapeDtypeStruct((8, LANES), f32),
         ),
-        in_specs=[VMEM, VMEM, SMEM, SMEM],
+        in_specs=[pl.BlockSpec(memory_space=pltpu.HBM)] * 4,
         out_specs=(VMEM,) * 4,
+        scratch_shapes=[
+            pltpu.VMEM((inlets, plates), jnp.int32),
+            pltpu.SMEM((OWNED,), f32),
+            pltpu.SMEM((OWNED,), f32),
+            pltpu.SemaphoreType.DMA((4,)),
+        ],
         compiler_params=pltpu.CompilerParams(vmem_limit_bytes=4 * 1024 * 1024),
         cost_estimate=pl.CostEstimate(flops=800000, bytes_accessed=3200000, transcendentals=0),
         name="prepare",
@@ -426,10 +454,11 @@
     tall = (wide[0], wide[1] + 2 * HALO, nx)
     cells = cz * cy
     copies = lax.axis_size("x")
+    lines = tiles // (WIDTH * PACKED)
     payload, basis, last = pl.pallas_call(
         basis_kernel,
         out_shape=(
-            jax.ShapeDtypeStruct((copies * tiles, LANES), f32),
+            jax.ShapeDtypeStruct((copies * WIDTH * (lines + 1), LANES), f32),
             jax.ShapeDtypeStruct((cells * FIELDS, nx), f32),
             jax.ShapeDtypeStruct((cells, nx), f32),
         ),
@@ -442,27 +471,28 @@
             pltpu.VMEM(tall, f32),
             pltpu.VMEM((24 * 8, nx), f32),
             pltpu.VMEM((plates * FIELDS, nx), f32),
-            pltpu.SMEM((plates * inlets // LANES, LANES), jnp.int32),
+            pltpu.SMEM((plates * inlets,), jnp.int32),
             pltpu.SMEM((plates,), jnp.int32),
             pltpu.SemaphoreType.DMA((2,)),
         ],
         compiler_params=pltpu.CompilerParams(vmem_limit_bytes=8 * 1024 * 1024),
         name="basis",
-    )(own, low, high, hot, table, order)
-
-    group = copies * lax.axis_size("z")
-    width = lax.axis_size("y")
-    arrived = lax.all_to_all(payload.reshape(group, width, LANES), ("x", "z"), 0, 0, tiled=True)
-    ends = lax.axis_size("core") * width
+    )(own, low, high, hot, table.reshape(plates * inlets), order)
+
+    group = copies * WIDTH
+    arrived = lax.all_to_all(
+        payload.reshape(group * (lines + 1), 1, LANES), ("x", "y"), 0, 0, tiled=True
+    )
+    ends = lax.axis_size("core") * lax.axis_size("z")
     rows = pl.pallas_call(
-        rows_kernel,
+        functools.partial(rows_kernel, lines=lines),
         out_shape=jax.ShapeDtypeStruct((ends, LANES), f32),
         in_specs=[VMEM],
         out_specs=VMEM,
         compiler_params=pltpu.CompilerParams(vmem_limit_bytes=2 * 1024 * 1024),
         name="rows",
-    )(arrived.reshape(group * width, LANES))
-    arrived = lax.all_to_all(rows.reshape(ends, 1, LANES), ("core", "y"), 0, 0, tiled=True)
+    )(arrived.reshape(group * (lines + 1), LANES))
+    arrived = lax.all_to_all(rows.reshape(ends, 1, LANES), ("core", "z"), 0, 0, tiled=True)
     scale = float(1.0 / (devices * inlets) ** 0.5)
     solution, residual, flow = pl.pallas_call(
         functools.partial(final_kernel, scale=scale),
@@ -481,7 +511,7 @@
 
 def solution(mesh):
     slabs, tiles = mesh.devices.shape
-    chips = mesh.devices.reshape(slabs // 2, 2, tiles // 8, 8)
+    chips = mesh.devices.reshape(slabs // 2, 2, tiles // WIDTH, WIDTH)
     fine = jax.sharding.Mesh(chips, SLAB + TILE)
     in_specs = (
         P(SLAB, TILE, None),

time: 91.8 us -> 78.1 us (0.85)
  Pallas kernels: 21.9 us -> 13 us
  blocking collectives: 42.5 us -> 38.5 us
    pallas_call x2, Pallas kernels: 17.9 us -> 9.11 us  [the longest x1 9.01 us: on_device(): pl.pallas_call(basis_kernel, out_shape=(jax.ShapeDtypeStruct((copies * WI...]
    all_to_all x2, blocking collectives: 42.5 us -> 38.5 us  [the longest x1 26 us: on_device(): lax.all_to_all(rows.reshape(ends, 1, LANES), ('core', 'z'), 0, 0, tiled=T...]
  transfers between devices with their start and end apart: 4 -> 4, of which waited for: 1 -> 1; matrix products, arithmetic and copies ran while one was open for 0% -> 0% of each run, Pallas kernels for 2% -> 3%
where the time goes in v3:
time: 78.1 us; the launch traced here: 77.7 us
  blocking collectives  38.5 us (49%)
  starting transfers between devices  18.1 us (23%)
  Pallas kernels  13 us (17%)
  waiting for transfers between devices  3.71 us (5%)
  local copies, waits for them, and re-layouts  2.73 us (3%)
  other arithmetic  0.9 us (1%)
    all_to_all x1, blocking collectives, on_device(): lax.all_to_all(rows.reshape(ends, 1, LANES), ('core', 'z'), 0, 0, tiled=T...  26 us
    all_to_all x1, blocking collectives, on_device(): lax.all_to_all(payload.reshape(group * (lines + 1), 1, LANES), ('x', 'y')...  12.6 us
    ppermute x2, starting transfers between devices, both_ways(): lax.ppermute(to_previous, axis, backward)  12.1 us
    pallas_call x1, Pallas kernels, on_device(): pl.pallas_call(basis_kernel, out_shape=(jax.ShapeDtypeStruct((copies * WI...  9.01 us
    ppermute x2, starting transfers between devices, both_ways(): lax.ppermute(to_next, axis, forward)  5.95 us
    ppermute x2, waiting for transfers between devices, both_ways(): lax.ppermute(to_previous, axis, backward)  3.7 us
    unnamed x8, local copies, waits for them, and re-layouts  2.72 us
    pallas_call x1, Pallas kernels, on_device(): pl.pallas_call(prepare_kernel, out_shape=(jax.ShapeDtypeStruct((plates *...  1.96 us
  transfers between devices with their start and end apart: 4, of which 1 were waited for; matrix products, arithmetic and copies ran while one was open for 0% of the time, Pallas kernels for 3%

profile of v3, /device:TPU:1, one launch (start us, length us, event | category | flops | bytes accessed | tf_op | source)
XLA Modules:
  0.0 77.7 jit_solution(4188327291067191247)
XLA Ops:
  0.6 0.9 %pad_maximum_fusion.1 = f32[2,8,16,128]{3,2,1,0:T(8,128)S(1)} fusion(f32[1,8,16,128]{3,2,1,0:T(8,128)} %bitcast.22, f32[1,8,16,128]{3,2,1,0:T(8,128)} %bitcast.23), kind=kLoop, calls=%fused_computation.1 | loop fusion | flops 32768 | bytes 262144 | tf_op jit(solution)/shard_map/stack | solution.py:427
  1.5 4.0 %collective-permute-start = (f32[2,8,8,128]{3,2,1,0:T(8,128)S(1)}, f32[2,8,8,128]{3,2,1,0:T(8,128)S(1)}, u32[]{:S(2)}, u32[]{:S(2)}) collective-permute-start(f32[2,8,8,128]{3,2,1,0:T(8,128)S(1)} %get-tuple-element.23), channel_id=1, source_target_pairs={{0,1},{1,2},{2,3},{3,4},{4,5},{5,6},{6,7},{7,8},{8,9},{9,10},{10,1... | collective-permute-start | bytes 196616 | tf_op jit(solution)/shard_map/ppermute | solution.py:425
  5.6 1.3 %collective-permute-start.1 = (f32[2,8,8,128]{3,2,1,0:T(8,128)S(1)}, f32[2,8,8,128]{3,2,1,0:T(8,128)S(1)}, u32[]{:S(2)}, u32[]{:S(2)}) collective-permute-start(f32[2,8,8,128]{3,2,1,0:T(8,128)S(1)} %get-tuple-element.24), channel_id=1, source_target_pairs={{1,0},{2,1},{3,2},{4,3},{5,4},{6,5},{7,6},{8,7},{9,8},{10,9},{11,1... | collective-permute-start | bytes 196616 | tf_op jit(solution)/shard_map/ppermute | solution.py:425
  6.9 0.0 collective-permute-done
  6.9 3.7 %collective-permute-done.1 = f32[2,8,8,128]{3,2,1,0:T(8,128)S(1)} collective-permute-done((f32[2,8,8,128]{3,2,1,0:T(8,128)S(1)}, f32[2,8,8,128]{3,2,1,0:T(8,128)S(1)}, u32[]{:S(2)}, u32[]{:S(2)}) %collective-permute-start.1) | collective-permute-done | bytes 65568 | tf_op jit(solution)/shard_map/ppermute | solution.py:425
  10.6 10.8 %collective-permute-start.3 = (f32[2,8,32,128]{3,2,1,0:T(8,128)S(1)}, f32[2,8,32,128]{3,2,1,0:T(8,128)S(1)}, u32[]{:S(2)}, u32[]{:S(2)}) collective-permute-start(f32[2,8,32,128]{3,2,1,0:T(8,128)S(1)} %pad_maximum_fusion.own), channel_id=1, source_target_pairs={{96,0},{192,96},{288,192},{384,288},{480,384},{576,480},{672,576},... | collective-permute-start | bytes 786440 | tf_op jit(solution)/shard_map/ppermute | solution.py:425
  21.4 1.9 %collective-permute-start.2 = (f32[2,8,32,128]{3,2,1,0:T(8,128)S(1)}, f32[2,8,32,128]{3,2,1,0:T(8,128)S(1)}, u32[]{:S(2)}, u32[]{:S(2)}) collective-permute-start(f32[2,8,32,128]{3,2,1,0:T(8,128)S(1)} %pad_maximum_fusion.own), channel_id=1, source_target_pairs={{0,96},{96,192},{192,288},{288,384},{384,480},{480,576},{576,672},... | collective-permute-start | bytes 786440 | tf_op jit(solution)/shard_map/ppermute | solution.py:425
  23.4 0.0 copy-start
  23.4 0.7 copy-done
  24.1 0.0 copy-start.1
  24.1 0.7 copy-done.1
  24.8 0.0 copy-start.2
  24.8 0.7 copy-done.2
  25.5 0.0 copy-start.3
  25.5 0.7 copy-done.3
  26.1 2.0 %prepare.1 = (f32[6152,128]{1,0:T(8,128)S(1)}, s32[48,128]{1,0:T(8,128)S(1)}, s32[384]{0:T(512)S(1)}, f32[8,128]{1,0:T(8,128)S(1)}) custom-call(s32[16,384]{1,0:T(8,128)S(1)} %bitcast.21, s32[384]{0:T(512)S(1)} %copy-done.1, f32[4]{0:T(128)S(1)} %copy-done.2, f32[4]{0:T(128)S(1)} %copy-done.3), custom_call_target="tpu_custom_call" | custom-call | flops 800000 | bytes 3200000 | tf_op jit(solution)/shard_map/prepare/pallas_call | solution.py:432
  28.1 0.0 collective-permute-done.3.high
  28.1 0.0 collective-permute-done.2.low
  28.1 9.0 %basis.1 = (f32[128,128]{1,0:T(8,128)S(1)}, f32[1024,128]{1,0:T(8,128)S(1)}, f32[128,128]{1,0:T(8,128)S(1)}) custom-call(f32[2,8,32,128]{3,2,1,0:T(8,128)S(1)} %pad_maximum_fusion.own, f32[2,8,32,128]{3,2,1,0:T(8,128)S(1)} %collective-permute-done.2.low, f32[2,8,32,128]{3,2,1,0:T(8,128)S(1)} %collective-permute-done.3.high, ...), custom_call_target="tpu_custom_call" | custom-call | tf_op jit(solution)/shard_map/basis/pallas_call | solution.py:458
  37.1 12.6 %all_to_all.10 = f32[128,1,128]{2,1,0:T(1,128)S(1)} all-to-all(f32[128,1,128]{2,1,0:T(1,128)S(1)} %bitcast.17), channel_id=1, replica_groups=mesh['x'=4,'core'=2,'z'=12,'y'=8] {'x','y'}, dimensions={0} | all-to-all | bytes 131072 | tf_op jit(solution)/shard_map/all_to_all | solution.py:483
  49.7 0.1 rows.1
  49.8 26.0 %all_to_all.11 = f32[24,1,128]{2,1,0:T(1,128)S(1)} all-to-all(f32[24,1,128]{2,1,0:T(1,128)S(1)} %bitcast.18), channel_id=1, replica_groups=mesh['x'=4,'core'=2,'z'=12,'y'=8] {'core','z'}, dimensions={0} | all-to-all | bytes 24576 | tf_op jit(solution)/shard_map/all_to_all | solution.py:495
  75.8 1.9 %final.1 = (f32[128,128]{1,0:T(8,128)}, f32[128,128]{1,0:T(8,128)}, f32[4]{0:T(128)}) custom-call(f32[24,128]{1,0:T(8,128)S(1)} %bitcast.19, f32[1024,128]{1,0:T(8,128)S(1)} %get-tuple-element.17.basis, f32[128,128]{1,0:T(8,128)S(1)} %get-tuple-element.18.last, f32[8,128]{1,0:T(8,128)S(1)} %get-tuple-element.19.owner), custom_call_target="tpu_custom_call" | custom-call | tf_op jit(solution)/shard_map/final/pallas_call | solution.py:497
  (2 shorter events, 0.0 us)
Async XLA Ops:
  1.5 5.4 %collective-permute-start = (f32[2,8,8,128]{3,2,1,0:T(8,128)S(1)}, f32[2,8,8,128]{3,2,1,0:T(8,128)S(1)}, u32[]{:S(2)}, u32[]{:S(2)}) collective-permute-start(f32[2,8,8,128]{3,2,1,0:T(8,128)S(1)} %get-tuple-element.23), channel_id=1, source_target_pairs={{0,1},{1,2},{2,3},{3,4},{4,5},{5,6},{6,7},{7,8},{8,9},{9,10},{10,1... | collective-permute-start | bytes 196616 | tf_op jit(solution)/shard_map/ppermute | solution.py:425
  5.6 5.0 %collective-permute-start.1 = (f32[2,8,8,128]{3,2,1,0:T(8,128)S(1)}, f32[2,8,8,128]{3,2,1,0:T(8,128)S(1)}, u32[]{:S(2)}, u32[]{:S(2)}) collective-permute-start(f32[2,8,8,128]{3,2,1,0:T(8,128)S(1)} %get-tuple-element.24), channel_id=1, source_target_pairs={{1,0},{2,1},{3,2},{4,3},{5,4},{6,5},{7,6},{8,7},{9,8},{10,9},{11,1... | collective-permute-start | bytes 196616 | tf_op jit(solution)/shard_map/ppermute | solution.py:425
  10.6 17.5 %collective-permute-start.3 = (f32[2,8,32,128]{3,2,1,0:T(8,128)S(1)}, f32[2,8,32,128]{3,2,1,0:T(8,128)S(1)}, u32[]{:S(2)}, u32[]{:S(2)}) collective-permute-start(f32[2,8,32,128]{3,2,1,0:T(8,128)S(1)} %pad_maximum_fusion.own), channel_id=1, source_target_pairs={{96,0},{192,96},{288,192},{384,288},{480,384},{576,480},{672,576},... | collective-permute-start | bytes 786440 | tf_op jit(solution)/shard_map/ppermute | solution.py:425
  21.4 6.6 %collective-permute-start.2 = (f32[2,8,32,128]{3,2,1,0:T(8,128)S(1)}, f32[2,8,32,128]{3,2,1,0:T(8,128)S(1)}, u32[]{:S(2)}, u32[]{:S(2)}) collective-permute-start(f32[2,8,32,128]{3,2,1,0:T(8,128)S(1)} %pad_maximum_fusion.own), channel_id=1, source_target_pairs={{0,96},{96,192},{192,288},{288,384},{384,480},{480,576},{576,672},... | collective-permute-start | bytes 786440 | tf_op jit(solution)/shard_map/ppermute | solution.py:425
  23.4 0.7 copy-start
  24.1 0.7 copy-start.1
  24.8 0.7 copy-start.2
  25.5 0.7 copy-start.3

commit v4 on v3

--- a/solution.py
+++ b/solution.py
@@ -76,48 +76,46 @@
     return lax.broadcasted_iota(jnp.int32, shape, len(shape) - 1)
 
 
-def prepare_kernel(index, order, conductance, level, hot, table, plate_of, owner, cells, factor, offset, arrivals):
-    copies = [
-        pltpu.make_async_copy(source, target, arrivals.at[at])
-        for at, (source, target) in enumerate(
-            ((index, cells), (order, plate_of), (conductance, factor), (level, offset))
+def one_hot(found, dtype):
+    return jnp.where(found, 1.0, 0.0).astype(dtype)
+
+
+def prepare_kernel(index, order, conductance, level, lanes_hot, rows_hot, owner):
+    inlets, plates = index.shape
+    low = (index[...] & 127).astype(jnp.float32)
+    high = (index[...] >> 7).astype(jnp.float32)
+    both = jnp.concatenate([low, high], axis=0).astype(jnp.bfloat16)
+    row = lax.broadcasted_iota(jnp.int32, (plates, plates), 0)
+    column = lane_of((plates, plates))
+    group = column // (PACKED * OWNED)
+    line, y = group // WIDTH, group % WIDTH
+    place, q = (column // OWNED) % PACKED, column % OWNED
+    owned = ((line * PACKED + place) * WIDTH + y) * OWNED + q
+    for choice in (row == order[...], row == owned):
+        both = jnp.dot(both, one_hot(choice, jnp.bfloat16), preferred_element_type=jnp.float32)
+        both = both.astype(jnp.bfloat16)
+    cells = both.astype(jnp.float32).astype(jnp.int32)
+    at = lax.broadcasted_iota(jnp.int32, (LANES, plates), 0)
+    for slot in range(inlets):
+        step, start = slot // 2, (slot % 2) * plates
+        hot = one_hot(at == cells[slot : slot + 1], jnp.bfloat16)
+        lanes_hot[step, :LANES, start : start + plates] = hot
+        lanes_hot[step, LANES:, start : start + plates] = hot
+        rows_hot[step, :, start : start + plates] = one_hot(
+            at == cells[inlets + slot : inlets + slot + 1], jnp.float32
         )
-    ]
-    for copy in copies:
-        copy.start()
-    for copy in copies:
-        copy.wait()
-    cells = cells[...]
-    inlets, plates = cells.shape
-    lane = lane_of((inlets, LANES))
-    slot = lax.broadcasted_iota(jnp.int32, (inlets, LANES), 0)
-    packed = LANES // inlets
-    for row in range(plates // packed):
-        total = jnp.zeros((inlets, LANES), jnp.int32)
-        for place in range(packed):
-            at = row * packed + place
-            cell = jnp.broadcast_to(cells[:, at : at + 1], (inlets, LANES))
-            hot[pl.ds(at * inlets, inlets), :] = jnp.where(lane == (cell & 127), 1.0, 0.0)
-            total = total + jnp.where(lane == slot + place * inlets, (cell >> 7) * FIELDS, 0)
-        table[pl.ds(row, 1), :] = jnp.sum(total, axis=0, keepdims=True)
     lane = lane_of((8, LANES))
     first = lax.broadcasted_iota(jnp.int32, (8, LANES), 0) == 0
     values = jnp.zeros((8, LANES), jnp.float32)
     for q in range(OWNED):
-        values = jnp.where(lane == q * FIELDS, jnp.where(first, factor[q], offset[q]), values)
+        values = jnp.where(lane == q * FIELDS, jnp.where(first, conductance[q], level[q]), values)
     owner[...] = values
 
 
 def basis_kernel(
-    own, low, high, hot, table, order, payload, basis, last,
-    alpha, beta, even, odd, parts, sums, index, plate_of, arrivals,
+    own, low, high, lanes_hot, rows_hot, payload, basis,
+    alpha, beta, even, odd, parts, halves, turned,
 ):
-    copies = [
-        pltpu.make_async_copy(table, index, arrivals.at[0]),
-        pltpu.make_async_copy(order, plate_of, arrivals.at[1]),
-    ]
-    for copy in copies:
-        copy.start()
     cz = own.shape[1]
     wide_y = own.shape[2]
     cy = wide_y - 2 * HALO
@@ -137,13 +135,17 @@
     rows = pl.ds(HALO, wide_y)
     inner = pl.ds(2 * HALO, cy)
 
+    cells = cz * cy
+
     def emit(field, degree):
         for z in range(cz):
             value = field[cz + z, inner, :]
+            at = pl.ds(degree * cells + z * cy, cy)
+            basis[at, :] = value
             if degree < FIELDS:
-                basis[pl.ds(z * cy * FIELDS + degree, cy, stride=FIELDS), :] = value
-            else:
-                last[pl.ds(z * cy, cy), :] = value
+                upper = value.astype(jnp.bfloat16)
+                halves[at, :LANES] = upper
+                halves[at, LANES:] = (value - upper.astype(jnp.float32)).astype(jnp.bfloat16)
 
     def product(first, second, slot):
         total = None
@@ -203,38 +205,39 @@
     placed = jnp.where(row_s <= 2 * DEGREE, placed, 0.0)
     moments = jnp.sum(placed, axis=0, keepdims=True)
 
-    for copy in copies:
-        copy.wait()
-    plates = sums.shape[0] // FIELDS
-    inlets = index.shape[0] // plates
-
-    def plate(at, carry):
-        start = pl.multiple_of(plate_of[at] * inlets, inlets)
-        totals = [None, None]
-        for slot in range(inlets):
-            row = pl.multiple_of(index[start + slot], FIELDS)
-            picked = basis[pl.ds(row, FIELDS), :] * hot[pl.ds(start + slot, FIELDS, stride=0), :]
-            side = slot % 2
-            totals[side] = picked if totals[side] is None else totals[side] + picked
-        sums[pl.ds(pl.multiple_of(at * FIELDS, FIELDS), FIELDS), :] = totals[0] + totals[1]
-        return carry
-
-    lax.fori_loop(0, plates, plate, 0, unroll=8)
+    steps, depth, columns = rows_hot.shape
+    plates = columns // 2
+    tile = 2 * LANES
+    groups = plates // LANES
+
+    totals = [jnp.zeros((FIELDS, 8, LANES), jnp.float32)] * groups
+    for step in range(steps):
+        for start in range(0, columns, tile):
+            picked = jnp.dot(
+                halves[...], lanes_hot[step, :, start : start + tile], preferred_element_type=jnp.float32
+            )
+            mask = rows_hot[step, :, start : start + tile].reshape(1, depth // 8, 8, tile)
+            picked = jnp.sum(picked.reshape(FIELDS, depth // 8, 8, tile) * mask, axis=1)
+            for side in range(2):
+                group = (start // LANES + side) % groups
+                totals[group] = totals[group] + picked[:, :, side * LANES : (side + 1) * LANES]
+    for group, total in enumerate(totals):
+        turned[pl.ds(group * LANES, LANES), :FIELDS] = jnp.sum(total, axis=1).T
+
     lines = plates // (OWNED * WIDTH * PACKED)
-    lane_w = lane_of((WIDTH, LANES))
-    span = OWNED * FIELDS
     rows_per = WIDTH * (lines + 1)
     sources = payload.shape[0] // rows_per
-
+    packed = PACKED * OWNED
+    lane_w = lane_of((lines * WIDTH, LANES))
+    out = jnp.zeros((lines * WIDTH, LANES), jnp.float32)
+    for at in range(packed):
+        column = turned[pl.ds(at, lines * WIDTH, stride=packed), :]
+        if at:
+            column = pltpu.roll(column, at * FIELDS, 1)
+        out = jnp.where(lane_w // FIELDS == at, column, out)
     for line in range(lines):
-        out = jnp.zeros((WIDTH, LANES), jnp.float32)
-        for at in range(LANES):
-            place, slot = divmod(at, span)
-            first = (line * PACKED + place) * WIDTH * span + slot
-            column = sums[pl.ds(first, WIDTH, stride=span), :]
-            out = jnp.where(lane_w == at, jnp.sum(column, axis=1, keepdims=True), out)
         for at in range(sources):
-            payload[pl.ds(at * rows_per + line, WIDTH, stride=lines + 1), :] = out
+            payload[pl.ds(at * rows_per + line, WIDTH, stride=lines + 1), :] = out[line * WIDTH : (line + 1) * WIDTH]
     out = jnp.broadcast_to(moments, (WIDTH, LANES))
     for at in range(sources):
         payload[pl.ds(at * rows_per + lines, WIDTH, stride=lines + 1), :] = out
@@ -349,7 +352,7 @@
     return result
 
 
-def final_kernel(rows, basis, last, owner, solution, residual, flow, scale=1.0):
+def final_kernel(rows, basis, owner, solution, residual, flow, scale=1.0):
     row = with_error(*sum_rows(rows, 1))
     lane = lane_of((8, LANES))
     valid = jnp.abs(lane - CENTER) <= 2 * DEGREE
@@ -385,8 +388,7 @@
 
     cells = solution.shape[0]
     for at in range(0, cells, 8):
-        fields = [basis[pl.ds(at * FIELDS + k, 8, stride=FIELDS), :] for k in range(FIELDS)]
-        fields.append(last[pl.ds(at, 8), :])
+        fields = [basis[pl.ds(k * cells + at, 8), :] for k in range(DEGREE + 1)]
         total = solved[0] * fields[0]
         rest = left[0] * fields[0]
         for k in range(1, DEGREE + 1):
@@ -429,55 +431,45 @@
     own = jnp.concatenate([before, own, after], axis=2)
     low, high = both_ways(own, own, SLAB)
 
-    hot, table, order, owner = pl.pallas_call(
+    lanes_hot, rows_hot, owner = pl.pallas_call(
         prepare_kernel,
         out_shape=(
-            jax.ShapeDtypeStruct((plates * inlets + 8, LANES), f32),
-            jax.ShapeDtypeStruct((plates * inlets // LANES, LANES), jnp.int32),
-            jax.ShapeDtypeStruct((plates,), jnp.int32),
+            jax.ShapeDtypeStruct((inlets // 2, 2 * LANES, 2 * plates), jnp.bfloat16),
+            jax.ShapeDtypeStruct((inlets // 2, LANES, 2 * plates), f32),
             jax.ShapeDtypeStruct((8, LANES), f32),
         ),
-        in_specs=[pl.BlockSpec(memory_space=pltpu.HBM)] * 4,
-        out_specs=(VMEM,) * 4,
-        scratch_shapes=[
-            pltpu.VMEM((inlets, plates), jnp.int32),
-            pltpu.SMEM((OWNED,), f32),
-            pltpu.SMEM((OWNED,), f32),
-            pltpu.SemaphoreType.DMA((4,)),
-        ],
-        compiler_params=pltpu.CompilerParams(vmem_limit_bytes=4 * 1024 * 1024),
-        cost_estimate=pl.CostEstimate(flops=800000, bytes_accessed=3200000, transcendentals=0),
+        in_specs=[VMEM, VMEM, SMEM, SMEM],
+        out_specs=(VMEM,) * 3,
+        compiler_params=pltpu.CompilerParams(vmem_limit_bytes=8 * 1024 * 1024),
+        cost_estimate=pl.CostEstimate(flops=20000000, bytes_accessed=6400000, transcendentals=0),
         name="prepare",
-    )(inlet_index[0, 0].T, plate_order, conductance, plate_level)
+    )(inlet_index[0, 0].T, plate_order.reshape(1, plates), conductance, plate_level)
 
     wide = (3 * cz, cy + 2 * HALO, nx)
     tall = (wide[0], wide[1] + 2 * HALO, nx)
     cells = cz * cy
     copies = lax.axis_size("x")
     lines = tiles // (WIDTH * PACKED)
-    payload, basis, last = pl.pallas_call(
+    payload, basis = pl.pallas_call(
         basis_kernel,
         out_shape=(
             jax.ShapeDtypeStruct((copies * WIDTH * (lines + 1), LANES), f32),
-            jax.ShapeDtypeStruct((cells * FIELDS, nx), f32),
-            jax.ShapeDtypeStruct((cells, nx), f32),
+            jax.ShapeDtypeStruct(((DEGREE + 1) * cells, nx), f32),
         ),
-        in_specs=[VMEM] * 6,
-        out_specs=(VMEM, VMEM, VMEM),
+        in_specs=[VMEM] * 5,
+        out_specs=(VMEM, VMEM),
         scratch_shapes=[
             pltpu.VMEM(wide, f32),
             pltpu.VMEM(wide, f32),
             pltpu.VMEM(tall, f32),
             pltpu.VMEM(tall, f32),
             pltpu.VMEM((24 * 8, nx), f32),
-            pltpu.VMEM((plates * FIELDS, nx), f32),
-            pltpu.SMEM((plates * inlets,), jnp.int32),
-            pltpu.SMEM((plates,), jnp.int32),
-            pltpu.SemaphoreType.DMA((2,)),
+            pltpu.VMEM((FIELDS * cells, 2 * nx), jnp.bfloat16),
+            pltpu.VMEM((plates, LANES), f32),
         ],
         compiler_params=pltpu.CompilerParams(vmem_limit_bytes=8 * 1024 * 1024),
         name="basis",
-    )(own, low, high, hot, table.reshape(plates * inlets), order)
+    )(own, low, high, lanes_hot, rows_hot)
 
     group = copies * WIDTH
     arrived = lax.all_to_all(
@@ -501,11 +493,11 @@
             jax.ShapeDtypeStruct((cells, nx), f32),
             jax.ShapeDtypeStruct((OWNED,), f32),
         ),
-        in_specs=[VMEM, VMEM, VMEM, VMEM],
+        in_specs=[VMEM, VMEM, VMEM],
         out_specs=(VMEM, VMEM, SMEM),
         compiler_params=pltpu.CompilerParams(vmem_limit_bytes=4 * 1024 * 1024),
         name="final",
-    )(arrived.reshape(ends, LANES), basis, last, owner)
+    )(arrived.reshape(ends, LANES), basis, owner)
     return (solution.reshape(cz, cy, nx), residual.reshape(cz, cy, nx), flow)
 
 

time: 78.1 us -> 73.8 us (0.945)
  Pallas kernels: 13 us -> 8.32 us
    pallas_call x1, Pallas kernels: 9.01 us -> 4.77 us  [on_device(): pl.pallas_call(basis_kernel, out_shape=(jax.ShapeDtypeStruct((copies * WI...]
    unnamed x8 -> x6, local copies, waits for them, and re-layouts: 2.72 us -> 2.05 us
  transfers between devices with their start and end apart: 4 -> 4, of which waited for: 1 -> 1; matrix products, arithmetic and copies ran while one was open for 0% -> 1% of each run, Pallas kernels for 3% -> 2%
where the time goes in v4:
time: 73.8 us; the launch traced here: 73.4 us
  blocking collectives  38.9 us (53%)
  starting transfers between devices  18.1 us (25%)
  Pallas kernels  8.32 us (11%)
  waiting for transfers between devices  3.71 us (5%)
  local copies, waits for them, and re-layouts  2.74 us (4%)
  other arithmetic  0.9 us (1%)
    all_to_all x1, blocking collectives, on_device(): lax.all_to_all(rows.reshape(ends, 1, LANES), ('core', 'z'), 0, 0, tiled=T...  26.4 us
    all_to_all x1, blocking collectives, on_device(): lax.all_to_all(payload.reshape(group * (lines + 1), 1, LANES), ('x', 'y')...  12.5 us
    ppermute x2, starting transfers between devices, both_ways(): lax.ppermute(to_previous, axis, backward)  12.1 us
    ppermute x2, starting transfers between devices, both_ways(): lax.ppermute(to_next, axis, forward)  5.95 us
    pallas_call x1, Pallas kernels, on_device(): pl.pallas_call(basis_kernel, out_shape=(jax.ShapeDtypeStruct((copies * WI...  4.77 us
    ppermute x2, waiting for transfers between devices, both_ways(): lax.ppermute(to_previous, axis, backward)  3.7 us
    unnamed x6, local copies, waits for them, and re-layouts  2.05 us
    pallas_call x1, Pallas kernels, on_device(): pl.pallas_call(functools.partial(final_kernel, scale=scale), out_shape=(j...  1.88 us
  transfers between devices with their start and end apart: 4, of which 1 were waited for; matrix products, arithmetic and copies ran while one was open for 1% of the time, Pallas kernels for 2%

profile of v4, /device:TPU:1, one launch (start us, length us, event | category | flops | bytes accessed | tf_op | source)
XLA Modules:
  0.0 73.4 jit_solution(6964956513319861513)
XLA Ops:
  0.6 0.9 %pad_maximum_fusion.1 = f32[2,8,16,128]{3,2,1,0:T(8,128)S(1)} fusion(f32[1,8,16,128]{3,2,1,0:T(8,128)} %bitcast.20, f32[1,8,16,128]{3,2,1,0:T(8,128)} %bitcast.21), kind=kLoop, calls=%fused_computation.1 | loop fusion | flops 32768 | bytes 262144 | tf_op jit(solution)/shard_map/stack | solution.py:429
  1.5 4.0 %collective-permute-start = (f32[2,8,8,128]{3,2,1,0:T(8,128)S(1)}, f32[2,8,8,128]{3,2,1,0:T(8,128)S(1)}, u32[]{:S(2)}, u32[]{:S(2)}) collective-permute-start(f32[2,8,8,128]{3,2,1,0:T(8,128)S(1)} %get-tuple-element.19), channel_id=1, source_target_pairs={{0,1},{1,2},{2,3},{3,4},{4,5},{5,6},{6,7},{7,8},{8,9},{9,10},{10,1... | collective-permute-start | bytes 196616 | tf_op jit(solution)/shard_map/ppermute | solution.py:427
  5.6 1.3 %collective-permute-start.1 = (f32[2,8,8,128]{3,2,1,0:T(8,128)S(1)}, f32[2,8,8,128]{3,2,1,0:T(8,128)S(1)}, u32[]{:S(2)}, u32[]{:S(2)}) collective-permute-start(f32[2,8,8,128]{3,2,1,0:T(8,128)S(1)} %get-tuple-element.20), channel_id=1, source_target_pairs={{1,0},{2,1},{3,2},{4,3},{5,4},{6,5},{7,6},{8,7},{9,8},{10,9},{11,1... | collective-permute-start | bytes 196616 | tf_op jit(solution)/shard_map/ppermute | solution.py:427
  6.9 0.0 collective-permute-done
  6.9 3.7 %collective-permute-done.1 = f32[2,8,8,128]{3,2,1,0:T(8,128)S(1)} collective-permute-done((f32[2,8,8,128]{3,2,1,0:T(8,128)S(1)}, f32[2,8,8,128]{3,2,1,0:T(8,128)S(1)}, u32[]{:S(2)}, u32[]{:S(2)}) %collective-permute-start.1) | collective-permute-done | bytes 65568 | tf_op jit(solution)/shard_map/ppermute | solution.py:427
  10.6 10.8 %collective-permute-start.3 = (f32[2,8,32,128]{3,2,1,0:T(8,128)S(1)}, f32[2,8,32,128]{3,2,1,0:T(8,128)S(1)}, u32[]{:S(2)}, u32[]{:S(2)}) collective-permute-start(f32[2,8,32,128]{3,2,1,0:T(8,128)S(1)} %pad_maximum_fusion.own), channel_id=1, source_target_pairs={{96,0},{192,96},{288,192},{384,288},{480,384},{576,480},{672,576},... | collective-permute-start | bytes 786440 | tf_op jit(solution)/shard_map/ppermute | solution.py:427
  21.5 1.9 %collective-permute-start.2 = (f32[2,8,32,128]{3,2,1,0:T(8,128)S(1)}, f32[2,8,32,128]{3,2,1,0:T(8,128)S(1)}, u32[]{:S(2)}, u32[]{:S(2)}) collective-permute-start(f32[2,8,32,128]{3,2,1,0:T(8,128)S(1)} %pad_maximum_fusion.own), channel_id=1, source_target_pairs={{0,96},{96,192},{192,288},{288,384},{384,480},{480,576},{576,672},... | collective-permute-start | bytes 786440 | tf_op jit(solution)/shard_map/ppermute | solution.py:427
  23.4 0.7 reshape.27.order
  24.1 0.0 copy-start
  24.1 0.7 %copy-done = s32[1,1,384,16]{2,3,1,0:T(8,128)S(1)} copy-done((s32[1,1,384,16]{2,3,1,0:T(8,128)S(1)}, s32[1,1,384,16]{2,3,1,0:T(8,128)}, u32[]{:S(2)}) %copy-start) | copy-done | bytes 24600
  24.8 0.0 copy-start.1
  24.8 0.7 copy-done.1
  25.5 0.0 copy-start.2
  25.5 0.7 copy-done.2
  26.1 1.6 %prepare.1 = (bf16[8,256,768]{2,1,0:T(8,128)(2,1)S(1)}, f32[8,128,768]{2,1,0:T(8,128)S(1)}, f32[8,128]{1,0:T(8,128)S(1)}) custom-call(s32[16,384]{1,0:T(8,128)S(1)} %bitcast.19, s32[1,384]{1,0:T(1,128)S(1)} %reshape.27.order, f32[4]{0:T(128)S(1)} %copy-done.1, f32[4]{0:T(128)S(1)} %copy-done.2), custom_call_target="tpu_custom_call" | custom-call | flops 20000000 | bytes 6400000 | tf_op jit(solution)/shard_map/prepare/pallas_call | solution.py:434
  27.7 0.0 collective-permute-done.3.high
  27.7 0.0 collective-permute-done.2.low
  27.7 4.8 %basis.1 = (f32[128,128]{1,0:T(8,128)S(1)}, f32[1152,128]{1,0:T(8,128)S(1)}) custom-call(f32[2,8,32,128]{3,2,1,0:T(8,128)S(1)} %pad_maximum_fusion.own, f32[2,8,32,128]{3,2,1,0:T(8,128)S(1)} %collective-permute-done.2.low, f32[2,8,32,128]{3,2,1,0:T(8,128)S(1)} %collective-permute-done.3.high, bf16[8,256,768]{2,1,0:T(8,128)(2,1)S(1)} %get-tuple-element.11.lanes_hot, ...), custom_call_target="tpu_custom_call" | custom-call | tf_op jit(solution)/shard_map/basis/pallas_call | solution.py:453
  32.5 12.5 %all_to_all.10 = f32[128,1,128]{2,1,0:T(1,128)S(1)} all-to-all(f32[128,1,128]{2,1,0:T(1,128)S(1)} %bitcast.16), channel_id=1, replica_groups=mesh['x'=4,'core'=2,'z'=12,'y'=8] {'x','y'}, dimensions={0} | all-to-all | bytes 131072 | tf_op jit(solution)/shard_map/all_to_all | solution.py:475
  45.0 0.1 rows.1
  45.1 26.4 %all_to_all.11 = f32[24,1,128]{2,1,0:T(1,128)S(1)} all-to-all(f32[24,1,128]{2,1,0:T(1,128)S(1)} %bitcast.17), channel_id=1, replica_groups=mesh['x'=4,'core'=2,'z'=12,'y'=8] {'core','z'}, dimensions={0} | all-to-all | bytes 24576 | tf_op jit(solution)/shard_map/all_to_all | solution.py:487
  71.5 1.9 %final.1 = (f32[128,128]{1,0:T(8,128)}, f32[128,128]{1,0:T(8,128)}, f32[4]{0:T(128)}) custom-call(f32[24,128]{1,0:T(8,128)S(1)} %bitcast.18, f32[1152,128]{1,0:T(8,128)S(1)} %get-tuple-element.14.basis, f32[8,128]{1,0:T(8,128)S(1)} %get-tuple-element.15.owner), custom_call_target="tpu_custom_call" | custom-call | tf_op jit(solution)/shard_map/final/pallas_call | solution.py:489
  (2 shorter events, 0.0 us)
Async XLA Ops:
  1.5 5.4 %collective-permute-start = (f32[2,8,8,128]{3,2,1,0:T(8,128)S(1)}, f32[2,8,8,128]{3,2,1,0:T(8,128)S(1)}, u32[]{:S(2)}, u32[]{:S(2)}) collective-permute-start(f32[2,8,8,128]{3,2,1,0:T(8,128)S(1)} %get-tuple-element.19), channel_id=1, source_target_pairs={{0,1},{1,2},{2,3},{3,4},{4,5},{5,6},{6,7},{7,8},{8,9},{9,10},{10,1... | collective-permute-start | bytes 196616 | tf_op jit(solution)/shard_map/ppermute | solution.py:427
  5.6 5.0 %collective-permute-start.1 = (f32[2,8,8,128]{3,2,1,0:T(8,128)S(1)}, f32[2,8,8,128]{3,2,1,0:T(8,128)S(1)}, u32[]{:S(2)}, u32[]{:S(2)}) collective-permute-start(f32[2,8,8,128]{3,2,1,0:T(8,128)S(1)} %get-tuple-element.20), channel_id=1, source_target_pairs={{1,0},{2,1},{3,2},{4,3},{5,4},{6,5},{7,6},{8,7},{9,8},{10,9},{11,1... | collective-permute-start | bytes 196616 | tf_op jit(solution)/shard_map/ppermute | solution.py:427
  10.6 17.1 %collective-permute-start.3 = (f32[2,8,32,128]{3,2,1,0:T(8,128)S(1)}, f32[2,8,32,128]{3,2,1,0:T(8,128)S(1)}, u32[]{:S(2)}, u32[]{:S(2)}) collective-permute-start(f32[2,8,32,128]{3,2,1,0:T(8,128)S(1)} %pad_maximum_fusion.own), channel_id=1, source_target_pairs={{96,0},{192,96},{288,192},{384,288},{480,384},{576,480},{672,576},... | collective-permute-start | bytes 786440 | tf_op jit(solution)/shard_map/ppermute | solution.py:427
  21.5 6.2 %collective-permute-start.2 = (f32[2,8,32,128]{3,2,1,0:T(8,128)S(1)}, f32[2,8,32,128]{3,2,1,0:T(8,128)S(1)}, u32[]{:S(2)}, u32[]{:S(2)}) collective-permute-start(f32[2,8,32,128]{3,2,1,0:T(8,128)S(1)} %pad_maximum_fusion.own), channel_id=1, source_target_pairs={{0,96},{96,192},{192,288},{288,384},{384,480},{480,576},{576,672},... | collective-permute-start | bytes 786440 | tf_op jit(solution)/shard_map/ppermute | solution.py:427
  24.1 0.7 %copy-start = (s32[1,1,384,16]{2,3,1,0:T(8,128)S(1)}, s32[1,1,384,16]{2,3,1,0:T(8,128)}, u32[]{:S(2)}) copy-start(s32[1,1,384,16]{2,3,1,0:T(8,128)} %param.8) | copy-start | bytes 73732
  24.8 0.7 copy-start.1
  25.5 0.7 copy-start.2

commit v5 on v4

--- a/solution.py
+++ b/solution.py
@@ -47,9 +47,7 @@
 
 def dd_add(x, y):
     s, e = two_sum(x[0], y[0])
-    t, f = two_sum(x[1], y[1])
-    s, e = quick_two_sum(s, e + t)
-    return quick_two_sum(s, e + f)
+    return quick_two_sum(s, e + (x[1] + y[1]))
 
 
 def dd_mul(x, y):
@@ -66,10 +64,10 @@
 
 
 def dd_sum(terms):
-    total = terms[0]
-    for term in terms[1:]:
-        total = dd_add(total, term)
-    return total
+    terms = list(terms)
+    while len(terms) > 1:
+        terms = [dd_add(*terms[at : at + 2]) if at + 1 < len(terms) else terms[at] for at in range(0, len(terms), 2)]
+    return terms[0]
 
 
 def lane_of(shape):
@@ -80,10 +78,13 @@
     return jnp.where(found, 1.0, 0.0).astype(dtype)
 
 
-def prepare_kernel(index, order, conductance, level, lanes_hot, rows_hot, owner):
-    inlets, plates = index.shape
-    low = (index[...] & 127).astype(jnp.float32)
-    high = (index[...] >> 7).astype(jnp.float32)
+def prepare_kernel(packed, lanes_hot, rows_hot, owner):
+    steps, _, columns = rows_hot.shape
+    inlets, plates = 2 * steps, columns // 2
+    index = packed[:inlets].astype(jnp.int32)
+    order = packed[inlets : inlets + 1].astype(jnp.int32)
+    low = (index & 127).astype(jnp.float32)
+    high = (index >> 7).astype(jnp.float32)
     both = jnp.concatenate([low, high], axis=0).astype(jnp.bfloat16)
     row = lax.broadcasted_iota(jnp.int32, (plates, plates), 0)
     column = lane_of((plates, plates))
@@ -91,7 +92,7 @@
     line, y = group // WIDTH, group % WIDTH
     place, q = (column // OWNED) % PACKED, column % OWNED
     owned = ((line * PACKED + place) * WIDTH + y) * OWNED + q
-    for choice in (row == order[...], row == owned):
+    for choice in (row == order, row == owned):
         both = jnp.dot(both, one_hot(choice, jnp.bfloat16), preferred_element_type=jnp.float32)
         both = both.astype(jnp.bfloat16)
     cells = both.astype(jnp.float32).astype(jnp.int32)
@@ -108,7 +109,8 @@
     first = lax.broadcasted_iota(jnp.int32, (8, LANES), 0) == 0
     values = jnp.zeros((8, LANES), jnp.float32)
     for q in range(OWNED):
-        values = jnp.where(lane == q * FIELDS, jnp.where(first, conductance[q], level[q]), values)
+        own, other = (packed[inlets + 1 : inlets + 2, at : at + 1] for at in (q, OWNED + q))
+        values = jnp.where(lane == q * FIELDS, jnp.where(first, own, other), values)
     owner[...] = values
 
 
@@ -364,7 +366,7 @@
     change = apply_operator([(value, zero) for value in first_coeffs])
     poly = [dd_neg(value) for value in change]
     poly[0] = dd_add(poly[0], (zero + 1.0, zero))
-    nu = None
+    terms = []
     for c, value in enumerate(square(poly)):
         if c == 0:
             overlap = mu
@@ -372,8 +374,8 @@
             up = (shift(mu[0], c), shift(mu[1], c))
             down = (shift(mu[0], -c), shift(mu[1], -c))
             overlap = dd_scale(dd_add(up, down), 0.5)
-        term = dd_mul(value, overlap)
-        nu = term if nu is None else dd_add(nu, term)
+        terms.append(dd_mul(value, overlap))
+    nu = dd_sum(terms)
     second_coeffs = galerkin(nu)
     gain = multiply([(value, zero) for value in second_coeffs], poly)
     drop = apply_operator(gain)
@@ -431,6 +433,8 @@
     own = jnp.concatenate([before, own, after], axis=2)
     low, high = both_ways(own, own, SLAB)
 
+    owned = jnp.pad(jnp.concatenate([conductance, plate_level]), (0, plates - 2 * OWNED))
+    packed = jnp.concatenate([inlet_index[0, 0].T.astype(f32), plate_order.astype(f32)[None], owned[None]])
     lanes_hot, rows_hot, owner = pl.pallas_call(
         prepare_kernel,
         out_shape=(
@@ -438,12 +442,12 @@
             jax.ShapeDtypeStruct((inlets // 2, LANES, 2 * plates), f32),
             jax.ShapeDtypeStruct((8, LANES), f32),
         ),
-        in_specs=[VMEM, VMEM, SMEM, SMEM],
+        in_specs=[VMEM],
         out_specs=(VMEM,) * 3,
         compiler_params=pltpu.CompilerParams(vmem_limit_bytes=8 * 1024 * 1024),
         cost_estimate=pl.CostEstimate(flops=20000000, bytes_accessed=6400000, transcendentals=0),
         name="prepare",
-    )(inlet_index[0, 0].T, plate_order.reshape(1, plates), conductance, plate_level)
+    )(packed)
 
     wide = (3 * cz, cy + 2 * HALO, nx)
     tall = (wide[0], wide[1] + 2 * HALO, nx)

time: 73.8 us -> 73.6 us (level)
  local copies, waits for them, and re-layouts: 2.74 us -> 0.02 us
  other arithmetic: 0.9 us -> 3.09 us
  blocking collectives: 38.9 us -> 39.9 us
    unnamed x6 -> x0, local copies, waits for them, and re-layouts: 2.05 us -> none
    ppermute x2, waiting for transfers between devices: 0.01 us -> 1.5 us  [both_ways(): lax.ppermute(to_next, axis, forward)]
    ppermute x2, waiting for transfers between devices: 3.7 us -> 2.26 us  [both_ways(): lax.ppermute(to_previous, axis, backward)]
    convert_element_type x0 -> x2, other arithmetic: none -> 1.43 us  [the longest x1 0.74 us: on_device(): inlet_index[0, 0].T.astype(f32)]
    all_to_all x1, blocking collectives: 26.4 us -> 27.4 us  [on_device(): lax.all_to_all(rows.reshape(ends, 1, LANES), ('core', 'z'), 0, 0, tiled=T...]
    concatenate x0 -> x2, other arithmetic: none -> 0.76 us  [the longest x1 0.75 us: on_device(): jnp.concatenate([conductance, plate_level])]
  transfers between devices with their start and end apart: 4 -> 4, of which waited for: 1 -> 2; matrix products, arithmetic and copies ran while one was open for 1% -> 3% of each run, Pallas kernels for 2% -> 1%
where the time goes in v5:
time: 73.6 us; the launch traced here: 73.2 us
  blocking collectives  39.9 us (54%)
  starting transfers between devices  18.1 us (25%)
  Pallas kernels  7.62 us (10%)
  waiting for transfers between devices  3.77 us (5%)
  other arithmetic  3.09 us (4%)
    all_to_all x1, blocking collectives, on_device(): lax.all_to_all(rows.reshape(ends, 1, LANES), ('core', 'z'), 0, 0, tiled=T...  27.4 us
    all_to_all x1, blocking collectives, on_device(): lax.all_to_all(payload.reshape(group * (lines + 1), 1, LANES), ('x', 'y')...  12.5 us
    ppermute x2, starting transfers between devices, both_ways(): lax.ppermute(to_previous, axis, backward)  12.1 us
    ppermute x2, starting transfers between devices, both_ways(): lax.ppermute(to_next, axis, forward)  5.95 us
    pallas_call x1, Pallas kernels, on_device(): pl.pallas_call(basis_kernel, out_shape=(jax.ShapeDtypeStruct((copies * WI...  4.77 us
    ppermute x2, waiting for transfers between devices, both_ways(): lax.ppermute(to_previous, axis, backward)  2.26 us
    pallas_call x1, Pallas kernels, on_device(): pl.pallas_call(functools.partial(final_kernel, scale=scale), out_shape=(j...  1.73 us
    ppermute x2, waiting for transfers between devices, both_ways(): lax.ppermute(to_next, axis, forward)  1.5 us
  transfers between devices with their start and end apart: 4, of which 2 were waited for; matrix products, arithmetic and copies ran while one was open for 3% of the time, Pallas kernels for 1%

profile of v5, /device:TPU:1, one launch (start us, length us, event | category | flops | bytes accessed | tf_op | source)
XLA Modules:
  0.0 73.2 jit_solution(8234149583842931041)
XLA Ops:
  0.6 0.9 %pad_maximum_fusion.1 = f32[2,8,16,128]{3,2,1,0:T(8,128)S(1)} fusion(f32[1,8,16,128]{3,2,1,0:T(8,128)} %bitcast.20, f32[1,8,16,128]{3,2,1,0:T(8,128)} %bitcast.21), kind=kLoop, calls=%fused_computation.1 | loop fusion | flops 32768 | bytes 262144 | tf_op jit(solution)/shard_map/stack | solution.py:431
  1.5 4.0 %collective-permute-start = (f32[2,8,8,128]{3,2,1,0:T(8,128)S(1)}, f32[2,8,8,128]{3,2,1,0:T(8,128)S(1)}, u32[]{:S(2)}, u32[]{:S(2)}) collective-permute-start(f32[2,8,8,128]{3,2,1,0:T(8,128)S(1)} %get-tuple-element.19), channel_id=1, source_target_pairs={{0,1},{1,2},{2,3},{3,4},{4,5},{5,6},{6,7},{7,8},{8,9},{9,10},{10,1... | collective-permute-start | bytes 196616 | tf_op jit(solution)/shard_map/ppermute | solution.py:429
  5.6 1.3 %collective-permute-start.1 = (f32[2,8,8,128]{3,2,1,0:T(8,128)S(1)}, f32[2,8,8,128]{3,2,1,0:T(8,128)S(1)}, u32[]{:S(2)}, u32[]{:S(2)}) collective-permute-start(f32[2,8,8,128]{3,2,1,0:T(8,128)S(1)} %get-tuple-element.20), channel_id=1, source_target_pairs={{1,0},{2,1},{3,2},{4,3},{5,4},{6,5},{7,6},{8,7},{9,8},{10,9},{11,1... | collective-permute-start | bytes 196616 | tf_op jit(solution)/shard_map/ppermute | solution.py:429
  6.9 0.7 convert_element_type.17
  7.6 0.7 %select_maximum_fusion = f32[384]{0:T(512)S(1)} fusion(f32[4]{0:T(128)} %param.11, f32[4]{0:T(128)} %param.10), kind=kLoop, calls=%fused_computation.4 | loop fusion | flops 1536 | bytes 1568 | tf_op jit(solution)/shard_map/concatenate | solution.py:436
  8.3 0.0 collective-permute-done
  8.3 2.3 %collective-permute-done.1 = f32[2,8,8,128]{3,2,1,0:T(8,128)S(1)} collective-permute-done((f32[2,8,8,128]{3,2,1,0:T(8,128)S(1)}, f32[2,8,8,128]{3,2,1,0:T(8,128)S(1)}, u32[]{:S(2)}, u32[]{:S(2)}) %collective-permute-start.1) | collective-permute-done | bytes 65568 | tf_op jit(solution)/shard_map/ppermute | solution.py:429
  10.6 10.8 %collective-permute-start.3 = (f32[2,8,32,128]{3,2,1,0:T(8,128)S(1)}, f32[2,8,32,128]{3,2,1,0:T(8,128)S(1)}, u32[]{:S(2)}, u32[]{:S(2)}) collective-permute-start(f32[2,8,32,128]{3,2,1,0:T(8,128)S(1)} %pad_maximum_fusion.own), channel_id=1, source_target_pairs={{96,0},{192,96},{288,192},{384,288},{480,384},{576,480},{672,576},... | collective-permute-start | bytes 786440 | tf_op jit(solution)/shard_map/ppermute | solution.py:429
  21.5 1.9 %collective-permute-start.2 = (f32[2,8,32,128]{3,2,1,0:T(8,128)S(1)}, f32[2,8,32,128]{3,2,1,0:T(8,128)S(1)}, u32[]{:S(2)}, u32[]{:S(2)}) collective-permute-start(f32[2,8,32,128]{3,2,1,0:T(8,128)S(1)} %pad_maximum_fusion.own), channel_id=1, source_target_pairs={{0,96},{96,192},{192,288},{288,384},{384,480},{480,576},{576,672},... | collective-permute-start | bytes 786440 | tf_op jit(solution)/shard_map/ppermute | solution.py:429
  23.4 0.7 %convert_bitcast_fusion = f32[16,384]{1,0:T(8,128)S(1)} fusion(s32[1,1,384,16]{2,3,1,0:T(8,128)} %param.8), kind=kLoop, calls=%fused_computation.3 | loop fusion | flops 6144 | bytes 49152 | tf_op jit(solution)/shard_map/convert_element_type | solution.py:437
  24.1 1.0 %prepare.1 = (bf16[8,256,768]{2,1,0:T(8,128)(2,1)S(1)}, f32[8,128,768]{2,1,0:T(8,128)S(1)}, f32[8,128]{1,0:T(8,128)S(1)}) custom-call(f32[18,384]{1,0:T(8,128)S(1)} %pad_maximum_fusion.2.packed), custom_call_target="tpu_custom_call" | custom-call | flops 20000000 | bytes 6400000 | tf_op jit(solution)/shard_map/prepare/pallas_call | solution.py:438
  25.2 0.0 collective-permute-done.3.high
  25.2 1.5 %collective-permute-done.2.low = f32[2,8,32,128]{3,2,1,0:T(8,128)S(1)} collective-permute-done((f32[2,8,32,128]{3,2,1,0:T(8,128)S(1)}, f32[2,8,32,128]{3,2,1,0:T(8,128)S(1)}, u32[]{:S(2)}, u32[]{:S(2)}) %collective-permute-start.2) | collective-permute-done | bytes 262176 | tf_op jit(solution)/shard_map/ppermute | solution.py:429
  26.7 4.8 %basis.1 = (f32[128,128]{1,0:T(8,128)S(1)}, f32[1152,128]{1,0:T(8,128)S(1)}) custom-call(f32[2,8,32,128]{3,2,1,0:T(8,128)S(1)} %pad_maximum_fusion.own, f32[2,8,32,128]{3,2,1,0:T(8,128)S(1)} %collective-permute-done.2.low, f32[2,8,32,128]{3,2,1,0:T(8,128)S(1)} %collective-permute-done.3.high, bf16[8,256,768]{2,1,0:T(8,128)(2,1)S(1)} %get-tuple-element.11.lanes_hot, ...), custom_call_target="tpu_custom_call" | custom-call | tf_op jit(solution)/shard_map/basis/pallas_call | solution.py:457
  31.5 12.5 %all_to_all.10 = f32[128,1,128]{2,1,0:T(1,128)S(1)} all-to-all(f32[128,1,128]{2,1,0:T(1,128)S(1)} %bitcast.17), channel_id=1, replica_groups=mesh['x'=4,'core'=2,'z'=12,'y'=8] {'x','y'}, dimensions={0} | all-to-all | bytes 131072 | tf_op jit(solution)/shard_map/all_to_all | solution.py:479
  44.0 0.1 rows.1
  44.1 27.4 %all_to_all.11 = f32[24,1,128]{2,1,0:T(1,128)S(1)} all-to-all(f32[24,1,128]{2,1,0:T(1,128)S(1)} %bitcast.18), channel_id=1, replica_groups=mesh['x'=4,'core'=2,'z'=12,'y'=8] {'core','z'}, dimensions={0} | all-to-all | bytes 24576 | tf_op jit(solution)/shard_map/all_to_all | solution.py:491
  71.5 1.7 %final.1 = (f32[128,128]{1,0:T(8,128)}, f32[128,128]{1,0:T(8,128)}, f32[4]{0:T(128)}) custom-call(f32[24,128]{1,0:T(8,128)S(1)} %bitcast.19, f32[1152,128]{1,0:T(8,128)S(1)} %get-tuple-element.14.basis, f32[8,128]{1,0:T(8,128)S(1)} %get-tuple-element.15.owner), custom_call_target="tpu_custom_call" | custom-call | tf_op jit(solution)/shard_map/final/pallas_call | solution.py:493
  (5 shorter events, 0.0 us)
Async XLA Ops:
  1.5 6.8 %collective-permute-start = (f32[2,8,8,128]{3,2,1,0:T(8,128)S(1)}, f32[2,8,8,128]{3,2,1,0:T(8,128)S(1)}, u32[]{:S(2)}, u32[]{:S(2)}) collective-permute-start(f32[2,8,8,128]{3,2,1,0:T(8,128)S(1)} %get-tuple-element.19), channel_id=1, source_target_pairs={{0,1},{1,2},{2,3},{3,4},{4,5},{5,6},{6,7},{7,8},{8,9},{9,10},{10,1... | collective-permute-start | bytes 196616 | tf_op jit(solution)/shard_map/ppermute | solution.py:429
  5.6 5.0 %collective-permute-start.1 = (f32[2,8,8,128]{3,2,1,0:T(8,128)S(1)}, f32[2,8,8,128]{3,2,1,0:T(8,128)S(1)}, u32[]{:S(2)}, u32[]{:S(2)}) collective-permute-start(f32[2,8,8,128]{3,2,1,0:T(8,128)S(1)} %get-tuple-element.20), channel_id=1, source_target_pairs={{1,0},{2,1},{3,2},{4,3},{5,4},{6,5},{7,6},{8,7},{9,8},{10,9},{11,1... | collective-permute-start | bytes 196616 | tf_op jit(solution)/shard_map/ppermute | solution.py:429
  10.6 14.6 %collective-permute-start.3 = (f32[2,8,32,128]{3,2,1,0:T(8,128)S(1)}, f32[2,8,32,128]{3,2,1,0:T(8,128)S(1)}, u32[]{:S(2)}, u32[]{:S(2)}) collective-permute-start(f32[2,8,32,128]{3,2,1,0:T(8,128)S(1)} %pad_maximum_fusion.own), channel_id=1, source_target_pairs={{96,0},{192,96},{288,192},{384,288},{480,384},{576,480},{672,576},... | collective-permute-start | bytes 786440 | tf_op jit(solution)/shard_map/ppermute | solution.py:429
  21.5 5.2 %collective-permute-start.2 = (f32[2,8,32,128]{3,2,1,0:T(8,128)S(1)}, f32[2,8,32,128]{3,2,1,0:T(8,128)S(1)}, u32[]{:S(2)}, u32[]{:S(2)}) collective-permute-start(f32[2,8,32,128]{3,2,1,0:T(8,128)S(1)} %pad_maximum_fusion.own), channel_id=1, source_target_pairs={{0,96},{96,192},{192,288},{288,384},{384,480},{480,576},{576,672},... | collective-permute-start | bytes 786440 | tf_op jit(solution)/shard_map/ppermute | solution.py:429

commit v6 on v5

--- a/solution.py
+++ b/solution.py
@@ -424,9 +424,18 @@
 
     def both_ways(to_next, to_previous, axis):
         count = lax.axis_size(axis)
-        forward = [(i, i + 1) for i in range(count - 1)]
-        backward = [(target, source) for source, target in forward]
-        return lax.ppermute(to_next, axis, forward), lax.ppermute(to_previous, axis, backward)
+        even = lax.axis_index(axis) % 2 == 0
+
+        def swap(value, start):
+            pairs = [(i, i + 1) for i in range(start, count - 1, 2)]
+            return lax.ppermute(value, axis, pairs + [(target, source) for source, target in pairs])
+
+        if to_next is to_previous:
+            outer, inner = swap(to_next, 1), swap(to_next, 0)
+        else:
+            outer = swap(jnp.where(even, to_previous, to_next), 1)
+            inner = swap(jnp.where(even, to_next, to_previous), 0)
+        return jnp.where(even, outer, inner), jnp.where(even, inner, outer)
 
     own = lax.optimization_barrier(jnp.stack([right_side, diagonal]))
     before, after = both_ways(own[:, :, cy - HALO :], own[:, :, :HALO], TILE)

time: 73.6 us -> 72.3 us (0.982)
  blocking collectives: 39.9 us -> 36.9 us
  starting transfers between devices: 18.1 us -> 19.5 us
    all_to_all x1, blocking collectives: 27.4 us -> 24.5 us  [on_device(): lax.all_to_all(rows.reshape(ends, 1, LANES), ('core', 'z'), 0, 0, tiled=T...]
    ppermute x4, starting transfers between devices: 18.1 us -> 19.5 us  [swap(): lax.ppermute(value, axis, pairs + [(target, source) for source, target in...]
where the time goes in v6:
time: 72.3 us; the launch traced here: 71.9 us
  blocking collectives  36.9 us (51%)
  starting transfers between devices  19.5 us (27%)
  Pallas kernels  7.41 us (10%)
  waiting for transfers between devices  4.15 us (6%)
  other arithmetic  3.15 us (4%)
  between operations  0.77 us (1%)
    all_to_all x1, blocking collectives, on_device(): lax.all_to_all(rows.reshape(ends, 1, LANES), ('core', 'z'), 0, 0, tiled=T...  24.5 us
    ppermute x4, starting transfers between devices, swap(): lax.ppermute(value, axis, pairs + [(target, source) for source, target in...  19.5 us
    all_to_all x1, blocking collectives, on_device(): lax.all_to_all(payload.reshape(group * (lines + 1), 1, LANES), ('x', 'y')...  12.4 us
    pallas_call x1, Pallas kernels, on_device(): pl.pallas_call(basis_kernel, out_shape=(jax.ShapeDtypeStruct((copies * WI...  4.56 us
    ppermute x4, waiting for transfers between devices, swap(): lax.ppermute(value, axis, pairs + [(target, source) for source, target in...  4.15 us
    pallas_call x1, Pallas kernels, on_device(): pl.pallas_call(functools.partial(final_kernel, scale=scale), out_shape=(j...  1.73 us
  transfers between devices with their start and end apart: 4, of which 2 were waited for; matrix products, arithmetic and copies ran while one was open for 3% of the time, Pallas kernels for 1%

profile of v6, /device:TPU:1, one launch (start us, length us, event | category | flops | bytes accessed | tf_op | source)
XLA Modules:
  0.0 71.9 jit_solution(5131329063689113275)
XLA Ops:
  0.7 0.9 %pad_maximum_fusion.1 = f32[2,8,16,128]{3,2,1,0:T(8,128)S(1)} fusion(f32[1,8,16,128]{3,2,1,0:T(8,128)} %bitcast.20, f32[1,8,16,128]{3,2,1,0:T(8,128)} %bitcast.21), kind=kLoop, calls=%fused_computation.1 | loop fusion | flops 32768 | bytes 262144 | tf_op jit(solution)/shard_map/stack | solution.py:440
  1.6 0.7 collective-permute-start
  2.2 6.6 %collective-permute-start.1 = (f32[2,8,8,128]{3,2,1,0:T(8,128)S(1)}, f32[2,8,8,128]{3,2,1,0:T(8,128)S(1)}, u32[]{:S(2)}, u32[]{:S(2)}) collective-permute-start(f32[2,8,8,128]{3,2,1,0:T(8,128)S(1)} %get-tuple-element.24), channel_id=1, source_target_pairs={{0,1},{2,3},{4,5},{6,7},{8,9},{10,11},{12,13},{14,15},{16,17},{18,... | collective-permute-start | bytes 196616 | tf_op jit(solution)/shard_map/ppermute | solution.py:431
  8.8 0.7 convert_element_type.17
  9.5 0.7 %select_maximum_fusion = f32[384]{0:T(512)S(1)} fusion(f32[4]{0:T(128)} %param.11, f32[4]{0:T(128)} %param.10), kind=kLoop, calls=%fused_computation.10 | loop fusion | flops 1536 | bytes 1568 | tf_op jit(solution)/shard_map/concatenate | solution.py:445
  10.3 0.0 collective-permute-done
  10.3 0.2 collective-permute-done.1
  10.5 10.4 %collective-permute-start.3 = (f32[2,8,32,128]{3,2,1,0:T(8,128)S(1)}, f32[2,8,32,128]{3,2,1,0:T(8,128)S(1)}, u32[]{:S(2)}, u32[]{:S(2)}) collective-permute-start(f32[2,8,32,128]{3,2,1,0:T(8,128)S(1)} %pad_maximum_fusion.own), channel_id=1, source_target_pairs={{0,96},{192,288},{384,480},{576,672},{96,0},{288,192},{480,384},{6... | collective-permute-start | bytes 786440 | tf_op jit(solution)/shard_map/ppermute | solution.py:431
  20.9 1.9 %collective-permute-start.2 = (f32[2,8,32,128]{3,2,1,0:T(8,128)S(1)}, f32[2,8,32,128]{3,2,1,0:T(8,128)S(1)}, u32[]{:S(2)}, u32[]{:S(2)}) collective-permute-start(f32[2,8,32,128]{3,2,1,0:T(8,128)S(1)} %pad_maximum_fusion.own), channel_id=1, source_target_pairs={{96,192},{288,384},{480,576},{192,96},{384,288},{576,480},{97,193}... | collective-permute-start | bytes 786440 | tf_op jit(solution)/shard_map/ppermute | solution.py:431
  22.8 0.7 %convert_bitcast_fusion = f32[16,384]{1,0:T(8,128)S(1)} fusion(s32[1,1,384,16]{2,3,1,0:T(8,128)} %param.8), kind=kLoop, calls=%fused_computation.9 | loop fusion | flops 6144 | bytes 49152 | tf_op jit(solution)/shard_map/convert_element_type | solution.py:446
  23.6 1.0 %prepare.1 = (bf16[8,256,768]{2,1,0:T(8,128)(2,1)S(1)}, f32[8,128,768]{2,1,0:T(8,128)S(1)}, f32[8,128]{1,0:T(8,128)S(1)}) custom-call(f32[18,384]{1,0:T(8,128)S(1)} %pad_maximum_fusion.2.packed), custom_call_target="tpu_custom_call" | custom-call | flops 20000000 | bytes 6400000 | tf_op jit(solution)/shard_map/prepare/pallas_call | solution.py:447
  24.6 0.0 collective-permute-done.3
  24.6 4.0 %collective-permute-done.2 = f32[2,8,32,128]{3,2,1,0:T(8,128)S(1)} collective-permute-done((f32[2,8,32,128]{3,2,1,0:T(8,128)S(1)}, f32[2,8,32,128]{3,2,1,0:T(8,128)S(1)}, u32[]{:S(2)}, u32[]{:S(2)}) %collective-permute-start.2) | collective-permute-done | bytes 262176 | tf_op jit(solution)/shard_map/ppermute | solution.py:431
  28.6 4.6 %basis.1 = (f32[128,128]{1,0:T(8,128)S(1)}, f32[1152,128]{1,0:T(8,128)S(1)}) custom-call(f32[2,8,32,128]{3,2,1,0:T(8,128)S(1)} %pad_maximum_fusion.own, f32[2,8,32,128]{3,2,1,0:T(8,128)S(1)} %get-tuple-element.20.low, f32[2,8,32,128]{3,2,1,0:T(8,128)S(1)} %get-tuple-element.19.high, bf16[8,256,768]{2,1,0:T(8,128)(2,1)S(1)} %get-tuple-element.11.lanes_hot, ...), custom_call_target="tpu_custom_call" | custom-call | tf_op jit(solution)/shard_map/basis/pallas_call | solution.py:466
  33.2 12.4 %all_to_all.10 = f32[128,1,128]{2,1,0:T(1,128)S(1)} all-to-all(f32[128,1,128]{2,1,0:T(1,128)S(1)} %bitcast.17), channel_id=1, replica_groups=mesh['x'=4,'core'=2,'z'=12,'y'=8] {'x','y'}, dimensions={0} | all-to-all | bytes 131072 | tf_op jit(solution)/shard_map/all_to_all | solution.py:488
  45.6 0.1 rows.1
  45.7 24.5 %all_to_all.11 = f32[24,1,128]{2,1,0:T(1,128)S(1)} all-to-all(f32[24,1,128]{2,1,0:T(1,128)S(1)} %bitcast.18), channel_id=1, replica_groups=mesh['x'=4,'core'=2,'z'=12,'y'=8] {'core','z'}, dimensions={0} | all-to-all | bytes 24576 | tf_op jit(solution)/shard_map/all_to_all | solution.py:500
  70.2 1.7 %final.1 = (f32[128,128]{1,0:T(8,128)}, f32[128,128]{1,0:T(8,128)}, f32[4]{0:T(128)}) custom-call(f32[24,128]{1,0:T(8,128)S(1)} %bitcast.19, f32[1152,128]{1,0:T(8,128)S(1)} %get-tuple-element.14.basis, f32[8,128]{1,0:T(8,128)S(1)} %get-tuple-element.15.owner), custom_call_target="tpu_custom_call" | custom-call | tf_op jit(solution)/shard_map/final/pallas_call | solution.py:502
  (7 shorter events, 0.1 us)
Async XLA Ops:
  1.6 8.7 %collective-permute-start = (f32[2,8,8,128]{3,2,1,0:T(8,128)S(1)}, f32[2,8,8,128]{3,2,1,0:T(8,128)S(1)}, u32[]{:S(2)}, u32[]{:S(2)}) collective-permute-start(f32[2,8,8,128]{3,2,1,0:T(8,128)S(1)} %get-tuple-element.23), channel_id=1, source_target_pairs={{1,2},{3,4},{5,6},{7,8},{9,10},{11,12},{13,14},{15,16},{17,18},{19... | collective-permute-start | bytes 196616 | tf_op jit(solution)/shard_map/ppermute | solution.py:431
  2.2 8.2 %collective-permute-start.1 = (f32[2,8,8,128]{3,2,1,0:T(8,128)S(1)}, f32[2,8,8,128]{3,2,1,0:T(8,128)S(1)}, u32[]{:S(2)}, u32[]{:S(2)}) collective-permute-start(f32[2,8,8,128]{3,2,1,0:T(8,128)S(1)} %get-tuple-element.24), channel_id=1, source_target_pairs={{0,1},{2,3},{4,5},{6,7},{8,9},{10,11},{12,13},{14,15},{16,17},{18,... | collective-permute-start | bytes 196616 | tf_op jit(solution)/shard_map/ppermute | solution.py:431
  10.5 14.1 %collective-permute-start.3 = (f32[2,8,32,128]{3,2,1,0:T(8,128)S(1)}, f32[2,8,32,128]{3,2,1,0:T(8,128)S(1)}, u32[]{:S(2)}, u32[]{:S(2)}) collective-permute-start(f32[2,8,32,128]{3,2,1,0:T(8,128)S(1)} %pad_maximum_fusion.own), channel_id=1, source_target_pairs={{0,96},{192,288},{384,480},{576,672},{96,0},{288,192},{480,384},{6... | collective-permute-start | bytes 786440 | tf_op jit(solution)/shard_map/ppermute | solution.py:431
  20.9 7.7 %collective-permute-start.2 = (f32[2,8,32,128]{3,2,1,0:T(8,128)S(1)}, f32[2,8,32,128]{3,2,1,0:T(8,128)S(1)}, u32[]{:S(2)}, u32[]{:S(2)}) collective-permute-start(f32[2,8,32,128]{3,2,1,0:T(8,128)S(1)} %pad_maximum_fusion.own), channel_id=1, source_target_pairs={{96,192},{288,384},{480,576},{192,96},{384,288},{576,480},{97,193}... | collective-permute-start | bytes 786440 | tf_op jit(solution)/shard_map/ppermute | solution.py:431

commit v7 on v5

--- a/solution.py
+++ b/solution.py
@@ -422,19 +422,23 @@
     plates, inlets = inlet_index.shape[2:]
     f32 = jnp.float32
 
-    def both_ways(to_next, to_previous, axis):
-        count = lax.axis_size(axis)
-        forward = [(i, i + 1) for i in range(count - 1)]
-        backward = [(target, source) for source, target in forward]
-        return lax.ppermute(to_next, axis, forward), lax.ppermute(to_previous, axis, backward)
+    def swap(value, axis, start):
+        pairs = [(i, i + 1) for i in range(start, lax.axis_size(axis) - 1, 2)]
+        return lax.ppermute(value, axis, pairs + [(target, source) for source, target in pairs])
 
     own = lax.optimization_barrier(jnp.stack([right_side, diagonal]))
-    before, after = both_ways(own[:, :, cy - HALO :], own[:, :, :HALO], TILE)
+    even = lax.axis_index(TILE) % 2 == 0
+    first, last = own[:, :, :HALO], own[:, :, cy - HALO :]
+    outer = swap(jnp.where(even, first, last), TILE, 1)
+    inner = swap(jnp.where(even, last, first), TILE, 0)
+    before, after = jnp.where(even, outer, inner), jnp.where(even, inner, outer)
     own = jnp.concatenate([before, own, after], axis=2)
-    low, high = both_ways(own, own, SLAB)
-
     owned = jnp.pad(jnp.concatenate([conductance, plate_level]), (0, plates - 2 * OWNED))
     packed = jnp.concatenate([inlet_index[0, 0].T.astype(f32), plate_order.astype(f32)[None], owned[None]])
+    outer, inner = swap(own, SLAB, 1), swap(own, SLAB, 0)
+    odd = lax.axis_index(SLAB) % 2 == 1
+    low, high = jnp.where(odd, inner, outer), jnp.where(odd, outer, inner)
+
     lanes_hot, rows_hot, owner = pl.pallas_call(
         prepare_kernel,
         out_shape=(

time: 73.6 us -> 70.4 us (0.957)
  waiting for transfers between devices: 3.77 us -> 0.18 us
    ppermute x4, waiting for transfers between devices: 3.77 us -> 0.18 us  [swap(): lax.ppermute(value, axis, pairs + [(target, source) for source, target in...]
    all_to_all x1, blocking collectives: 12.5 us -> 13.8 us  [on_device(): lax.all_to_all(payload.reshape(group * (lines + 1), 1, LANES), ('x', 'y')...]
    all_to_all x1, blocking collectives: 27.4 us -> 26.4 us  [on_device(): lax.all_to_all(rows.reshape(ends, 1, LANES), ('core', 'z'), 0, 0, tiled=T...]
  transfers between devices with their start and end apart: 4 -> 4, of which waited for: 2 -> 1; matrix products, arithmetic and copies ran while one was open for 3% -> 3% of each run, Pallas kernels for 1% -> 1%
where the time goes in v7:
time: 70.4 us; the launch traced here: 70 us
  blocking collectives  40.2 us (57%)
  starting transfers between devices  18.3 us (26%)
  Pallas kernels  7.42 us (11%)
  other arithmetic  3.15 us (4%)
  between operations  0.78 us (1%)
    all_to_all x1, blocking collectives, on_device(): lax.all_to_all(rows.reshape(ends, 1, LANES), ('core', 'z'), 0, 0, tiled=T...  26.4 us
    ppermute x4, starting transfers between devices, swap(): lax.ppermute(value, axis, pairs + [(target, source) for source, target in...  18.3 us
    all_to_all x1, blocking collectives, on_device(): lax.all_to_all(payload.reshape(group * (lines + 1), 1, LANES), ('x', 'y')...  13.8 us
    pallas_call x1, Pallas kernels, on_device(): pl.pallas_call(basis_kernel, out_shape=(jax.ShapeDtypeStruct((copies * WI...  4.57 us
    pallas_call x1, Pallas kernels, on_device(): pl.pallas_call(functools.partial(final_kernel, scale=scale), out_shape=(j...  1.73 us
  transfers between devices with their start and end apart: 4, of which 1 were waited for; matrix products, arithmetic and copies ran while one was open for 3% of the time, Pallas kernels for 1%

profile of v7, /device:TPU:1, one launch (start us, length us, event | category | flops | bytes accessed | tf_op | source)
XLA Modules:
  0.0 70.0 jit_solution(8811442826608998642)
XLA Ops:
  0.7 0.9 %pad_maximum_fusion.1 = f32[2,8,16,128]{3,2,1,0:T(8,128)S(1)} fusion(f32[1,8,16,128]{3,2,1,0:T(8,128)} %bitcast.20, f32[1,8,16,128]{3,2,1,0:T(8,128)} %bitcast.21), kind=kLoop, calls=%fused_computation.1 | loop fusion | flops 32768 | bytes 262144 | tf_op jit(solution)/shard_map/stack | solution.py:429
  1.6 0.7 collective-permute-start
  2.2 6.6 %collective-permute-start.1 = (f32[2,8,8,128]{3,2,1,0:T(8,128)S(1)}, f32[2,8,8,128]{3,2,1,0:T(8,128)S(1)}, u32[]{:S(2)}, u32[]{:S(2)}) collective-permute-start(f32[2,8,8,128]{3,2,1,0:T(8,128)S(1)} %get-tuple-element.24), channel_id=1, source_target_pairs={{0,1},{2,3},{4,5},{6,7},{8,9},{10,11},{12,13},{14,15},{16,17},{18,... | collective-permute-start | bytes 196616 | tf_op jit(solution)/shard_map/ppermute | solution.py:427
  8.8 0.7 convert_element_type.17
  9.5 0.7 %select_maximum_fusion = f32[384]{0:T(512)S(1)} fusion(f32[4]{0:T(128)} %param.11, f32[4]{0:T(128)} %param.10), kind=kLoop, calls=%fused_computation.10 | loop fusion | flops 1536 | bytes 1568 | tf_op jit(solution)/shard_map/concatenate | solution.py:436
  10.3 0.0 collective-permute-done
  10.3 0.2 collective-permute-done.1
  10.5 4.8 %collective-permute-start.3 = (f32[2,8,32,128]{3,2,1,0:T(8,128)S(1)}, f32[2,8,32,128]{3,2,1,0:T(8,128)S(1)}, u32[]{:S(2)}, u32[]{:S(2)}) collective-permute-start(f32[2,8,32,128]{3,2,1,0:T(8,128)S(1)} %pad_maximum_fusion.own), channel_id=1, source_target_pairs={{96,192},{288,384},{480,576},{192,96},{384,288},{576,480},{97,193}... | collective-permute-start | bytes 786440 | tf_op jit(solution)/shard_map/ppermute | solution.py:427
  15.3 6.2 %collective-permute-start.2 = (f32[2,8,32,128]{3,2,1,0:T(8,128)S(1)}, f32[2,8,32,128]{3,2,1,0:T(8,128)S(1)}, u32[]{:S(2)}, u32[]{:S(2)}) collective-permute-start(f32[2,8,32,128]{3,2,1,0:T(8,128)S(1)} %pad_maximum_fusion.own), channel_id=1, source_target_pairs={{0,96},{192,288},{384,480},{576,672},{96,0},{288,192},{480,384},{6... | collective-permute-start | bytes 786440 | tf_op jit(solution)/shard_map/ppermute | solution.py:427
  21.6 0.7 %convert_bitcast_fusion = f32[16,384]{1,0:T(8,128)S(1)} fusion(s32[1,1,384,16]{2,3,1,0:T(8,128)} %param.8), kind=kLoop, calls=%fused_computation.9 | loop fusion | flops 6144 | bytes 49152 | tf_op jit(solution)/shard_map/convert_element_type | solution.py:437
  22.3 1.0 %prepare.1 = (bf16[8,256,768]{2,1,0:T(8,128)(2,1)S(1)}, f32[8,128,768]{2,1,0:T(8,128)S(1)}, f32[8,128]{1,0:T(8,128)S(1)}) custom-call(f32[18,384]{1,0:T(8,128)S(1)} %pad_maximum_fusion.2.packed), custom_call_target="tpu_custom_call" | custom-call | flops 20000000 | bytes 6400000 | tf_op jit(solution)/shard_map/prepare/pallas_call | solution.py:442
  23.3 0.0 collective-permute-done.3
  23.4 0.0 collective-permute-done.2
  23.4 4.6 %basis.1 = (f32[128,128]{1,0:T(8,128)S(1)}, f32[1152,128]{1,0:T(8,128)S(1)}) custom-call(f32[2,8,32,128]{3,2,1,0:T(8,128)S(1)} %pad_maximum_fusion.own, f32[2,8,32,128]{3,2,1,0:T(8,128)S(1)} %get-tuple-element.20.low, f32[2,8,32,128]{3,2,1,0:T(8,128)S(1)} %get-tuple-element.19.high, bf16[8,256,768]{2,1,0:T(8,128)(2,1)S(1)} %get-tuple-element.11.lanes_hot, ...), custom_call_target="tpu_custom_call" | custom-call | tf_op jit(solution)/shard_map/basis/pallas_call | solution.py:461
  28.0 13.8 %all_to_all.10 = f32[128,1,128]{2,1,0:T(1,128)S(1)} all-to-all(f32[128,1,128]{2,1,0:T(1,128)S(1)} %bitcast.17), channel_id=1, replica_groups=mesh['x'=4,'core'=2,'z'=12,'y'=8] {'x','y'}, dimensions={0} | all-to-all | bytes 131072 | tf_op jit(solution)/shard_map/all_to_all | solution.py:483
  41.8 0.1 rows.1
  41.9 26.4 %all_to_all.11 = f32[24,1,128]{2,1,0:T(1,128)S(1)} all-to-all(f32[24,1,128]{2,1,0:T(1,128)S(1)} %bitcast.18), channel_id=1, replica_groups=mesh['x'=4,'core'=2,'z'=12,'y'=8] {'core','z'}, dimensions={0} | all-to-all | bytes 24576 | tf_op jit(solution)/shard_map/all_to_all | solution.py:495
  68.3 1.7 %final.1 = (f32[128,128]{1,0:T(8,128)}, f32[128,128]{1,0:T(8,128)}, f32[4]{0:T(128)}) custom-call(f32[24,128]{1,0:T(8,128)S(1)} %bitcast.19, f32[1152,128]{1,0:T(8,128)S(1)} %get-tuple-element.14.basis, f32[8,128]{1,0:T(8,128)S(1)} %get-tuple-element.15.owner), custom_call_target="tpu_custom_call" | custom-call | tf_op jit(solution)/shard_map/final/pallas_call | solution.py:497
  (7 shorter events, 0.1 us)
Async XLA Ops:
  1.6 8.7 %collective-permute-start = (f32[2,8,8,128]{3,2,1,0:T(8,128)S(1)}, f32[2,8,8,128]{3,2,1,0:T(8,128)S(1)}, u32[]{:S(2)}, u32[]{:S(2)}) collective-permute-start(f32[2,8,8,128]{3,2,1,0:T(8,128)S(1)} %get-tuple-element.23), channel_id=1, source_target_pairs={{1,2},{3,4},{5,6},{7,8},{9,10},{11,12},{13,14},{15,16},{17,18},{19... | collective-permute-start | bytes 196616 | tf_op jit(solution)/shard_map/ppermute | solution.py:427
  2.2 8.2 %collective-permute-start.1 = (f32[2,8,8,128]{3,2,1,0:T(8,128)S(1)}, f32[2,8,8,128]{3,2,1,0:T(8,128)S(1)}, u32[]{:S(2)}, u32[]{:S(2)}) collective-permute-start(f32[2,8,8,128]{3,2,1,0:T(8,128)S(1)} %get-tuple-element.24), channel_id=1, source_target_pairs={{0,1},{2,3},{4,5},{6,7},{8,9},{10,11},{12,13},{14,15},{16,17},{18,... | collective-permute-start | bytes 196616 | tf_op jit(solution)/shard_map/ppermute | solution.py:427
  10.5 12.8 %collective-permute-start.3 = (f32[2,8,32,128]{3,2,1,0:T(8,128)S(1)}, f32[2,8,32,128]{3,2,1,0:T(8,128)S(1)}, u32[]{:S(2)}, u32[]{:S(2)}) collective-permute-start(f32[2,8,32,128]{3,2,1,0:T(8,128)S(1)} %pad_maximum_fusion.own), channel_id=1, source_target_pairs={{96,192},{288,384},{480,576},{192,96},{384,288},{576,480},{97,193}... | collective-permute-start | bytes 786440 | tf_op jit(solution)/shard_map/ppermute | solution.py:427
  15.3 8.0 %collective-permute-start.2 = (f32[2,8,32,128]{3,2,1,0:T(8,128)S(1)}, f32[2,8,32,128]{3,2,1,0:T(8,128)S(1)}, u32[]{:S(2)}, u32[]{:S(2)}) collective-permute-start(f32[2,8,32,128]{3,2,1,0:T(8,128)S(1)} %pad_maximum_fusion.own), channel_id=1, source_target_pairs={{0,96},{192,288},{384,480},{576,672},{96,0},{288,192},{480,384},{6... | collective-permute-start | bytes 786440 | tf_op jit(solution)/shard_map/ppermute | solution.py:427

commit v8 on v7

--- a/solution.py
+++ b/solution.py
@@ -435,9 +435,21 @@
     own = jnp.concatenate([before, own, after], axis=2)
     owned = jnp.pad(jnp.concatenate([conductance, plate_level]), (0, plates - 2 * OWNED))
     packed = jnp.concatenate([inlet_index[0, 0].T.astype(f32), plate_order.astype(f32)[None], owned[None]])
-    outer, inner = swap(own, SLAB, 1), swap(own, SLAB, 0)
     odd = lax.axis_index(SLAB) % 2 == 1
-    low, high = jnp.where(odd, inner, outer), jnp.where(odd, outer, inner)
+    near = jnp.where(odd, own[:, ::-1], own)
+    middle = slice(HALO, HALO + cy)
+    sides = jnp.concatenate([near[:, :, :HALO], near[:, :, HALO + cy :]], axis=2)
+    sent = [near[0, :, middle], near[1, : cz - 1, middle], sides[0, : cz - 1], sides[1, : cz - 2]]
+    arrived = swap(jnp.concatenate(sent), SLAB, 1)
+    inner = swap(own, SLAB, 0)
+    pieces, start = [], 0
+    for piece in sent:
+        count = piece.shape[0]
+        pieces.append(jnp.pad(arrived[start : start + count], ((0, cz - count), (0, 0), (0, 0))))
+        start += count
+    middle, sides = jnp.stack(pieces[:2]), jnp.stack(pieces[2:])
+    outer = jnp.concatenate([sides[:, :, :HALO], middle, sides[:, :, HALO:]], axis=2)
+    low, high = jnp.where(odd, inner, outer[:, ::-1]), jnp.where(odd, outer, inner)
 
     lanes_hot, rows_hot, owner = pl.pallas_call(
         prepare_kernel,

time: 70.4 us -> 70.3 us (level)
  waiting for transfers between devices: 0.18 us -> 1.23 us
    ppermute x4, waiting for transfers between devices: 0.18 us -> 1.23 us  [swap(): lax.ppermute(value, axis, pairs + [(target, source) for source, target in...]
    convert_element_type x1, other arithmetic: 0.74 us -> 0.01 us  [on_device(): inlet_index[0, 0].T.astype(f32)]
  transfers between devices with their start and end apart: 4 -> 4, of which waited for: 1 -> 2; matrix products, arithmetic and copies ran while one was open for 3% -> 2% of each run, Pallas kernels for 1% -> 1%
where the time goes in v8:
time: 70.3 us; the launch traced here: 69.9 us
  blocking collectives  39.5 us (56%)
  starting transfers between devices  18.3 us (26%)
  Pallas kernels  7.42 us (11%)
  other arithmetic  2.53 us (4%)
  waiting for transfers between devices  1.23 us (2%)
  between operations  0.9 us (1%)
    all_to_all x1, blocking collectives, on_device(): lax.all_to_all(rows.reshape(ends, 1, LANES), ('core', 'z'), 0, 0, tiled=T...  26 us
    ppermute x4, starting transfers between devices, swap(): lax.ppermute(value, axis, pairs + [(target, source) for source, target in...  18.3 us
    all_to_all x1, blocking collectives, on_device(): lax.all_to_all(payload.reshape(group * (lines + 1), 1, LANES), ('x', 'y')...  13.5 us
    pallas_call x1, Pallas kernels, on_device(): pl.pallas_call(basis_kernel, out_shape=(jax.ShapeDtypeStruct((copies * WI...  4.57 us
    pallas_call x1, Pallas kernels, on_device(): pl.pallas_call(functools.partial(final_kernel, scale=scale), out_shape=(j...  1.73 us
  transfers between devices with their start and end apart: 4, of which 2 were waited for; matrix products, arithmetic and copies ran while one was open for 2% of the time, Pallas kernels for 1%

profile of v8, /device:TPU:1, one launch (start us, length us, event | category | flops | bytes accessed | tf_op | source)
XLA Modules:
  0.0 69.9 jit_solution(3271137534499897490)
XLA Ops:
  0.6 0.0 copy-start
  0.7 0.9 %pad_maximum_fusion.2 = f32[2,8,16,128]{3,2,1,0:T(8,128)S(1)} fusion(f32[1,8,16,128]{3,2,1,0:T(8,128)} %bitcast.36, f32[1,8,16,128]{3,2,1,0:T(8,128)} %bitcast.37), kind=kLoop, calls=%fused_computation.7 | loop fusion | flops 32768 | bytes 262144 | tf_op jit(solution)/shard_map/stack | solution.py:429
  1.6 0.7 collective-permute-start
  2.2 6.6 %collective-permute-start.1 = (f32[2,8,8,128]{3,2,1,0:T(8,128)S(1)}, f32[2,8,8,128]{3,2,1,0:T(8,128)S(1)}, u32[]{:S(2)}, u32[]{:S(2)}) collective-permute-start(f32[2,8,8,128]{3,2,1,0:T(8,128)S(1)} %get-tuple-element.28), channel_id=1, source_target_pairs={{0,1},{2,3},{4,5},{6,7},{8,9},{10,11},{12,13},{14,15},{16,17},{18,... | collective-permute-start | bytes 196616 | tf_op jit(solution)/shard_map/ppermute | solution.py:427
  8.8 0.7 convert_element_type.22
  9.5 0.7 %select_maximum_fusion.1 = f32[384]{0:T(512)S(1)} fusion(f32[4]{0:T(128)} %param.11, f32[4]{0:T(128)} %param.10), kind=kLoop, calls=%fused_computation.27 | loop fusion | flops 1536 | bytes 1568 | tf_op jit(solution)/shard_map/concatenate | solution.py:436
  10.3 0.0 collective-permute-done
  10.3 0.2 collective-permute-done.1
  10.6 4.8 %collective-permute-start.3 = (f32[28,16,128]{2,1,0:T(8,128)S(1)}, f32[28,16,128]{2,1,0:T(8,128)S(1)}, u32[]{:S(2)}, u32[]{:S(2)}) collective-permute-start(f32[28,16,128]{2,1,0:T(8,128)S(1)} %pad_maximum_fusion.1), channel_id=1, source_target_pairs={{96,192},{288,384},{480,576},{192,96},{384,288},{576,480},{97,193}... | collective-permute-start | bytes 688136 | tf_op jit(solution)/shard_map/ppermute | solution.py:427
  15.5 0.0 copy-done
  15.5 1.0 %prepare.1 = (bf16[8,256,768]{2,1,0:T(8,128)(2,1)S(1)}, f32[8,128,768]{2,1,0:T(8,128)S(1)}, f32[8,128]{1,0:T(8,128)S(1)}) custom-call(f32[18,384]{1,0:T(8,128)S(1)} %pad_maximum_fusion.4.packed), custom_call_target="tpu_custom_call" | custom-call | flops 20000000 | bytes 6400000 | tf_op jit(solution)/shard_map/prepare/pallas_call | solution.py:454
  16.5 6.2 %collective-permute-start.2 = (f32[2,8,32,128]{3,2,1,0:T(8,128)S(1)}, f32[2,8,32,128]{3,2,1,0:T(8,128)S(1)}, u32[]{:S(2)}, u32[]{:S(2)}) collective-permute-start(f32[2,8,32,128]{3,2,1,0:T(8,128)S(1)} %pad_maximum_fusion.own), channel_id=1, source_target_pairs={{0,96},{192,288},{384,480},{576,672},{96,0},{288,192},{480,384},{6... | collective-permute-start | bytes 786440 | tf_op jit(solution)/shard_map/ppermute | solution.py:427
  22.8 0.0 collective-permute-done.3
  22.9 1.0 %collective-permute-done.2 = f32[2,8,32,128]{3,2,1,0:T(8,128)S(1)} collective-permute-done((f32[2,8,32,128]{3,2,1,0:T(8,128)S(1)}, f32[2,8,32,128]{3,2,1,0:T(8,128)S(1)}, u32[]{:S(2)}, u32[]{:S(2)}) %collective-permute-start.2) | collective-permute-done | bytes 262176 | tf_op jit(solution)/shard_map/ppermute | solution.py:427
  23.9 0.1 broadcast_select_fusion
  24.0 4.6 %basis.1 = (f32[128,128]{1,0:T(8,128)S(1)}, f32[1152,128]{1,0:T(8,128)S(1)}) custom-call(f32[2,8,32,128]{3,2,1,0:T(8,128)S(1)} %pad_maximum_fusion.own, f32[2,8,32,128]{3,2,1,0:T(8,128)S(1)} %reverse_select_fusion.1.low, f32[2,8,32,128]{3,2,1,0:T(8,128)S(1)} %get-tuple-element.19.high, bf16[8,256,768]{2,1,0:T(8,128)(2,1)S(1)} %get-tuple-element.11.lanes_hot, ...), custom_call_target="tpu_custom_call" | custom-call | tf_op jit(solution)/shard_map/basis/pallas_call | solution.py:473
  28.6 13.5 %all_to_all.10 = f32[128,1,128]{2,1,0:T(1,128)S(1)} all-to-all(f32[128,1,128]{2,1,0:T(1,128)S(1)} %bitcast.33), channel_id=1, replica_groups=mesh['x'=4,'core'=2,'z'=12,'y'=8] {'x','y'}, dimensions={0} | all-to-all | bytes 131072 | tf_op jit(solution)/shard_map/all_to_all | solution.py:495
  42.1 0.1 rows.1
  42.2 26.0 %all_to_all.11 = f32[24,1,128]{2,1,0:T(1,128)S(1)} all-to-all(f32[24,1,128]{2,1,0:T(1,128)S(1)} %bitcast.34), channel_id=1, replica_groups=mesh['x'=4,'core'=2,'z'=12,'y'=8] {'core','z'}, dimensions={0} | all-to-all | bytes 24576 | tf_op jit(solution)/shard_map/all_to_all | solution.py:507
  68.2 1.7 %final.1 = (f32[128,128]{1,0:T(8,128)}, f32[128,128]{1,0:T(8,128)}, f32[4]{0:T(128)}) custom-call(f32[24,128]{1,0:T(8,128)S(1)} %bitcast.35, f32[1152,128]{1,0:T(8,128)S(1)} %get-tuple-element.14.basis, f32[8,128]{1,0:T(8,128)S(1)} %get-tuple-element.15.owner), custom_call_target="tpu_custom_call" | custom-call | tf_op jit(solution)/shard_map/final/pallas_call | solution.py:509
  (20 shorter events, 0.2 us)
Async XLA Ops:
  0.6 14.9 %copy-start = (s32[1,1,384,16]{2,3,1,0:T(8,128)S(1)}, s32[1,1,384,16]{2,3,1,0:T(8,128)}, u32[]{:S(2)}) copy-start(s32[1,1,384,16]{2,3,1,0:T(8,128)} %param.8) | copy-start | bytes 73732
  1.6 8.7 %collective-permute-start = (f32[2,8,8,128]{3,2,1,0:T(8,128)S(1)}, f32[2,8,8,128]{3,2,1,0:T(8,128)S(1)}, u32[]{:S(2)}, u32[]{:S(2)}) collective-permute-start(f32[2,8,8,128]{3,2,1,0:T(8,128)S(1)} %get-tuple-element.27), channel_id=1, source_target_pairs={{1,2},{3,4},{5,6},{7,8},{9,10},{11,12},{13,14},{15,16},{17,18},{19... | collective-permute-start | bytes 196616 | tf_op jit(solution)/shard_map/ppermute | solution.py:427
  2.2 8.2 %collective-permute-start.1 = (f32[2,8,8,128]{3,2,1,0:T(8,128)S(1)}, f32[2,8,8,128]{3,2,1,0:T(8,128)S(1)}, u32[]{:S(2)}, u32[]{:S(2)}) collective-permute-start(f32[2,8,8,128]{3,2,1,0:T(8,128)S(1)} %get-tuple-element.28), channel_id=1, source_target_pairs={{0,1},{2,3},{4,5},{6,7},{8,9},{10,11},{12,13},{14,15},{16,17},{18,... | collective-permute-start | bytes 196616 | tf_op jit(solution)/shard_map/ppermute | solution.py:427
  10.6 12.1 %collective-permute-start.3 = (f32[28,16,128]{2,1,0:T(8,128)S(1)}, f32[28,16,128]{2,1,0:T(8,128)S(1)}, u32[]{:S(2)}, u32[]{:S(2)}) collective-permute-start(f32[28,16,128]{2,1,0:T(8,128)S(1)} %pad_maximum_fusion.1), channel_id=1, source_target_pairs={{96,192},{288,384},{480,576},{192,96},{384,288},{576,480},{97,193}... | collective-permute-start | bytes 688136 | tf_op jit(solution)/shard_map/ppermute | solution.py:427
  16.5 7.4 %collective-permute-start.2 = (f32[2,8,32,128]{3,2,1,0:T(8,128)S(1)}, f32[2,8,32,128]{3,2,1,0:T(8,128)S(1)}, u32[]{:S(2)}, u32[]{:S(2)}) collective-permute-start(f32[2,8,32,128]{3,2,1,0:T(8,128)S(1)} %pad_maximum_fusion.own), channel_id=1, source_target_pairs={{0,96},{192,288},{384,480},{576,672},{96,0},{288,192},{480,384},{6... | collective-permute-start | bytes 786440 | tf_op jit(solution)/shard_map/ppermute | solution.py:427

commit v9 on v7

--- a/solution.py
+++ b/solution.py
@@ -305,7 +305,8 @@
     terms = [[] for _ in range(len(left) + len(right) - 1)]
     for i, a in enumerate(left):
         for j, b in enumerate(right):
-            half = dd_scale(dd_mul(a, b), 0.5)
+            product, error = two_prod(a, b[0])
+            half = dd_scale(quick_two_sum(product, error + a * b[1]), 0.5)
             terms[i + j].append(half)
             terms[abs(i - j)].append(half)
     return [dd_sum(group) for group in terms]
@@ -377,7 +378,7 @@
         terms.append(dd_mul(value, overlap))
     nu = dd_sum(terms)
     second_coeffs = galerkin(nu)
-    gain = multiply([(value, zero) for value in second_coeffs], poly)
+    gain = multiply(second_coeffs, poly)
     drop = apply_operator(gain)
     solved = list(gain)
     for j in range(4):

time: 70.4 us -> 70.4 us (level)
  no operation moved by 1% of the time
where the time goes in v9:
time: 70.4 us; the launch traced here: 70 us
  blocking collectives  40.2 us (57%)
  starting transfers between devices  18.3 us (26%)
  Pallas kernels  7.41 us (11%)
  other arithmetic  3.15 us (4%)
  between operations  0.78 us (1%)
    all_to_all x1, blocking collectives, on_device(): lax.all_to_all(rows.reshape(ends, 1, LANES), ('core', 'z'), 0, 0, tiled=T...  26.4 us
    ppermute x4, starting transfers between devices, swap(): lax.ppermute(value, axis, pairs + [(target, source) for source, target in...  18.3 us
    all_to_all x1, blocking collectives, on_device(): lax.all_to_all(payload.reshape(group * (lines + 1), 1, LANES), ('x', 'y')...  13.8 us
    pallas_call x1, Pallas kernels, on_device(): pl.pallas_call(basis_kernel, out_shape=(jax.ShapeDtypeStruct((copies * WI...  4.57 us
    pallas_call x1, Pallas kernels, on_device(): pl.pallas_call(functools.partial(final_kernel, scale=scale), out_shape=(j...  1.72 us
  transfers between devices with their start and end apart: 4, of which 1 were waited for; matrix products, arithmetic and copies ran while one was open for 3% of the time, Pallas kernels for 1%

profile of v9, /device:TPU:1, one launch (start us, length us, event | category | flops | bytes accessed | tf_op | source)
XLA Modules:
  0.0 70.0 jit_solution(10020703240887894663)
XLA Ops:
  0.7 0.9 %pad_maximum_fusion.1 = f32[2,8,16,128]{3,2,1,0:T(8,128)S(1)} fusion(f32[1,8,16,128]{3,2,1,0:T(8,128)} %bitcast.20, f32[1,8,16,128]{3,2,1,0:T(8,128)} %bitcast.21), kind=kLoop, calls=%fused_computation.1 | loop fusion | flops 32768 | bytes 262144 | tf_op jit(solution)/shard_map/stack | solution.py:430
  1.6 0.7 collective-permute-start
  2.2 6.6 %collective-permute-start.1 = (f32[2,8,8,128]{3,2,1,0:T(8,128)S(1)}, f32[2,8,8,128]{3,2,1,0:T(8,128)S(1)}, u32[]{:S(2)}, u32[]{:S(2)}) collective-permute-start(f32[2,8,8,128]{3,2,1,0:T(8,128)S(1)} %get-tuple-element.24), channel_id=1, source_target_pairs={{0,1},{2,3},{4,5},{6,7},{8,9},{10,11},{12,13},{14,15},{16,17},{18,... | collective-permute-start | bytes 196616 | tf_op jit(solution)/shard_map/ppermute | solution.py:428
  8.8 0.7 convert_element_type.17
  9.5 0.7 %select_maximum_fusion = f32[384]{0:T(512)S(1)} fusion(f32[4]{0:T(128)} %param.11, f32[4]{0:T(128)} %param.10), kind=kLoop, calls=%fused_computation.10 | loop fusion | flops 1536 | bytes 1568 | tf_op jit(solution)/shard_map/concatenate | solution.py:437
  10.3 0.0 collective-permute-done
  10.3 0.2 collective-permute-done.1
  10.5 4.8 %collective-permute-start.3 = (f32[2,8,32,128]{3,2,1,0:T(8,128)S(1)}, f32[2,8,32,128]{3,2,1,0:T(8,128)S(1)}, u32[]{:S(2)}, u32[]{:S(2)}) collective-permute-start(f32[2,8,32,128]{3,2,1,0:T(8,128)S(1)} %pad_maximum_fusion.own), channel_id=1, source_target_pairs={{96,192},{288,384},{480,576},{192,96},{384,288},{576,480},{97,193}... | collective-permute-start | bytes 786440 | tf_op jit(solution)/shard_map/ppermute | solution.py:428
  15.3 6.2 %collective-permute-start.2 = (f32[2,8,32,128]{3,2,1,0:T(8,128)S(1)}, f32[2,8,32,128]{3,2,1,0:T(8,128)S(1)}, u32[]{:S(2)}, u32[]{:S(2)}) collective-permute-start(f32[2,8,32,128]{3,2,1,0:T(8,128)S(1)} %pad_maximum_fusion.own), channel_id=1, source_target_pairs={{0,96},{192,288},{384,480},{576,672},{96,0},{288,192},{480,384},{6... | collective-permute-start | bytes 786440 | tf_op jit(solution)/shard_map/ppermute | solution.py:428
  21.6 0.7 %convert_bitcast_fusion = f32[16,384]{1,0:T(8,128)S(1)} fusion(s32[1,1,384,16]{2,3,1,0:T(8,128)} %param.8), kind=kLoop, calls=%fused_computation.9 | loop fusion | flops 6144 | bytes 49152 | tf_op jit(solution)/shard_map/convert_element_type | solution.py:438
  22.3 1.0 %prepare.1 = (bf16[8,256,768]{2,1,0:T(8,128)(2,1)S(1)}, f32[8,128,768]{2,1,0:T(8,128)S(1)}, f32[8,128]{1,0:T(8,128)S(1)}) custom-call(f32[18,384]{1,0:T(8,128)S(1)} %pad_maximum_fusion.2.packed), custom_call_target="tpu_custom_call" | custom-call | flops 20000000 | bytes 6400000 | tf_op jit(solution)/shard_map/prepare/pallas_call | solution.py:443
  23.3 0.0 collective-permute-done.3
  23.4 0.0 collective-permute-done.2
  23.4 4.6 %basis.1 = (f32[128,128]{1,0:T(8,128)S(1)}, f32[1152,128]{1,0:T(8,128)S(1)}) custom-call(f32[2,8,32,128]{3,2,1,0:T(8,128)S(1)} %pad_maximum_fusion.own, f32[2,8,32,128]{3,2,1,0:T(8,128)S(1)} %get-tuple-element.20.low, f32[2,8,32,128]{3,2,1,0:T(8,128)S(1)} %get-tuple-element.19.high, bf16[8,256,768]{2,1,0:T(8,128)(2,1)S(1)} %get-tuple-element.11.lanes_hot, ...), custom_call_target="tpu_custom_call" | custom-call | tf_op jit(solution)/shard_map/basis/pallas_call | solution.py:462
  28.0 13.8 %all_to_all.10 = f32[128,1,128]{2,1,0:T(1,128)S(1)} all-to-all(f32[128,1,128]{2,1,0:T(1,128)S(1)} %bitcast.17), channel_id=1, replica_groups=mesh['x'=4,'core'=2,'z'=12,'y'=8] {'x','y'}, dimensions={0} | all-to-all | bytes 131072 | tf_op jit(solution)/shard_map/all_to_all | solution.py:484
  41.8 0.1 rows.1
  41.9 26.4 %all_to_all.11 = f32[24,1,128]{2,1,0:T(1,128)S(1)} all-to-all(f32[24,1,128]{2,1,0:T(1,128)S(1)} %bitcast.18), channel_id=1, replica_groups=mesh['x'=4,'core'=2,'z'=12,'y'=8] {'core','z'}, dimensions={0} | all-to-all | bytes 24576 | tf_op jit(solution)/shard_map/all_to_all | solution.py:496
  68.3 1.7 %final.1 = (f32[128,128]{1,0:T(8,128)}, f32[128,128]{1,0:T(8,128)}, f32[4]{0:T(128)}) custom-call(f32[24,128]{1,0:T(8,128)S(1)} %bitcast.19, f32[1152,128]{1,0:T(8,128)S(1)} %get-tuple-element.14.basis, f32[8,128]{1,0:T(8,128)S(1)} %get-tuple-element.15.owner), custom_call_target="tpu_custom_call" | custom-call | tf_op jit(solution)/shard_map/final/pallas_call | solution.py:498
  (7 shorter events, 0.1 us)
Async XLA Ops:
  1.6 8.7 %collective-permute-start = (f32[2,8,8,128]{3,2,1,0:T(8,128)S(1)}, f32[2,8,8,128]{3,2,1,0:T(8,128)S(1)}, u32[]{:S(2)}, u32[]{:S(2)}) collective-permute-start(f32[2,8,8,128]{3,2,1,0:T(8,128)S(1)} %get-tuple-element.23), channel_id=1, source_target_pairs={{1,2},{3,4},{5,6},{7,8},{9,10},{11,12},{13,14},{15,16},{17,18},{19... | collective-permute-start | bytes 196616 | tf_op jit(solution)/shard_map/ppermute | solution.py:428
  2.2 8.2 %collective-permute-start.1 = (f32[2,8,8,128]{3,2,1,0:T(8,128)S(1)}, f32[2,8,8,128]{3,2,1,0:T(8,128)S(1)}, u32[]{:S(2)}, u32[]{:S(2)}) collective-permute-start(f32[2,8,8,128]{3,2,1,0:T(8,128)S(1)} %get-tuple-element.24), channel_id=1, source_target_pairs={{0,1},{2,3},{4,5},{6,7},{8,9},{10,11},{12,13},{14,15},{16,17},{18,... | collective-permute-start | bytes 196616 | tf_op jit(solution)/shard_map/ppermute | solution.py:428
  10.5 12.8 %collective-permute-start.3 = (f32[2,8,32,128]{3,2,1,0:T(8,128)S(1)}, f32[2,8,32,128]{3,2,1,0:T(8,128)S(1)}, u32[]{:S(2)}, u32[]{:S(2)}) collective-permute-start(f32[2,8,32,128]{3,2,1,0:T(8,128)S(1)} %pad_maximum_fusion.own), channel_id=1, source_target_pairs={{96,192},{288,384},{480,576},{192,96},{384,288},{576,480},{97,193}... | collective-permute-start | bytes 786440 | tf_op jit(solution)/shard_map/ppermute | solution.py:428
  15.3 8.0 %collective-permute-start.2 = (f32[2,8,32,128]{3,2,1,0:T(8,128)S(1)}, f32[2,8,32,128]{3,2,1,0:T(8,128)S(1)}, u32[]{:S(2)}, u32[]{:S(2)}) collective-permute-start(f32[2,8,32,128]{3,2,1,0:T(8,128)S(1)} %pad_maximum_fusion.own), channel_id=1, source_target_pairs={{0,96},{192,288},{384,480},{576,672},{96,0},{288,192},{480,384},{6... | collective-permute-start | bytes 786440 | tf_op jit(solution)/shard_map/ppermute | solution.py:428
